TPU v7x, 32 devices: a whole 2x2x4 slice. The times are simulated.
32 devices in a mesh: dp: 8 (over z, x), shard: 4 (over y, core).
Axes of the slice: x: 2, y: 2, z: 4, core: 2. Of those that a mesh axis runs over, the one named last changes fastest.
Arguments:
- noisy: float32 [128, 256, 16], P(('dp', 'shard')), may hold values from -6 to 6
- velocity: float32 [128, 256, 16], P(('dp', 'shard')), may hold values from -6 to 6
- tstep_idx: int32 [128], P(('dp', 'shard')), may hold values from 0 to 999
- class_ids: int32 [128], P(('dp', 'shard')), may hold values from 0 to 1000
- time_weight: float32 [128], P(('dp', 'shard')), may hold values from 0.3 to 3
- dino: bfloat16 [128, 256, 768], P(('dp', 'shard')), may hold values from -6 to 6
- owner_map: int32 [12], replicated, may hold values from 0 to 11, each once
- adam_flat: float32 [2129920], P(('dp', 'shard')), may hold values from -4 to 4
- adam_m: float32 [2129920], P(('dp', 'shard')), may hold values from -0.015625 to 0.015625
- adam_v: float32 [2129920], P(('dp', 'shard')), may hold values from 1e-06 to 0.0001
- blocks_w: float32 [12, 384, 384], P('shard'), may hold values from -0.3125 to 0.3125
- stat_left: float32 [12, 384, 384], P('shard'), may hold values from -0.005 to 0.01, as said below
- stat_right: float32 [12, 384, 384], P('shard'), may hold values from -0.005 to 0.01, as said below
- root_left: float32 [12, 384, 384], P('shard'), may hold values from -3 to 3, as said below
- root_right: float32 [12, 384, 384], P('shard'), may hold values from -3 to 3, as said below
Outputs:
- loss: float32 [], replicated
- block_update: float32 [12, 384, 384], P('shard')
- stat_left_new: float32 [12, 384, 384], P('shard')
- stat_right_new: float32 [12, 384, 384], P('shard')
- adam_update: float32 [2129920], P(('dp', 'shard'))
- adam_m_new: float32 [2129920], P(('dp', 'shard'))
- adam_v_new: float32 [2129920], P(('dp', 'shard'))
Inputs may be any that keep to these rules, and one draw needn't show every extreme that they name: `owner_map`: each block number appears once. `stat_left`: each slot is symmetric positive definite. `stat_right`: each slot is symmetric positive definite. `root_left`: each slot is symmetric positive definite. `root_right`: each slot is symmetric positive definite.
All inputs are finite; a program needn't handle non-finite values.
Results may differ from a plain program's by a relative error of at most 0.0097.
Values may be sent and summed in bfloat16 or wider, within the bound.
No kernel may reach another device: no remote copies, remote signals or barrier semaphores. Data moves between devices by JAX's collectives and lax.ppermute only.
A program may use at most 192 MiB of HBM per device.

v0:
```python
import functools
import math

import jax
import jax.numpy as jnp
from jax import lax
from jax.experimental import pallas as pl
from jax.experimental.pallas import tpu as pltpu
from jax.sharding import PartitionSpec as P


D = 384
HEADS = 6
HDIM = 64
F = 1536
PD = 16
GRID = 16
SEQ = 256
FREQ = 256
DINO = 768
STEP = 10
NBLK = 12
ADAM_PAD = 2129920

BETA_ONE = 0.9
BETA_TWO = 0.95
ADAM_EPS = 1e-08
ADAM_RATE = 0.01
DECAY_RATE = 0.1
STAT_BETA = 0.9
SHAMPOO_RATE = 0.02
RMS_EPS = 1e-08
REPA_WEIGHT = 0.5
NORM_EPS = 1e-06
QK_SCALE = HDIM ** (-0.5)

AXES = ("dp", "shard")
BF = jnp.bfloat16
F32 = jnp.float32
VM = pl.BlockSpec(memory_space=pltpu.VMEM)
SM = pl.BlockSpec(memory_space=pltpu.SMEM)

FLAT_ROWS = ADAM_PAD // 128
R_PATCH = 0
R_PATCH_B = 48
R_TIME_IN = 51
R_TIME_IN_B = 819
R_TIME_OUT = 822
R_TIME_OUT_B = 1974
R_CLASS = 1977
R_MOD = 4980
R_MOD_B = 11892
R_QUERY_B = 11910
R_VALUE_B = 11913
R_PROJ_B = 11916
R_HIDDEN_B = 11919
R_DOWN_B = 11931
R_FMOD = 11934
R_FMOD_B = 14238
R_FINAL = 14244
R_FINAL_B = 14292
ALIGN_ROWS = 2310

PAY = 64
PLANE_ROWS = FLAT_ROWS // 4


def shape(dims, kind=F32):
    return jax.ShapeDtypeStruct(dims, kind)


def cost(flops, moved):
    return pl.CostEstimate(flops=int(flops), bytes_accessed=int(moved), transcendentals=0)


def room(mib):
    return pltpu.CompilerParams(vmem_limit_bytes=mib * 1024 * 1024)


def mm(left, right):
    return jnp.dot(left, right, preferred_element_type=F32)


def mm_nt(left, right):
    return lax.dot_general(left, right, (((1,), (1,)), ((), ())), preferred_element_type=F32)


def mm_tn(left, right):
    return lax.dot_general(left, right, (((0,), (0,)), ((), ())), preferred_element_type=F32)


def silu(v):
    return v / (1.0 + jnp.exp(-v))


def silu_slope(v):
    s = 1.0 / (1.0 + jnp.exp(-v))
    return s * (1.0 + v * (1.0 - s))


def split3(v):
    one = v.astype(BF)
    rest = v - one.astype(F32)
    two = rest.astype(BF)
    return one, two, (rest - two.astype(F32)).astype(BF)


def split2(v):
    one = v.astype(BF)
    return one, (v - one.astype(F32)).astype(BF)


def stack3(v):
    one, two, three = split3(v)
    return jnp.concatenate([one.astype(F32), two.astype(F32), three.astype(F32)], axis=0).astype(BF)


def fold3(v):
    third = v.shape[0] // 3
    return v[:third] + v[third : 2 * third] + v[2 * third :]


def place_of(z, x, y, c):
    return ((z * 2 + x) * 2 + y) * 2 + c


def permutation(move):
    pairs = []
    for z in range(4):
        for x in range(2):
            for y in range(2):
                for c in range(2):
                    pairs.append((place_of(z, x, y, c), place_of(*move(z, x, y, c))))
    return pairs


TO_C = permutation(lambda z, x, y, c: (z, x, y, 1 - c))
TO_Y = permutation(lambda z, x, y, c: (z, x, 1 - y, c))
TO_X = permutation(lambda z, x, y, c: (z, 1 - x, y, c))
TO_Z = [permutation(lambda z, x, y, c, d=d: ((z + d) % 4, x, y, c)) for d in range(4)]


def send(value, pairs):
    return lax.ppermute(value, AXES, pairs)


def coordinates():
    dp = lax.axis_index("dp")
    sh = lax.axis_index("shard")
    return dp // 2, dp % 2, sh // 2, sh % 2


TO_XY = permutation(lambda z, x, y, c: (z, 1 - x, 1 - y, c))
TO_CY = permutation(lambda z, x, y, c: (z, x, 1 - y, 1 - c))
TO_PAIR = permutation(lambda z, x, y, c: (z + 1 - 2 * (z % 2), x, y, c))


def send_plane(value):
    return [send(value, TO_X), send(value, TO_Y), send(value, TO_XY)]


def gather_flat(piece, cut, ready):
    turned = [send(piece, TO_Z[d]) for d in (1, 2, 3)]
    own_x, own_y = send(piece, TO_X), send(piece, TO_Y)
    first = jnp.stack([t[:cut] for t in turned])
    second = jnp.stack([t[cut:] for t in turned])
    first_x = send(first, TO_X)
    second_y = send(second, TO_Y)
    first_x, second_y, ready = lax.optimization_barrier((first_x, second_y, ready))
    first = jnp.concatenate([own_x[None, :cut], first, first_x])
    second = jnp.concatenate([own_y[None, cut:], second, second_y])
    far = [send(first, TO_Y), send(second, TO_X)]
    own = [piece, own_x[cut:], own_y[:cut]]
    own_c = [send(p, TO_C) for p in own]
    rest_c = [send(p, TO_C) for p in (first, second, *far)]
    return [p[None] for p in own] + [first, second] + far + [p[None] for p in own_c] + rest_c, ready


def flip(value, bit):
    return 1 - value if bit else value


def flat_places(cut):
    def near(dc, dx, dy):
        return lambda i, at: place_of(at[0], flip(at[1], dx), flip(at[2], dy), flip(at[3], dc))

    def far(dc, kind):
        def entry(i, at):
            z, x, y, c = at
            dz, other = (0, 1) if i == 0 else ((i - 1) % 3 + 1, (i - 1) // 3)
            dx, dy = {0: (other, 0), 1: (0, other), 2: (other, 1), 3: (1, other)}[kind]
            return place_of(lax.rem(z + 4 - dz, 4), flip(x, dx), flip(y, dy), flip(c, dc))

        return entry

    places = []
    for dc in (0, 1):
        places += [(0, near(dc, 0, 0)), (cut, near(dc, 1, 0)), (0, near(dc, 0, 1))]
        places += [((0, cut, 0, cut)[kind], far(dc, kind)) for kind in range(4)]
    return places


def gather_rows(keep, away):
    turned = [send(v, TO_Z[d + 1]) for d, v in enumerate(away)]
    column = jnp.stack([keep] + turned)
    plane = [column] + send_plane(column)
    return plane + [send(p, TO_C) for p in plane]


def read_coordinates(ref):
    return ref[0], ref[1], ref[2], ref[3]


def cond_kernel(places, rows, at_ref, cls_ref, feat_ref, *refs):
    count = len(places)
    pieces = refs[:count]
    (mods_ref, pre_ref, th_ref, cond_ref, modw_ref, fmodw_ref, tout_ref, align_ref, bias_ref,
     patch_ref, final_ref, flat, rolled) = refs[count:]
    at = read_coordinates(at_ref)
    for ref, (offset, entry) in zip(pieces, places):
        for i in range(ref.shape[0]):
            start = pl.multiple_of(entry(i, at) * rows + offset, 8)
            flat[pl.ds(start, ref.shape[1]), :] = ref[i].astype(F32)

    def row(first, count):
        return jnp.concatenate([flat[first + l : first + l + 1, :] for l in range(count)], axis=1)

    def columns(first, depth, count, which):
        return flat[pl.ds(first + which, depth, stride=count), :].astype(BF)

    def wide(v, first, depth, count, keep=None):
        stacked = stack3(v)
        out = []
        for j in range(count):
            w = columns(first, depth, count, j)
            if keep is not None:
                keep[:, 128 * j : 128 * j + 128] = w
            out.append(fold3(mm(stacked, w)))
        return jnp.concatenate(out, axis=1)

    pre = wide(feat_ref[...], R_TIME_IN, FREQ, 3) + row(R_TIME_IN_B, 3)
    th = silu(pre)
    picked = []
    for m in range(4):
        r = R_CLASS + 3 * cls_ref[m]
        picked.append(jnp.concatenate([flat[pl.ds(r + l, 1), :] for l in range(3)], axis=1))
    picked = jnp.concatenate(picked + [jnp.zeros((4, D), F32)], axis=0)
    cond = wide(th, R_TIME_OUT, D, 3, tout_ref) + row(R_TIME_OUT_B, 3) + picked
    act = silu(cond)
    pre_ref[...] = pre
    th_ref[...] = th
    cond_ref[...] = cond
    mods_ref[:, : 6 * D] = wide(act, R_MOD, D, 18, modw_ref) + row(R_MOD_B, 18)
    mods_ref[:, 6 * D :] = wide(act, R_FMOD, D, 6, fmodw_ref) + row(R_FMOD_B, 6)

    spot = lax.broadcasted_iota(jnp.int32, (ALIGN_ROWS, 128), 1)
    here = pltpu.roll(flat[R_FINAL_B : R_FINAL_B + ALIGN_ROWS, :], 112, 1)
    after = pltpu.roll(flat[R_FINAL_B + 1 : R_FINAL_B + 1 + ALIGN_ROWS, :], 112, 1)
    rolled[...] = jnp.where(spot < 112, here, after)
    for j in range(6):
        align_ref[:, 128 * j : 128 * j + 128] = rolled[pl.ds(j, D, stride=6), :].astype(BF)

    bias_ref[...] = jnp.zeros_like(bias_ref)
    for at_row, first in ((0, R_PATCH_B), (1, R_QUERY_B), (2, R_VALUE_B), (3, R_PROJ_B),
                          (4, R_HIDDEN_B), (5, R_HIDDEN_B + 3), (6, R_HIDDEN_B + 6),
                          (7, R_HIDDEN_B + 9), (8, R_DOWN_B)):
        bias_ref[at_row : at_row + 1, :] = row(first, 3)
    for half in range(2):
        bias_ref[9 + half : 10 + half, :] = jnp.concatenate(
            [rolled[2304 + 3 * half + l : 2305 + 3 * half + l, :] for l in range(3)], axis=1)
    lane = lax.broadcasted_iota(jnp.int32, (1, 128), 1)
    bias_ref[11:12, :128] = jnp.where(lane < PD, flat[R_FINAL_B : R_FINAL_B + 1, :], 0.0)
    patch = [flat[pl.ds(R_PATCH + l, PD, stride=3), :] for l in range(3)]
    patch_ref[...] = jnp.concatenate(patch, axis=1).astype(BF)
    spread = (lax.broadcasted_iota(jnp.int32, (D, 48), 0) // 8
              == lax.broadcasted_iota(jnp.int32, (D, 48), 1)).astype(F32).astype(BF)
    wide_rows = mm(spread, flat[R_FINAL : R_FINAL + 48, :].astype(BF))
    keep = (lax.broadcasted_iota(jnp.int32, (D, 128), 1) // PD
            == lax.broadcasted_iota(jnp.int32, (D, 128), 0) % 8)
    fold = (lax.broadcasted_iota(jnp.int32, (128, 128), 0) % PD
            == lax.broadcasted_iota(jnp.int32, (128, 128), 1)).astype(F32).astype(BF)
    final_ref[...] = mm(jnp.where(keep, wide_rows, 0.0).astype(BF), fold).astype(BF)


def conditioning(at, classes, features, pieces, places, rows):
    kernel = functools.partial(cond_kernel, places, rows)
    return pl.pallas_call(
        kernel,
        name="conditioning",
        out_shape=(shape((8, 8 * D)), shape((8, D)), shape((8, D)), shape((8, D)),
                   shape((D, 6 * D), BF), shape((D, 2 * D), BF), shape((D, D), BF),
                   shape((D, DINO), BF), shape((16, D)), shape((PD, D), BF), shape((D, 128), BF)),
        in_specs=[SM, SM, VM] + [VM] * len(pieces),
        out_specs=[VM] * 11,
        scratch_shapes=[pltpu.VMEM((FLAT_ROWS + 8, 128), F32), pltpu.VMEM((ALIGN_ROWS, 128), F32)],
        compiler_params=room(28),
        cost_estimate=pl.CostEstimate(flops=10**9, bytes_accessed=10**7, transcendentals=0),
    )(at, classes, features, *pieces)


def gather_blocks(mine):
    z, _, _, _ = coordinates()
    half = lax.dynamic_slice_in_dim(mine, 192 * (z % 2), 192, 1)
    near = send(half, TO_Y)
    far = send(near, TO_PAIR)
    return [mine, near, far, send(mine, TO_C), send(near, TO_C), send(far, TO_C)]


def fetch_blocks(at, own_ref, refs, out_ref, sems):
    if len(refs) == 1:
        return [pltpu.make_async_copy(refs[0], out_ref, sems.at[0])]
    z, _, y, c = at
    copies = []
    odd = lax.rem(z, 2)
    for dc in range(2):
        core = flip(c, dc)
        for t in range(3):
            mine, near, far = refs[3 * dc : 3 * dc + 3]
            here = own_ref[3 * (2 * y + core) + t]
            there = own_ref[3 * (2 * (1 - y) + core) + t]
            for source, block, rows in (
                (mine.at[t], here, None),
                (near.at[t], there, pl.ds(pl.multiple_of(192 * odd, 16), 192)),
                (far.at[t], there, pl.ds(pl.multiple_of(192 * (1 - odd), 16), 192)),
            ):
                target = out_ref.at[block] if rows is None else out_ref.at[block, rows]
                copies.append(pltpu.make_async_copy(source, target, sems.at[len(copies)]))
    return copies


UNIT = 24


def unit_of(z, x, y):
    return (2 * x + y) * 4 + z


def quarter_kernel(at_ref, mine_ref, got_ref, *out_refs):
    _, x, y, _ = read_coordinates(at_ref)
    for out_ref, (dx, dy) in zip(out_refs, ((0, 0), (1, 0), (0, 1), (1, 1))):
        rows = pl.ds(4 * (2 * flip(x, dx) + flip(y, dy)), 4)
        out_ref[...] = (mine_ref[rows].astype(F32) + got_ref[rows].astype(F32)).astype(BF)


def turn_kernel(at_ref, *refs):
    z, _, _, _ = read_coordinates(at_ref)
    for d, out_ref in enumerate(refs[4:]):
        unit = lax.rem(z + d, 4)
        out_ref[...] = sum(ref[unit].astype(F32) for ref in refs[:4]).astype(BF)


def reduce_units(at, mine, other):
    rows = mine.shape[1]
    got = send(other, TO_C)
    own, *away = pl.pallas_call(
        quarter_kernel,
        name="quarter",
        out_shape=(shape((4, rows, D), BF),) * 4,
        in_specs=[SM, VM, VM],
        out_specs=[VM] * 4,
        compiler_params=room(12),
        cost_estimate=cost(1e6, 4e6),
    )(at, mine, got)
    got = [send(v, pairs) for v, pairs in zip(away, (TO_X, TO_Y, TO_XY))]
    own, *away = pl.pallas_call(
        turn_kernel,
        name="turn",
        out_shape=(shape((rows, D), BF),) * 4,
        in_specs=[SM] + [VM] * 4,
        out_specs=[VM] * 4,
        compiler_params=room(8),
        cost_estimate=cost(1e6, 2e6),
    )(at, own, *got)
    return [own] + [send(v, TO_Z[d + 1]) for d, v in enumerate(away)]


def owner_kernel(at_ref, own_ref, *refs):
    late, early = refs[:4], refs[4:8]
    out_refs, total = refs[8:12], refs[12]
    _, _, y, c = read_coordinates(at_ref)
    one = sum(ref[...].astype(F32) for ref in late)
    two = sum(ref[0 : 4 * UNIT, :].astype(F32) for ref in early)
    for k in range(6):
        total[k] = (one[UNIT * k : UNIT * k + UNIT] if k < 2 else two[UNIT * (k - 2) : UNIT * (k - 1)])
    for out_ref, (dy, dc) in zip(out_refs, ((0, 0), (0, 1), (1, 0), (1, 1))):
        first = 3 * (2 * flip(y, dy) + flip(c, dc))
        for t in range(3):
            block = own_ref[first + t]
            low = block < 4
            part = jnp.where(low, lax.div(block, 2), lax.div(block - 4, 4))
            entry = jnp.where(low, lax.rem(block, 2), 2 + lax.rem(jnp.maximum(block - 4, 0), 4))
            out_ref[t] = jnp.where(part == c, total[entry], 0.0).astype(BF)


def join_kernel(own_ref, pair_ref, near_ref, far_ref, out_ref):
    out_ref[0] = own_ref[...] + pair_ref[...]
    out_ref[1] = near_ref[...] + far_ref[...]


def gather_owned(at, late, early, owner_map):
    piece = (3, UNIT, D)
    own, to_c, to_y, to_cy = pl.pallas_call(
        owner_kernel,
        name="owner_rows",
        out_shape=(shape(piece, BF),) * 4,
        in_specs=[SM, SM] + [VM] * 8,
        out_specs=[VM] * 4,
        scratch_shapes=[pltpu.VMEM((6, UNIT, D), F32)],
        compiler_params=room(8),
        cost_estimate=cost(1e6, 1e6),
    )(at, owner_map, *late, *early)
    far, near, pair = send(to_cy, TO_CY), send(to_y, TO_Y), send(to_c, TO_C)
    both = pl.pallas_call(
        join_kernel,
        name="join",
        out_shape=shape((2,) + piece, BF),
        in_specs=[VM] * 4,
        out_specs=VM,
        compiler_params=room(8),
        cost_estimate=cost(1e6, 1e6),
    )(own, pair, near, far)
    column = [both] + [send(both, TO_Z[d]) for d in (1, 2, 3)]
    return column + [send(v, TO_X) for v in column]


def plane_gradient(plane, pay_ref, flat, rolled, align):
    rows = 8 * pay_ref.shape[0]

    def tile(j):
        return pay_ref[:, 8 * j : 8 * j + 8, :].astype(F32).reshape(rows, D)

    def sums(first, last):
        return jnp.sum(pay_ref[:, first:last, :].astype(F32), axis=0)

    upper = lax.broadcasted_iota(jnp.int32, (rows, 1), 0) % 8 < 4

    def first(v):
        return jnp.where(upper, v, 0.0)

    def second(v):
        return jnp.where(upper, 0.0, v)

    def put_row(v, row):
        for l in range(v.shape[1] // 128):
            flat[row + l : row + l + 1, :] = v[:, 128 * l : 128 * l + 128]

    def put_matrix(v, row, count, which):
        for l in range(v.shape[1] // 128):
            flat[pl.ds(row + which + l, v.shape[0], stride=count), :] = v[:, 128 * l : 128 * l + 128]

    def classes(ids, g_low):
        numbers = (ids[:, 0:1] * 256.0 + ids[:, 1:2]).astype(jnp.int32)
        for part in range(3):
            height = 336 if part < 2 else 329
            marks = lax.broadcasted_iota(jnp.int32, (rows, 336), 1) + 336 * part
            hits = first(jnp.where(marks == numbers, 1.0, 0.0)).astype(BF)
            put_matrix(mm_tn(hits, g_low)[:height], R_CLASS + 3 * 336 * part, 3, 0)

    def modulations(low, bias):
        act = tile(0)[:, low : low + 256]
        halves = (first(act).astype(BF), second(act).astype(BF))
        for t in range(3):
            g = tile(1 + t)
            for half in range(2):
                put_matrix(mm_tn(halves[half], g.astype(BF)), R_MOD + 18 * low, 18, 3 * (t + 3 * half))
                if bias:
                    put_row(column_sum((first, second)[half](g)), R_MOD_B + 3 * (t + 3 * half))

    def finals(which, bias):
        act, g = tile(0), tile(which)
        for half, part in enumerate((first, second)):
            put_matrix(mm_tn(part(act).astype(BF), g.astype(BF)), R_FMOD, 6, 3 * half)
            if bias:
                put_row(column_sum(part(g)), R_FMOD_B + 3 * half)

    if plane == 0:
        left, g = tile(0).astype(BF), tile(1)
        g_cond, g_pre = first(g), second(g)
        put_matrix(mm_tn(left[:, :FREQ], g_pre.astype(BF)), R_TIME_IN, 3, 0)
        put_row(column_sum(g_pre), R_TIME_IN_B)
        put_matrix(mm_tn(left, g_cond.astype(BF)), R_TIME_OUT, 3, 0)
        put_row(column_sum(g_cond), R_TIME_OUT_B)
        classes(tile(2)[:, :128], g.astype(BF))
        total = sums(40, 64)
        for l in range(3):
            flat[pl.ds(R_PATCH + l, PD, stride=3), :] = total[0:16, 128 * l : 128 * l + 128]
        put_row(total[16:17], R_PATCH_B)
    if plane == 1:
        classes(tile(5)[:, :128], tile(4).astype(BF))
        modulations(0, False)
    if plane == 2:
        modulations(128, True)
        finals(4, False)
        total = sums(40, 48)
        for k, row in enumerate((R_QUERY_B, R_VALUE_B, R_PROJ_B, R_HIDDEN_B, R_HIDDEN_B + 3, R_HIDDEN_B + 6,
                                 R_HIDDEN_B + 9, R_DOWN_B)):
            put_row(total[k : k + 1], row)
    if plane == 3:
        finals(1, True)
        total = sums(40, 64)
        for l in range(3):
            flat[R_FINAL + 16 * l : R_FINAL + 16 * l + 16, :] = total[0:16, 128 * l : 128 * l + 128]
        rolled[0:8, :] = jnp.zeros((8, 128), F32)
        rolled[8 + ALIGN_ROWS :, :] = jnp.zeros_like(rolled[8 + ALIGN_ROWS :, :])
        rolled[7:8, :] = pltpu.roll(total[16:17, 0:128], 112, 1)
        for half in range(2):
            for l in range(3):
                lanes = slice(128 * l, 128 * l + 128)
                rolled[pl.ds(8 + 3 * half + l, D, stride=6), :] = align[half, :, lanes].astype(F32)
                r = 8 + 2304 + 3 * half + l
                rolled[r : r + 1, :] = total[17 + half : 18 + half, lanes]
        count = FLAT_ROWS - R_FINAL_B
        spot = lax.broadcasted_iota(jnp.int32, (count, 128), 1)
        here = pltpu.roll(rolled[8 : 8 + count, :], 16, 1)
        before = pltpu.roll(rolled[7 : 7 + count, :], 16, 1)
        flat[R_FINAL_B:FLAT_ROWS, :] = jnp.where(spot < 16, before, here)


def loss_of(pay_ref):
    rows = 8 * pay_ref.shape[0]
    parts = pay_ref[:, PAY - 8 : PAY, 0:128].astype(F32).reshape(rows, 128)
    parts = column_sum(jnp.where(lax.broadcasted_iota(jnp.int32, (rows, 128), 0) % 8 == 7, parts, 0.0))
    return parts[:, 0:1] + parts[:, 1:2] + parts[:, 2:3]


def adam_near_kernel(at_ref, *refs):
    parts = refs[:8]
    w_ref, m_ref, v_ref, loss_ref, upd_ref, new_m_ref, new_v_ref, pay, align, flat, rolled = refs[8:]
    at = read_coordinates(at_ref)
    z, x, y, c = at
    for k, ref in enumerate(parts):
        dc, dy, dx = k // 4, k // 2 % 2, k % 2
        for dz in range(4):
            there = (lax.rem(z + 4 - dz, 4), flip(x, dx), flip(y, dy), flip(c, dc))
            value = ref[dz].astype(F32)
            pay[place_of(*there)] = value
            start = pl.multiple_of(unit_of(*there[:3]) * UNIT, 8)
            align[there[3], pl.ds(start, UNIT), :] = value[16:40]
    loss_ref[...] = loss_of(pay)
    for plane in range(4):
        @pl.when(z == plane)
        def _():
            plane_gradient(plane, pay, flat, rolled, align)
    size = w_ref.shape[0]
    start = pl.multiple_of(place_of(z, x, y, c) * size, 8)
    adam_step(flat[pl.ds(start, size), :], w_ref, m_ref, v_ref, upd_ref, new_m_ref, new_v_ref)


def adam_plane_kernel(plane, pay_ref, align_ref, loss_ref, flat_ref, rolled):
    loss_ref[...] = loss_of(pay_ref)
    plane_gradient(plane, pay_ref, flat_ref, rolled, align_ref)


def adam_step(grad, w_ref, m_ref, v_ref, upd_ref, new_m_ref, new_v_ref):
    new_m = BETA_ONE * m_ref[...] + (1.0 - BETA_ONE) * grad
    new_v = BETA_TWO * v_ref[...] + (1.0 - BETA_TWO) * grad * grad
    new_m_ref[...] = new_m
    new_v_ref[...] = new_v
    right_m = new_m / (1.0 - BETA_ONE**STEP)
    right_v = new_v / (1.0 - BETA_TWO**STEP)
    upd_ref[...] = -ADAM_RATE * (right_m / (jnp.sqrt(right_v) + ADAM_EPS) + DECAY_RATE * w_ref[...])


ROLL_ROWS = 8 + FLAT_ROWS - R_FINAL_B + 8


ROLL_ROWS = 8 + FLAT_ROWS - R_FINAL_B + 8


def adam_near(at, parts, flat_w, m, v):
    size = flat_w.shape
    loss, upd, new_m, new_v = pl.pallas_call(
        adam_near_kernel,
        name="adam",
        out_shape=(shape((1, 1)), shape(size), shape(size), shape(size)),
        in_specs=[SM] + [VM] * 11,
        out_specs=[VM] * 4,
        scratch_shapes=[pltpu.VMEM((32, PAY, D), F32), pltpu.VMEM((2, D, D), F32),
                        pltpu.VMEM((FLAT_ROWS, 128), F32), pltpu.VMEM((ROLL_ROWS, 128), F32)],
        compiler_params=room(24),
        cost_estimate=pl.CostEstimate(flops=10**9, bytes_accessed=10**7, transcendentals=0),
    )(at, *parts, flat_w, m, v)
    return loss[0, 0], upd, new_m, new_v


def adam_wide(pays, align, flat_w, m, v):
    grads = []
    for plane in range(4):
        loss, flat = pl.pallas_call(
            functools.partial(adam_plane_kernel, plane),
            name="adam_gradient",
            out_shape=(shape((1, 1)), shape((FLAT_ROWS, 128))),
            in_specs=[VM] * 2,
            out_specs=[VM] * 2,
            scratch_shapes=[pltpu.VMEM((ROLL_ROWS, 128), F32)],
        )(pays[:, plane], align)
        grads.append(flat[PLANE_ROWS * plane : PLANE_ROWS * (plane + 1)])
    size = flat_w.shape[0]
    place = lax.axis_index("dp") * lax.axis_size("shard") + lax.axis_index("shard")
    grad = lax.dynamic_slice_in_dim(jnp.concatenate(grads), place * size, size, 0)
    upd, new_m, new_v = pl.pallas_call(
        lambda g, *refs: adam_step(g[...], *refs),
        name="adam",
        out_shape=(shape(flat_w.shape),) * 3,
        in_specs=[VM] * 4,
        out_specs=[VM] * 3,
    )(grad, flat_w, m, v)
    return loss[0, 0], upd, new_m, new_v


def shampoo_kernel(near, at_ref, *refs):
    t = pl.program_id(0)
    if near:
        parts = refs[:8]
        w_ref, sl_ref, sr_ref, rl_ref, rr_ref, upd_ref, nl_ref, nr_ref, grad = refs[8:]
        z, x, y, _ = read_coordinates(at_ref)
        for dx in range(2):
            for dz in range(4):
                for dy in range(2):
                    unit = unit_of(lax.rem(z + 4 - dz, 4), flip(x, dx), flip(y, dy))
                    rows = pl.ds(pl.multiple_of(unit * UNIT, 8), UNIT)
                    grad[rows, :] = parts[4 * dx + dz][dy, t].astype(F32)
        g = grad[...].astype(BF)
    else:
        grad_ref, w_ref, sl_ref, sr_ref, rl_ref, rr_ref, upd_ref, nl_ref, nr_ref = refs
        g = grad_ref[t]
    nl_ref[0] = STAT_BETA * sl_ref[t] + (1.0 - STAT_BETA) * mm_nt(g, g)
    nr_ref[0] = STAT_BETA * sr_ref[t] + (1.0 - STAT_BETA) * mm_tn(g, g)
    left = mm(jnp.concatenate(split2(rl_ref[t]), axis=1), jnp.concatenate([g, g], axis=0))
    l_one, l_two = split2(left)
    r_one, r_two = split2(rr_ref[t])
    p = mm(jnp.concatenate([l_one, l_two, l_one], axis=1), jnp.concatenate([r_one, r_one, r_two], axis=0))
    mean = jnp.sum(jnp.sum(p * p, axis=1, keepdims=True), axis=0, keepdims=True) * (1.0 / (D * D))
    root = jnp.sqrt(mean)
    upd_ref[0] = -SHAMPOO_RATE * (p / (root + RMS_EPS) + DECAY_RATE * w_ref[t])


def shampoo(at, grads, blocks_w, stat_left, stat_right, root_left, root_right):
    near = len(grads) == 8
    slots = blocks_w.shape[0]
    one = pl.BlockSpec((1, D, D), lambda t: (t, 0, 0))
    return pl.pallas_call(
        functools.partial(shampoo_kernel, near),
        name="shampoo",
        grid=(slots,),
        out_shape=(shape((slots, D, D)),) * 3,
        in_specs=[SM] + [VM] * (len(grads) + 5),
        out_specs=[one] * 3,
        scratch_shapes=[pltpu.VMEM((D, D), F32)] if near else [],
        compiler_params=room(26),
        cost_estimate=pl.CostEstimate(flops=3 * 10**9, bytes_accessed=15 * 10**6, transcendentals=0),
    )(at, *grads, blocks_w, stat_left, stat_right, root_left, root_right)


GELU_C = math.sqrt(2.0 / math.pi)
GELU_D = 0.044715
EARLY = 5 * 24
LATE = 2 * 24
SUMS_MLP = 24


def norm_stats(v):
    centered = v - jnp.sum(v, axis=-1, keepdims=True) * (1.0 / D)
    inv = lax.rsqrt(jnp.sum(centered * centered, axis=-1, keepdims=True) * (1.0 / D) + NORM_EPS)
    return centered * inv, inv


def norm_back(g, normed, inv):
    mean_g = jnp.sum(g, axis=-1, keepdims=True) * (1.0 / D)
    mean_gn = jnp.sum(g * normed, axis=-1, keepdims=True) * (1.0 / D)
    return inv * (g - mean_g - normed * mean_gn)


def column_sum(v):
    return jnp.sum(v, axis=0, keepdims=True)


def head(v, h):
    return v[:, HDIM * h : HDIM * h + HDIM]


def put_pair(core, mine_ref, other_ref, j, zero, one):
    zero, one = zero.astype(BF), one.astype(BF)
    mine, other = jnp.where(core == 0, zero, one), jnp.where(core == 0, one, zero)
    for u in range(16):
        rows = slice(24 * u, 24 * u + 24)
        mine_ref[u, 24 * j : 24 * j + 24, :] = mine[rows]
        other_ref[u, 24 * j : 24 * j + 24, :] = other[rows]


def front_kernel(at_ref, own_ref, noisy_ref, mods_ref, bias_ref, patch_ref, pos_ref, *refs):
    h0_ref, qkv_ref, att_ref, h1_ref, all_ref, w_ref, in_sems, out_sem = refs[-8:]
    i = pl.program_id(0)
    fetch = fetch_blocks(read_coordinates(at_ref), own_ref, refs[:-8], w_ref, in_sems)
    keep = pltpu.make_async_copy(w_ref, all_ref, out_sem)

    @pl.when(i == 0)
    def _():
        for copy in fetch:
            copy.start()
        for copy in fetch:
            copy.wait()
        keep.start()

    def mod(t):
        return mods_ref[pl.ds(i, 1), D * t : D * t + D]

    h0 = mm_tn(noisy_ref[0].astype(BF), patch_ref[...]) + bias_ref[0:1, :] + pos_ref[...]
    h0_ref[0] = h0
    normed, _ = norm_stats(h0)
    act = (normed * (1.0 + mod(1)) + mod(0)).astype(BF)
    q = (mm(act, w_ref[0]) + bias_ref[1:2, :]).astype(BF)
    k = mm(act, w_ref[1]).astype(BF)
    v = (mm(act, w_ref[2]) + bias_ref[2:3, :]).astype(BF)
    qkv_ref[0, :, 0:D] = q
    qkv_ref[0, :, D : 2 * D] = k
    qkv_ref[0, :, 2 * D :] = v
    outs = []
    for h in range(HEADS):
        s = mm_nt(head(q, h), head(k, h)) * QK_SCALE
        e = jnp.exp(s - jnp.max(s, axis=-1, keepdims=True))
        p = e * (1.0 / jnp.sum(e, axis=-1, keepdims=True))
        outs.append(mm(p.astype(BF), head(v, h)))
    att = jnp.concatenate(outs, axis=1).astype(BF)
    att_ref[0] = att
    h1_ref[0] = h0 + mod(2) * (mm(att, w_ref[3]) + bias_ref[3:4, :])

    @pl.when(i == pl.num_programs(0) - 1)
    def _():
        keep.wait()


def middle_kernel(images, total_img, at_ref, tw_ref, h1_ref, vel_ref, dino_ref, mods_ref, bias_ref, w_ref, aw_ref, fw_ref,
                  bh1_ref, gm_ref, mine_ref, other_ref, sums_ref,
                  act2_s, gelu_s, slope_s, bi_s, bb2_s, h1_s, ba_s, act3_s, bo_s):
    i = pl.program_id(0)
    rows = pl.ds(pl.multiple_of(i * SEQ, SEQ), SEQ)

    def mod(t):
        return mods_ref[pl.ds(i, 1), D * t : D * t + D]

    @pl.when(i == 0)
    def _():
        sums_ref[...] = jnp.zeros_like(sums_ref)

    h1 = h1_ref[0]
    n2, inv2 = norm_stats(h1)
    act2 = (n2 * (1.0 + mod(4)) + mod(3)).astype(BF)
    act2_s[rows, :] = act2
    branch = jnp.zeros((SEQ, D), F32) + bias_ref[8:9, :]
    for j in range(4):
        lanes = slice(D * j, D * j + D)
        x = mm(act2, w_ref[4 + j]) + bias_ref[4 + j : 5 + j, :]
        xx = x * x
        t = jnp.tanh(x * (GELU_C + (GELU_C * GELU_D) * xx))
        half = 0.5 + 0.5 * t
        g = (x * half).astype(BF)
        slope_s[:, lanes] = half + (0.5 * x) * (1.0 - t * t) * (GELU_C + (3.0 * GELU_C * GELU_D) * xx)
        gelu_s[rows, lanes] = g
        branch = branch + mm(g, w_ref[8 + j])
    h2 = h1 + mod(5) * branch
    n3, inv3 = norm_stats(h2)
    act3 = (n3 * (1.0 + mod(7)) + mod(6)).astype(BF)
    act3_s[rows, :] = act3
    out = mm(act3, fw_ref[...]) + bias_ref[11:12, 0:128]
    err = out[:, :PD] - vel_ref[0].T
    weight = tw_ref[i]
    loss = jnp.sum(column_sum(err * err), axis=1, keepdims=True) * (weight / (total_img * SEQ * PD))
    bo = jnp.concatenate([err * (2.0 * weight / (total_img * SEQ * PD)), jnp.zeros((SEQ, 128 - PD), F32)],
                         axis=1).astype(BF)
    bo_s[rows, :] = bo

    h1_low = h1.astype(BF)
    h1_s[rows, :] = h1_low
    aligned = mm(h1_low, aw_ref[...]) + jnp.concatenate([bias_ref[9:10, :], bias_ref[10:11, :]], axis=1)
    dino = dino_ref[0].astype(F32)
    dot = jnp.sum(aligned * dino, axis=-1, keepdims=True)
    ra = lax.rsqrt(jnp.sum(aligned * aligned, axis=-1, keepdims=True) + NORM_EPS)
    rd = lax.rsqrt(jnp.sum(dino * dino, axis=-1, keepdims=True) + NORM_EPS)
    scale = REPA_WEIGHT / (total_img * SEQ)
    both = ra * rd
    cosine = dot * both
    loss = loss - column_sum(cosine) * scale
    ba = (dino * (both * -scale) + aligned * (cosine * (ra * ra) * scale)).astype(BF)
    ba_s[rows, :] = ba
    through = mm_nt(ba, aw_ref[...])

    b3 = mm_nt(bo, fw_ref[...])
    bh2 = norm_back(b3 * (1.0 + mod(7)), n3, inv3)
    bb2 = (bh2 * mod(5)).astype(BF)
    bb2_s[rows, :] = bb2
    b2 = jnp.zeros((SEQ, D), F32)
    for j in range(4):
        lanes = slice(D * j, D * j + D)
        bi = (mm_nt(bb2, w_ref[8 + j]) * slope_s[:, lanes]).astype(BF)
        bi_s[rows, lanes] = bi
        sums_ref[16 + j : 17 + j, :] += column_sum(bi.astype(F32))
        b2 = b2 + mm_nt(bi, w_ref[4 + j])
    sums_ref[20:21, :] += column_sum(bb2.astype(F32))
    ba_sum = column_sum(ba.astype(F32))
    sums_ref[21:22, :] += ba_sum[:, :D]
    sums_ref[22:23, :] += ba_sum[:, D:]
    sums_ref[23:24, 0:128] += column_sum(bo.astype(F32))
    bh1_ref[0] = bh2 + norm_back(b2 * (1.0 + mod(4)), n2, inv2) + through
    gm_ref[0, 0:1, :] = column_sum(b2)
    gm_ref[0, 1:2, :] = column_sum(b2 * n2)
    gm_ref[0, 2:3, :] = column_sum(bh2 * branch)
    gm_ref[0, 3:4, :] = column_sum(b3)
    gm_ref[0, 4:5, :] = column_sum(b3 * n3)
    gm_ref[0, 5:6, :] = jnp.broadcast_to(loss, (1, D))
    gm_ref[0, 6:8, :] = jnp.zeros((2, D), F32)

    @pl.when(i == images - 1)
    def _():
        put = functools.partial(put_pair, at_ref[3], mine_ref, other_ref)
        for j in range(4):
            lanes = slice(D * j, D * j + D)
            put(j, mm_tn(act2_s[...], bi_s[:, lanes]), mm_tn(gelu_s[:, lanes], bb2_s[...]))
        put(4, mm_tn(h1_s[...], ba_s[:, 0:D]), mm_tn(h1_s[...], ba_s[:, D:]))
        g = mm_tn(act3_s[...], bo_s[...]).astype(BF)
        spread = (lax.broadcasted_iota(jnp.int32, (128, 128), 1) % PD
                  == lax.broadcasted_iota(jnp.int32, (128, 128), 0)).astype(F32).astype(BF)
        keep = (lax.broadcasted_iota(jnp.int32, (D, 128), 1) // PD
                == lax.broadcasted_iota(jnp.int32, (D, 128), 0) % 8)
        fold = (lax.broadcasted_iota(jnp.int32, (48, D), 1) // 8
                == lax.broadcasted_iota(jnp.int32, (48, D), 0)).astype(F32).astype(BF)
        flat = mm(fold, jnp.where(keep, mm(g, spread), 0.0).astype(BF))
        for l in range(3):
            sums_ref[0:16, 128 * l : 128 * l + 128] = flat[16 * l : 16 * l + 16, :]


def back_kernel(first, bh1_ref, h0_ref, qkv_ref, att_ref, noisy_ref, mods_ref, bias_ref, w_ref,
                bb1_ref, bp_ref, act_ref, gm_ref, patch_ref):
    i = pl.program_id(0) + first

    def mod(t):
        return mods_ref[pl.ds(i, 1), D * t : D * t + D]

    bh1 = bh1_ref[0]
    att = att_ref[0]
    bb1 = (bh1 * mod(2)).astype(BF)
    bb1_ref[0] = bb1
    gm_ref[0, 2:3, :] = column_sum(bh1 * (mm(att, w_ref[3]) + bias_ref[3:4, :]))
    batt = mm_nt(bb1, w_ref[3]).astype(BF)
    q, k, v = qkv_ref[0, :, 0:D], qkv_ref[0, :, D : 2 * D], qkv_ref[0, :, 2 * D :]
    gq, gk, gv = [], [], []
    for h in range(HEADS):
        qh, kh, vh, bh = head(q, h), head(k, h), head(v, h), head(batt, h)
        s = mm_nt(kh, qh) * QK_SCALE
        e = jnp.exp(s - jnp.max(s, axis=0, keepdims=True))
        p = e * (1.0 / column_sum(e))
        dp = mm_nt(vh, bh)
        ds = (p * (dp - column_sum(dp * p))).astype(BF)
        gv.append(mm(p.astype(BF), bh))
        gk.append(mm(ds, qh))
        gq.append(mm_tn(ds, kh))
    bq = (jnp.concatenate(gq, axis=1) * QK_SCALE).astype(BF)
    bk = (jnp.concatenate(gk, axis=1) * QK_SCALE).astype(BF)
    bv = jnp.concatenate(gv, axis=1).astype(BF)
    bp_ref[0, :, 0:D] = bq
    bp_ref[0, :, D : 2 * D] = bk
    bp_ref[0, :, 2 * D :] = bv
    b1 = mm_nt(bq, w_ref[0]) + mm_nt(bk, w_ref[1]) + mm_nt(bv, w_ref[2])
    n1, inv1 = norm_stats(h0_ref[0])
    act_ref[0] = (n1 * (1.0 + mod(1)) + mod(0)).astype(BF)
    gm_ref[0, 0:1, :] = column_sum(b1)
    gm_ref[0, 1:2, :] = column_sum(b1 * n1)
    bh0 = (bh1 + norm_back(b1 * (1.0 + mod(1)), n1, inv1)).astype(BF)
    patch_ref[0] = mm(noisy_ref[0].astype(BF), bh0)
    gm_ref[0, 3:4, :] = column_sum(bh0.astype(F32))
    gm_ref[0, 4:5, :] = column_sum(bq.astype(F32))
    gm_ref[0, 5:6, :] = column_sum(bv.astype(F32))
    gm_ref[0, 6:7, :] = column_sum(bb1.astype(F32))
    gm_ref[0, 7:8, :] = jnp.zeros((1, D), F32)


def last_kernel(counts, at_ref, att_ref, *refs):
    mine_ref, other_ref = refs[-2:]
    put = functools.partial(put_pair, at_ref[3], mine_ref, other_ref)
    parts = []
    first = 0
    for k, count in enumerate(counts):
        act_ref, bp_ref, bb1_ref = refs[3 * k : 3 * k + 3]
        parts.append((act_ref, bp_ref, att_ref, bb1_ref, first))
        first += count * SEQ

    def over(which):
        return sum(which(*p) for p in parts)

    def qkv(j):
        return over(lambda act, bp, att, bb1, first: mm_tn(act[...], bp[:, D * j : D * j + D]))

    put(0, qkv(0), qkv(2))
    put(1, qkv(1), over(lambda act, bp, att, bb1, first: mm_tn(
        att[first : first + bb1.shape[0], :], bb1[...])))


def cond_back_kernel(images, aligns, at_ref, cls_ref, gm2_ref, pre_ref, th_ref, cond_ref, feat_ref, modw_ref, fmodw_ref,
                     tout_ref, sums_ref, *refs):
    align_refs, refs = refs[:aligns], refs[aligns:]
    out_refs, pay_ref, refs = refs[-5:-1], refs[-1], refs[:-5]
    gm3_refs, patch_refs = refs[::2], refs[1::2]
    none = jnp.zeros((4, D), F32)
    gm2 = [gm2_ref[m] for m in range(images)]
    gm3 = [ref[m] for ref in gm3_refs for m in range(ref.shape[0])]
    patch = sum(ref[m] for ref in patch_refs for m in range(ref.shape[0]))

    def rows_of(values, r):
        return jnp.concatenate([v[r : r + 1, :] for v in values] + [none], axis=0)

    tiles = [rows_of(gm3, 0), rows_of(gm3, 1), rows_of(gm3, 2),
             rows_of(gm2, 0), rows_of(gm2, 1), rows_of(gm2, 2)]
    finals = [rows_of(gm2, 3), rows_of(gm2, 4)]
    g_act = jnp.zeros((24, D), F32)
    for t in range(6):
        g_act = g_act + mm_nt(stack3(tiles[t]), modw_ref[:, D * t : D * t + D])
    for t in range(2):
        g_act = g_act + mm_nt(stack3(finals[t]), fmodw_ref[:, D * t : D * t + D])
    cond = cond_ref[...]
    g_cond = fold3(g_act) * silu_slope(cond)
    g_pre = fold3(mm_nt(stack3(g_cond), tout_ref[...])) * silu_slope(pre_ref[...])
    act = silu(cond)
    lane = lax.broadcasted_iota(jnp.int32, (1, 128), 1)
    ids = []
    for m in range(images):
        number = cls_ref[m]
        row = jnp.where(lane == 0, (number // 256).astype(F32), 0.0)
        ids.append(jnp.where(lane == 1, (number % 256).astype(F32), row))
    ids = jnp.concatenate(ids, axis=0)
    loss = sum(v[5:6, 0:128] for v in gm2)
    pieces = [v.astype(F32) for v in split3(loss)]
    loss = jnp.where(lane == 0, pieces[0], jnp.where(lane == 1, pieces[1], jnp.where(lane == 2, pieces[2], 0.0)))
    loss = jnp.concatenate([loss, jnp.zeros((1, D - 128), F32)], axis=1)

    def put(plane, j, upper, lower):
        pay_ref[plane, 8 * j : 8 * j + 8, :] = jnp.concatenate([upper[:4], lower[:4]], axis=0)

    def put_rows(plane, first, v):
        pay_ref[plane, first : first + v.shape[0], :] = v

    def over(r):
        return sum(v[r : r + 1, :] for v in gm3)

    none = jnp.zeros((8, D), F32)
    row = jnp.zeros((1, D), F32)
    tags = jnp.concatenate([ids, jnp.zeros((4, D - 128), F32)], axis=1)
    pay_ref[...] = jnp.zeros_like(pay_ref)
    put(0, 0, th_ref[...], jnp.concatenate([feat_ref[...], jnp.zeros((8, D - FREQ), F32)], axis=1))
    put(0, 1, g_cond, g_pre)
    put(0, 2, tags, none)
    put_rows(0, 40, patch)
    for plane in (1, 2):
        put(plane, 0, act, act)
        for t in range(3):
            put(plane, 1 + t, tiles[t], tiles[t + 3])
    put(1, 4, g_cond, none)
    put(1, 5, tags, none)
    put(2, 4, finals[0], finals[1])
    sums = sums_ref[...]
    put_rows(2, 40, jnp.concatenate([over(4), over(5), over(6), sums[16:21]], axis=0))
    put(3, 0, act, act)
    put(3, 1, finals[0], finals[1])
    put_rows(3, 16, sum(ref[4 * UNIT :, :].astype(F32) for ref in align_refs))
    put_rows(3, 40, sums[0:16])
    last = [[over(3)] + [row] * 6, [row] * 7, [row] * 7, [sums[23:24], sums[21:22], sums[22:23]] + [row] * 4]
    for plane in range(4):
        put_rows(plane, 56, jnp.concatenate(last[plane] + [loss], axis=0))
    for d, out_ref in enumerate(out_refs):
        out_ref[...] = pay_ref[lax.rem(at_ref[0] + d, 4)].astype(BF)


def rows_each(first, *dims):
    return pl.BlockSpec((1,) + dims, lambda i: (i + first,) + (0,) * len(dims))


def front(at, owner_map, noisy, mods, bias, patch_low, pos, pieces):
    images = noisy.shape[0]
    each = functools.partial(rows_each, 0)
    anywhere = pl.BlockSpec(memory_space=pl.ANY)
    return pl.pallas_call(
        front_kernel,
        name="front",
        grid=(images,),
        out_shape=(shape((images, SEQ, D)), shape((images, SEQ, 3 * D), BF),
                   shape((images, SEQ, D), BF), shape((images, SEQ, D)), shape((NBLK, D, D), BF)),
        in_specs=[SM, SM, each(PD, SEQ), VM, VM, VM, VM] + [anywhere] * len(pieces),
        out_specs=[each(SEQ, D), each(SEQ, 3 * D), each(SEQ, D), each(SEQ, D), anywhere],
        scratch_shapes=[pltpu.VMEM((NBLK, D, D), BF), pltpu.SemaphoreType.DMA((18,)), pltpu.SemaphoreType.DMA(())],
        compiler_params=room(24),
        cost_estimate=cost(2.2e9, 1.2e7),
    )(at, owner_map, noisy, mods, bias, patch_low, pos, *pieces)


def middle(total_img, at, time_weight, h1, velocity, dino, mods, bias, blocks, align_low, final_low):
    images = h1.shape[0]
    each = functools.partial(rows_each, 0)
    full = lambda lanes, kind=BF: pltpu.VMEM((images * SEQ, lanes), kind)
    return pl.pallas_call(
        functools.partial(middle_kernel, images, total_img),
        name="middle",
        grid=(images,),
        out_shape=(shape((images, SEQ, D)), shape((images, 8, D)),
                   shape((16, EARLY, D), BF), shape((16, EARLY, D), BF), shape((SUMS_MLP, D))),
        in_specs=[SM, SM, each(SEQ, D), each(PD, SEQ), each(SEQ, DINO), VM, VM, VM, VM, VM],
        out_specs=[each(SEQ, D), each(8, D), VM, VM, VM],
        scratch_shapes=[full(D), full(F), pltpu.VMEM((SEQ, F), F32), full(F), full(D), full(D),
                        full(DINO), full(D), full(128)],
        compiler_params=room(40),
        cost_estimate=cost(9e9, 1.4e7),
    )(at, time_weight, h1, velocity, dino, mods, bias, blocks, align_low, final_low)


def attention_back(first, count, bh1, h0, qkv, att, noisy, mods, bias, blocks):
    each = functools.partial(rows_each, first)
    out = functools.partial(rows_each, 0)
    return pl.pallas_call(
        functools.partial(back_kernel, first),
        name="attention_back",
        grid=(count,),
        out_shape=(shape((count, SEQ, D), BF), shape((count, SEQ, 3 * D), BF), shape((count, SEQ, D), BF),
                   shape((count, 8, D)), shape((count, PD, D))),
        in_specs=[each(SEQ, D), each(SEQ, D), each(SEQ, 3 * D), each(SEQ, D), each(PD, SEQ), VM, VM, VM],
        out_specs=[out(SEQ, D), out(SEQ, 3 * D), out(SEQ, D), out(8, D), out(PD, D)],
        compiler_params=room(24),
        cost_estimate=cost(1.2e9 * count, 3e6 * count),
    )(bh1, h0, qkv, att, noisy, mods, bias, blocks)


def last_gradients(at, att, parts):
    flat = lambda v: v.reshape(-1, v.shape[-1])
    arrays = [flat(v) for part in parts for v in part]
    counts = tuple(part[0].shape[0] for part in parts)
    return pl.pallas_call(
        functools.partial(last_kernel, counts),
        name="last_gradients",
        out_shape=(shape((16, LATE, D), BF),) * 2,
        in_specs=[SM] + [VM] * (len(arrays) + 1),
        out_specs=[VM] * 2,
        compiler_params=room(20),
        cost_estimate=cost(1.2e9, 9e6),
    )(at, flat(att), *arrays)


def cond_back(images, at, class_ids, gm2, pre, th, cond, features, mod_w, fmod_w, tout_w, sums, aligns, gm3):
    return pl.pallas_call(
        functools.partial(cond_back_kernel, images, len(aligns)),
        name="cond_back",
        out_shape=(shape((PAY, D), BF),) * 4,
        in_specs=[SM, SM] + [VM] * (9 + len(aligns) + len(gm3)),
        out_specs=[VM] * 4,
        scratch_shapes=[pltpu.VMEM((4, PAY, D), F32)],
        compiler_params=room(16),
        cost_estimate=cost(1e8, 4e6),
    )(at, class_ids, gm2, pre, th, cond, features, mod_w, fmod_w, tout_w, sums, *aligns, *gm3)


def position_table():
    quarter = D // 4
    frequencies = 1.0 / 10000.0 ** (jnp.arange(quarter, dtype=jnp.float32) / quarter)
    cell_ids = jnp.arange(SEQ, dtype=jnp.int32)
    row_arg = (cell_ids // GRID).astype(jnp.float32)[:, None] * frequencies[None, :]
    col_arg = (cell_ids % GRID).astype(jnp.float32)[:, None] * frequencies[None, :]
    return jnp.concatenate(
        [jnp.sin(col_arg), jnp.cos(col_arg), jnp.sin(row_arg), jnp.cos(row_arg)], axis=1
    )


def time_features(tstep_idx):
    half_freq = FREQ // 2
    frequencies = jnp.exp(-math.log(10000.0) * jnp.arange(half_freq, dtype=jnp.float32) / half_freq)
    angles = (tstep_idx.astype(jnp.float32) + 0.5)[:, None] * frequencies[None, :]
    return jnp.concatenate([jnp.cos(angles), jnp.sin(angles)], axis=1)


def body(
    noisy,
    velocity,
    tstep_idx,
    class_ids,
    time_weight,
    dino,
    owner_map,
    adam_flat,
    adam_m,
    adam_v,
    blocks_w,
    stat_left,
    stat_right,
    root_left,
    root_right,
):
    dp, group = lax.axis_size("dp"), lax.axis_size("shard")
    near = is_near(dp, group)
    images = noisy.shape[0]
    total_img = images * dp * group
    at = jnp.stack([jnp.asarray(v, jnp.int32) for v in coordinates()])
    flat_w = adam_flat.reshape(-1, 128)
    flat_m = adam_m.reshape(-1, 128)
    flat_v = adam_v.reshape(-1, 128)
    mine = flat_w.astype(BF)
    features = jnp.pad(time_features(tstep_idx), ((0, 4), (0, 0)))
    pos = position_table()
    noisy = jnp.transpose(noisy, (0, 2, 1))
    velocity = jnp.transpose(velocity, (0, 2, 1))
    rows = flat_w.shape[0]
    if near:
        cut = rows // 16 * 8 + 8 if rows // 8 % 2 else rows // 2
        block_parts = gather_blocks(blocks_w.astype(BF))
        pieces, (at, features, pos) = gather_flat(mine, cut, (at, features, pos))
        places = flat_places(cut)
    else:
        pieces = [lax.all_gather(mine, AXES, axis=0, tiled=True)[None]]
        places = [(0, lambda i, at: 0)]
        slot_low = lax.all_gather(blocks_w.astype(BF), "shard", axis=0, tiled=True)
        block_ids = jnp.arange(NBLK, dtype=jnp.int32)
        slot_of = jnp.sum(
            block_ids[:, None] * (owner_map[:, None] == block_ids[None, :]).astype(jnp.int32), axis=0
        )
        block_parts = [jnp.take(slot_low, slot_of, axis=0)]
    (mods, pre, th, cond, mod_w, fmod_w, tout_w, align_low, bias, patch_low, final_low) = conditioning(
        at, class_ids, features, pieces, places, rows)
    h0, qkv, att, h1, blocks = front(at, owner_map, noisy, mods, bias, patch_low, pos, block_parts)
    bh1, gm2, mine, other, sums = middle(
        total_img, at, time_weight, h1, velocity, dino, mods, bias, blocks, align_low, final_low)
    if near:
        early = reduce_units(at, mine, other)
    parts, gm3 = [], []
    for first, count in ((0, 1), (1, images - 1)):
        bb1, bp, act, gm, patch = attention_back(first, count, bh1, h0, qkv, att, noisy, mods, bias, blocks)
        parts.append((act, bp, bb1))
        gm3 += [gm, patch]
    late_mine, late_other = last_gradients(at, att, parts)
    aligns = early if near else [jnp.zeros((EARLY, D), BF)]
    keep, *away = cond_back(
        images, at, class_ids, gm2, pre, th, cond, features, mod_w, fmod_w, tout_w, sums, aligns, gm3)
    if near:
        late = reduce_units(at, late_mine, late_other)
        grads = gather_owned(at, late, early, owner_map)
        parts = gather_rows(keep, away)
        loss, upd, new_m, new_v = adam_near(at, parts, flat_w, flat_m, flat_v)
        *grads, loss, upd, new_m, new_v = lax.optimization_barrier((*grads, loss, upd, new_m, new_v))
    else:
        core = at[3]

        def by_part(mine, other):
            pair = jnp.where(core == 0, jnp.stack([mine, other]), jnp.stack([other, mine]))
            count = mine.shape[1] // UNIT
            return pair.reshape(2, 16, count, UNIT, D).transpose(0, 2, 1, 3, 4).reshape(2, count, D, D)

        early, late = by_part(mine, other), by_part(late_mine, late_other)
        late = jnp.stack([late[0, 0], late[0, 1], late[1, 0], late[1, 1]])
        grad_model = jnp.concatenate([late, early[:, :4].reshape(8, D, D)])
        planes = jnp.take(jnp.stack([keep, *away]), (jnp.arange(4) - at[0]) % 4, axis=0)
        pays = lax.all_gather(planes, AXES, axis=0, tiled=False)
        align_sum = lax.psum(early[:, 4].astype(F32), AXES)
        loss, upd, new_m, new_v = adam_wide(pays, align_sum, flat_w, flat_m, flat_v)
        slots = jnp.take(grad_model, owner_map, axis=0)
        owned = lax.psum_scatter(slots, "shard", scatter_dimension=0, tiled=True)
        grads = [lax.psum(owned.astype(F32), "dp").astype(BF)]
    block_update, new_left, new_right = shampoo(
        at, grads, blocks_w, stat_left, stat_right, root_left, root_right)
    return (loss, block_update, new_left, new_right,
            upd.reshape(-1), new_m.reshape(-1), new_v.reshape(-1))


def is_near(dp, group):
    return (dp, group) == (8, 4)


def solution(mesh):
    return jax.shard_map(
        body,
        mesh=mesh,
        in_specs=(
            P(("dp", "shard"), None, None),
            P(("dp", "shard"), None, None),
            P(("dp", "shard")),
            P(("dp", "shard")),
            P(("dp", "shard")),
            P(("dp", "shard"), None, None),
            P(),
            P(("dp", "shard")),
            P(("dp", "shard")),
            P(("dp", "shard")),
            P("shard", None, None),
            P("shard", None, None),
            P("shard", None, None),
            P("shard", None, None),
            P("shard", None, None),
        ),
        out_specs=(
            P(),
            P("shard", None, None),
            P("shard", None, None),
            P("shard", None, None),
            P(("dp", "shard")),
            P(("dp", "shard")),
            P(("dp", "shard")),
        ),
        check_vma=False,
    )
```

profile of v0, /device:TPU:0, one launch (start us, length us, event | category | flops | bytes accessed | tf_op | source)
XLA Modules:
  0.0 210.4 jit_solution(4874934414858998954)
XLA Ops:
  0.6 1.9 convert_bitcast_fusion
  2.5 5.1 %collective-permute-start.2 = (bf16[520,128]{1,0:T(8,128)(2,1)}, bf16[520,128]{1,0:T(8,128)(2,1)S(1)}, u32[]{:S(2)}, u32[]{:S(2)}) collective-permute-start(bf16[520,128]{1,0:T(8,128)(2,1)} %get-tuple-element.170), channel_id=1, source_target_pairs={{0,24},{1,25},{2,26},{3,27},{4,28},{5,29},{6,30},{7,31},{8,0},{9,1... | collective-permute-start | bytes 399368 | tf_op jit(solution)/shard_map/ppermute | solution.py:144
  14.0 5.1 %collective-permute-done.1 = bf16[520,128]{1,0:T(8,128)(2,1)S(1)} collective-permute-done((bf16[520,128]{1,0:T(8,128)(2,1)}, bf16[520,128]{1,0:T(8,128)(2,1)S(1)}, u32[]{:S(2)}, u32[]{:S(2)}) %collective-permute-start.1) | collective-permute-done | bytes 133152 | tf_op jit(solution)/shard_map/ppermute | solution.py:144
  29.1 5.7 %collective-permute-done.4 = bf16[3,256,128]{2,1,0:T(8,128)(2,1)S(1)} collective-permute-done((bf16[3,256,128]{2,1,0:T(8,128)(2,1)S(1)}, bf16[3,256,128]{2,1,0:T(8,128)(2,1)S(1)}, u32[]{:S(2)}, u32[]{:S(2)}) %collective-permute-start.4) | collective-permute-done | bytes 196640 | tf_op jit(solution)/shard_map/ppermute | solution.py:144
  36.6 1.6 collective-permute-start.7
  40.9 5.0 %collective-permute-done.8.refs_6_ = bf16[7,256,128]{2,1,0:T(8,128)(2,1)S(1)} collective-permute-done((bf16[7,256,128]{2,1,0:T(8,128)(2,1)S(1)}, bf16[7,256,128]{2,1,0:T(8,128)(2,1)S(1)}, u32[]{:S(2)}, u32[]{:S(2)}) %collective-permute-start.8) | collective-permute-done | bytes 458784 | tf_op jit(solution)/shard_map/ppermute | solution.py:144
  45.9 3.9 %collective-permute-done.7.refs_5_ = bf16[7,264,128]{2,1,0:T(8,128)(2,1)S(1)} collective-permute-done((bf16[7,264,128]{2,1,0:T(8,128)(2,1)S(1)}, bf16[7,264,128]{2,1,0:T(8,128)(2,1)S(1)}, u32[]{:S(2)}, u32[]{:S(2)}) %collective-permute-start.7) | collective-permute-done | bytes 473120 | tf_op jit(solution)/shard_map/ppermute | solution.py:144
  50.5 5.2 %collective-permute-done.17.refs_2_ = bf16[3,192,384]{2,1,0:T(8,128)(2,1)S(1)} collective-permute-done((bf16[3,192,384]{2,1,0:T(8,128)(2,1)S(1)}, bf16[3,192,384]{2,1,0:T(8,128)(2,1)S(1)}, u32[]{:S(2)}, u32[]{:S(2)}) %collective-permute-start.17) | collective-permute-done | bytes 442400 | tf_op jit(solution)/shard_map/ppermute | solution.py:144
  55.7 2.6 %conditioning.1 = (f32[8,3072]{1,0:T(8,128)S(1)}, f32[8,384]{1,0:T(8,128)S(1)}, f32[8,384]{1,0:T(8,128)S(1)}, f32[8,384]{1,0:T(8,128)S(1)}, bf16[384,2304]{1,0:T...) custom-call(s32[4]{0:T(128)S(1)} %pad_add_fusion.at_ref, ...), custom_call_target="tpu_custom_call" | custom-call | flops 1000000000 | bytes 10000000 | tf_op jit(solution)/shard_map/conditioning/pallas_call | solution.py:287
  58.4 14.1 %front.1 = (f32[4,256,384]{2,1,0:T(8,128)S(1)}, bf16[4,256,1152]{2,1,0:T(8,128)(2,1)S(1)}, bf16[4,256,384]{2,1,0:T(8,128)(2,1)S(1)}, f32[4,256,384]{2,1,0:T(8,128)S(1)}, bf16[12,384,384]{2,1,0:T(8,128)(2,1)S(1)}) custom-call(s32[4]{0:T(128)S(1)} %pad_add_fusion.at_ref, s32[12]{0:T(128)S(1)} %copy-done.4, f32[4,16,256]{2,1,0:T(8,128)S(1)} %bitcast.76, ...), custom_call_target="tpu_custom_call" | custom-call | flops 2200000000 | bytes 12000000 | tf_op jit(solution)/shard_map/front/pallas_call | solution.py:980
  75.1 24.9 %middle.1 = (f32[4,256,384]{2,1,0:T(8,128)S(1)}, f32[4,8,384]{2,1,0:T(8,128)S(1)}, bf16[16,120,384]{2,1,0:T(8,128)(2,1)S(1)}, bf16[16,120,384]{2,1,0:T(8,128)(2,1)S(1)}, f32[24,384]{1,0:T(8,128)S(1)}) custom-call(s32[4]{0:T(128)S(1)} %pad_add_fusion.at_ref, f32[4]{0:T(128)S(1)} %copy-done.13, f32[4,256,384]{2,1,0:T(8,128)S(1)} %copy-done.15, ...), custom_call_target="tpu_custom_call" | custom-call | flops 8999999488 | bytes 14000000 | tf_op jit(solution)/shard_map/middle/pallas_call | solution.py:998
  100.6 3.7 %attention_back.2 = (bf16[1,256,384]{2,1,0:T(8,128)(2,1)S(1)}, bf16[1,256,1152]{2,1,0:T(8,128)(2,1)S(1)}, bf16[1,256,384]{2,1,0:T(8,128)(2,1)S(1)}, f32[1,8,384]{2,1,0:T(8,128)S(1)}, f32[1,16,384]{2,1,0:T(8,128)S(1)}) custom-call(f32[4,256,384]{2,1,0:T(8,128)S(1)} %get-tuple-element.101.bh1_ref, f32[4,256,384]{2,1,0:T(8,128)S(1)} %get-tuple-element.102.h0_ref, ...), custom_call_target="tpu_custom_call" | custom-call | flops 1200000000 | bytes 3000000 | tf_op jit(solution)/shard_map/attention_back/pallas_call | solution.py:1016
  104.3 11.0 %attention_back.3 = (bf16[3,256,384]{2,1,0:T(8,128)(2,1)S(1)}, bf16[3,256,1152]{2,1,0:T(8,128)(2,1)S(1)}, bf16[3,256,384]{2,1,0:T(8,128)(2,1)S(1)}, f32[3,8,384]{2,1,0:T(8,128)S(1)}, f32[3,16,384]{2,1,0:T(8,128)S(1)}) custom-call(f32[4,256,384]{2,1,0:T(8,128)S(1)} %get-tuple-element.101.bh1_ref, f32[4,256,384]{2,1,0:T(8,128)S(1)} %get-tuple-element.102.h0_ref, ...), custom_call_target="tpu_custom_call" | custom-call | flops 3600000000 | bytes 9000000 | tf_op jit(solution)/shard_map/attention_back/pallas_call | solution.py:1016
  115.3 2.4 %last_gradients.1 = (bf16[16,48,384]{2,1,0:T(8,128)(2,1)S(1)}, bf16[16,48,384]{2,1,0:T(8,128)(2,1)S(1)}) custom-call(s32[4]{0:T(128)S(1)} %pad_add_fusion.at_ref, bf16[1024,384]{1,0:T(8,128)(2,1)S(1)} %bitcast.66, bf16[256,384]{1,0:T(8,128)(2,1)S(1)} %bitcast.73, bf16[256,1152]{1,0:T(8,128)(2,1)S(1)} %bitcast.68, bf16[256,384]{1,0:T(8,128)(2,1)S(1)} %bitcast.72, ...), custom_call_target="tpu_custom_call" | custom-call | flops 1200000000 | bytes 9000000 | tf_op jit(solution)/shard_map/last_gradients/pallas_call | solution.py:1033
  118.7 1.6 collective-permute-start.29
  123.0 1.6 collective-permute-start.22
  126.1 4.2 %collective-permute-done.29.refs_1_ = bf16[4,120,384]{2,1,0:T(8,128)(2,1)S(1)} collective-permute-done((bf16[4,120,384]{2,1,0:T(8,128)(2,1)S(1)}, bf16[4,120,384]{2,1,0:T(8,128)(2,1)S(1)}, u32[]{:S(2)}, u32[]{:S(2)}) %collective-permute-start.29) | collective-permute-done | bytes 368672 | tf_op jit(solution)/shard_map/ppermute | solution.py:144
  130.2 2.5 %collective-permute-start.24 = (bf16[4,48,384]{2,1,0:T(8,128)(2,1)S(1)}, bf16[4,48,384]{2,1,0:T(8,128)(2,1)S(1)}, u32[]{:S(2)}, u32[]{:S(2)}) collective-permute-start(bf16[4,48,384]{2,1,0:T(8,128)(2,1)S(1)} %get-tuple-element.115), channel_id=1, source_target_pairs={{0,6},{1,7},{2,4},{3,5},{4,2},{5,3},{6,0},{7,1},{8,14},{9,15},{10,... | collective-permute-start | bytes 442376 | tf_op jit(solution)/shard_map/ppermute | solution.py:144
  132.7 7.0 %collective-permute-done.30.refs_2_ = bf16[4,120,384]{2,1,0:T(8,128)(2,1)S(1)} collective-permute-done((bf16[4,120,384]{2,1,0:T(8,128)(2,1)S(1)}, bf16[4,120,384]{2,1,0:T(8,128)(2,1)S(1)}, u32[]{:S(2)}, u32[]{:S(2)}) %collective-permute-start.30) | collective-permute-done | bytes 368672 | tf_op jit(solution)/shard_map/ppermute | solution.py:144
  141.3 2.9 %collective-permute-start.34 = (bf16[120,384]{1,0:T(8,128)(2,1)S(1)}, bf16[120,384]{1,0:T(8,128)(2,1)S(1)}, u32[]{:S(2)}, u32[]{:S(2)}) collective-permute-start(bf16[120,384]{1,0:T(8,128)(2,1)S(1)} %get-tuple-element.129), channel_id=1, source_target_pairs={{0,24},{1,25},{2,26},{3,27},{4,28},{5,29},{6,30},{7,31},{8,0},{9,1... | collective-permute-start | bytes 276488 | tf_op jit(solution)/shard_map/ppermute | solution.py:144
  147.5 2.0 collective-permute-done.33.refs_6_.refs_2_
  149.5 1.7 cond_back.1
  151.3 2.1 collective-permute-start.45
  158.7 2.5 %collective-permute-done.26.refs_2_ = bf16[48,384]{1,0:T(8,128)(2,1)S(1)} collective-permute-done((bf16[48,384]{1,0:T(8,128)(2,1)S(1)}, bf16[48,384]{1,0:T(8,128)(2,1)S(1)}, u32[]{:S(2)}, u32[]{:S(2)}) %collective-permute-start.26) | collective-permute-done | bytes 36896 | tf_op jit(solution)/shard_map/ppermute | solution.py:144
  162.3 1.6 collective-permute-start.48
  167.3 9.7 %collective-permute-done.36.near_ref = bf16[3,24,384]{2,1,0:T(8,128)(2,1)S(1)} collective-permute-done((bf16[3,24,384]{2,1,0:T(8,128)(2,1)S(1)}, bf16[3,24,384]{2,1,0:T(8,128)(2,1)S(1)}, u32[]{:S(2)}, u32[]{:S(2)}) %collective-permute-start.36) | collective-permute-done | bytes 55328 | tf_op jit(solution)/shard_map/ppermute | solution.py:144
  178.0 2.3 %collective-permute-start.39 = (bf16[2,3,24,384]{3,2,1,0:T(8,128)(2,1)S(1)}, bf16[2,3,24,384]{3,2,1,0:T(8,128)(2,1)S(1)}, u32[]{:S(2)}, u32[]{:S(2)}) collective-permute-start(bf16[2,3,24,384]{3,2,1,0:T(8,128)(2,1)S(1)} %join.1.refs_0_), channel_id=1, source_target_pairs={{0,16},{1,17},{2,18},{3,19},{4,20},{5,21},{6,22},{7,23},{8,24},{9,... | collective-permute-start | bytes 331784 | tf_op jit(solution)/shard_map/ppermute | solution.py:144
  180.3 4.8 %collective-permute-done.38.refs_1_ = bf16[2,3,24,384]{3,2,1,0:T(8,128)(2,1)S(1)} collective-permute-done((bf16[2,3,24,384]{3,2,1,0:T(8,128)(2,1)S(1)}, bf16[2,3,24,384]{3,2,1,0:T(8,128)(2,1)S(1)}, u32[]{:S(2)}, u32[]{:S(2)}) %collective-permute-start.38) | collective-permute-done | bytes 110624 | tf_op jit(solution)/shard_map/ppermute | solution.py:144
  186.1 2.6 %collective-permute-done.39.refs_2_ = bf16[2,3,24,384]{3,2,1,0:T(8,128)(2,1)S(1)} collective-permute-done((bf16[2,3,24,384]{3,2,1,0:T(8,128)(2,1)S(1)}, bf16[2,3,24,384]{3,2,1,0:T(8,128)(2,1)S(1)}, u32[]{:S(2)}, u32[]{:S(2)}) %collective-permute-start.39) | collective-permute-done | bytes 110624 | tf_op jit(solution)/shard_map/ppermute | solution.py:144
  189.4 4.0 %collective-permute-done.40.refs_3_ = bf16[2,3,24,384]{3,2,1,0:T(8,128)(2,1)S(1)} collective-permute-done((bf16[2,3,24,384]{3,2,1,0:T(8,128)(2,1)S(1)}, bf16[2,3,24,384]{3,2,1,0:T(8,128)(2,1)S(1)}, u32[]{:S(2)}, u32[]{:S(2)}) %collective-permute-start.40) | collective-permute-done | bytes 110624 | tf_op jit(solution)/shard_map/ppermute | solution.py:144
  197.6 2.8 %adam.1 = (f32[1,1]{1,0:T(1,128)}, f32[520,128]{1,0:T(8,128)}, f32[520,128]{1,0:T(8,128)}, f32[520,128]{1,0:T(8,128)}) custom-call(s32[4]{0:T(128)S(1)} %pad_add_fusion.at_ref, bf16[4,64,384]{2,1,0:T(8,128)(2,1)S(1)} %pad_maximum_fusion.3.refs_0_, bf16[4,64,384]{2,1,0:T(8,128)(2,1)S(1)} %collective-permute-done.48.refs_1_, ...), custom_call_target="tpu_custom_call" | custom-call | flops 1000000000 | bytes 10000000 | tf_op jit(solution)/shard_map/adam/pallas_call | solution.py:572
  204.0 6.4 %shampoo.1 = (f32[3,384,384]{2,1,0:T(8,128)}, f32[3,384,384]{2,1,0:T(8,128)}, f32[3,384,384]{2,1,0:T(8,128)}) custom-call(s32[4]{0:T(128)S(1)} %pad_add_fusion.at_ref, bf16[2,3,24,384]{3,2,1,0:T(8,128)(2,1)S(1)} %join.1.refs_0_, bf16[2,3,24,384]{3,2,1,0:T(8,128)(2,1)S(1)} %collective-permute-done.38.refs_1_, ...), custom_call_target="tpu_custom_call" | custom-call | flops 3000000000 | bytes 15000000 | tf_op jit(solution)/shard_map/shampoo/pallas_call | solution.py:642
  (158 shorter events, 54.8 us)
Async XLA Ops:
  2.5 11.4 %collective-permute-start.2 = (bf16[520,128]{1,0:T(8,128)(2,1)}, bf16[520,128]{1,0:T(8,128)(2,1)S(1)}, u32[]{:S(2)}, u32[]{:S(2)}) collective-permute-start(bf16[520,128]{1,0:T(8,128)(2,1)} %get-tuple-element.170), channel_id=1, source_target_pairs={{0,24},{1,25},{2,26},{3,27},{4,28},{5,29},{6,30},{7,31},{8,0},{9,1... | collective-permute-start | bytes 399368 | tf_op jit(solution)/shard_map/ppermute | solution.py:144
  7.6 11.6 %collective-permute-start.1 = (bf16[520,128]{1,0:T(8,128)(2,1)}, bf16[520,128]{1,0:T(8,128)(2,1)S(1)}, u32[]{:S(2)}, u32[]{:S(2)}) collective-permute-start(bf16[520,128]{1,0:T(8,128)(2,1)} %get-tuple-element.170), channel_id=1, source_target_pairs={{0,16},{1,17},{2,18},{3,19},{4,20},{5,21},{6,22},{7,23},{8,24},{9,... | collective-permute-start | bytes 399368 | tf_op jit(solution)/shard_map/ppermute | solution.py:144
  7.6 13.1 %collective-permute-start = (bf16[520,128]{1,0:T(8,128)(2,1)}, bf16[520,128]{1,0:T(8,128)(2,1)}, u32[]{:S(2)}, u32[]{:S(2)}) collective-permute-start(bf16[520,128]{1,0:T(8,128)(2,1)} %get-tuple-element.170), channel_id=1, source_target_pairs={{0,8},{1,9},{2,10},{3,11},{4,12},{5,13},{6,14},{7,15},{8,16},{9,17... | collective-permute-start | bytes 399368 | tf_op jit(solution)/shard_map/ppermute | solution.py:144
  8.6 17.8 %collective-permute-start.6 = (bf16[520,128]{1,0:T(8,128)(2,1)}, bf16[520,128]{1,0:T(8,128)(2,1)}, u32[]{:S(2)}, u32[]{:S(2)}) collective-permute-start(bf16[520,128]{1,0:T(8,128)(2,1)} %get-tuple-element.170), channel_id=1, source_target_pairs={{0,2},{1,3},{2,0},{3,1},{4,6},{5,7},{6,4},{7,5},{8,10},{9,11},{10,... | collective-permute-start | bytes 399368 | tf_op jit(solution)/shard_map/ppermute | solution.py:144
  10.1 12.9 %collective-permute-start.5 = (bf16[520,128]{1,0:T(8,128)(2,1)}, bf16[520,128]{1,0:T(8,128)(2,1)}, u32[]{:S(2)}, u32[]{:S(2)}) collective-permute-start(bf16[520,128]{1,0:T(8,128)(2,1)} %get-tuple-element.170), channel_id=1, source_target_pairs={{0,4},{1,5},{2,6},{3,7},{4,0},{5,1},{6,2},{7,3},{8,12},{9,13},{10,... | collective-permute-start | bytes 399368 | tf_op jit(solution)/shard_map/ppermute | solution.py:144
  13.9 22.6 %collective-permute-start.9 = (bf16[520,128]{1,0:T(8,128)(2,1)}, bf16[520,128]{1,0:T(8,128)(2,1)S(1)}, u32[]{:S(2)}, u32[]{:S(2)}) collective-permute-start(bf16[520,128]{1,0:T(8,128)(2,1)} %get-tuple-element.170), channel_id=1, source_target_pairs={{0,1},{1,0},{2,3},{3,2},{4,5},{5,4},{6,7},{7,6},{8,9},{9,8},{10,11... | collective-permute-start | bytes 399368 | tf_op jit(solution)/shard_map/ppermute | solution.py:144
  19.2 21.5 %collective-permute-start.16 = (bf16[3,192,384]{2,1,0:T(8,128)(2,1)S(1)}, bf16[3,192,384]{2,1,0:T(8,128)(2,1)S(1)}, u32[]{:S(2)}, u32[]{:S(2)}) collective-permute-start(bf16[3,192,384]{2,1,0:T(8,128)(2,1)S(1)} %constant_dynamic-slice_fusion), channel_id=1, source_target_pairs={{0,2},{1,3},{2,0},{3,1},{4,6},{5,7},{6,4},{7,5},{8,10},{9,11},{10,... | collective-permute-start | bytes 1327112 | tf_op jit(solution)/shard_map/ppermute | solution.py:144
  21.6 13.3 %collective-permute-start.4 = (bf16[3,256,128]{2,1,0:T(8,128)(2,1)S(1)}, bf16[3,256,128]{2,1,0:T(8,128)(2,1)S(1)}, u32[]{:S(2)}, u32[]{:S(2)}) collective-permute-start(bf16[3,256,128]{2,1,0:T(8,128)(2,1)S(1)} %pad_maximum_fusion.2), channel_id=1, source_target_pairs={{0,2},{1,3},{2,0},{3,1},{4,6},{5,7},{6,4},{7,5},{8,10},{9,11},{10,... | collective-permute-start | bytes 589832 | tf_op jit(solution)/shard_map/ppermute | solution.py:144
  23.1 11.8 %collective-permute-start.3 = (bf16[3,264,128]{2,1,0:T(8,128)(2,1)S(1)}, bf16[3,264,128]{2,1,0:T(8,128)(2,1)S(1)}, u32[]{:S(2)}, u32[]{:S(2)}) collective-permute-start(bf16[3,264,128]{2,1,0:T(8,128)(2,1)S(1)} %pad_maximum_fusion.1), channel_id=1, source_target_pairs={{0,4},{1,5},{2,6},{3,7},{4,0},{5,1},{6,2},{7,3},{8,12},{9,13},{10,... | collective-permute-start | bytes 608264 | tf_op jit(solution)/shard_map/ppermute | solution.py:144
  26.4 12.7 %collective-permute-start.10 = (bf16[256,128]{1,0:T(8,128)(2,1)S(1)}, bf16[256,128]{1,0:T(8,128)(2,1)S(1)}, u32[]{:S(2)}, u32[]{:S(2)}) collective-permute-start(bf16[256,128]{1,0:T(8,128)(2,1)S(1)} %get-tuple-element.173), channel_id=1, source_target_pairs={{0,1},{1,0},{2,3},{3,2},{4,5},{5,4},{6,7},{7,6},{8,9},{9,8},{10,11... | collective-permute-start | bytes 196616 | tf_op jit(solution)/shard_map/ppermute | solution.py:144
  34.9 11.0 %collective-permute-start.8 = (bf16[7,256,128]{2,1,0:T(8,128)(2,1)S(1)}, bf16[7,256,128]{2,1,0:T(8,128)(2,1)S(1)}, u32[]{:S(2)}, u32[]{:S(2)}) collective-permute-start(bf16[7,256,128]{2,1,0:T(8,128)(2,1)S(1)} %constant_dynamic-update-slice_fusion.4.refs_4_), channel_id=1, source_target_pairs={{0,4},{1,5},{2,6},{3,7},{4,0},{5,1},{6,2},{7,3},{8,12},{9,13},{10,... | collective-permute-start | bytes 1376264 | tf_op jit(solution)/shard_map/ppermute | solution.py:144
  36.5 13.4 %collective-permute-start.13 = (bf16[7,256,128]{2,1,0:T(8,128)(2,1)S(1)}, bf16[7,256,128]{2,1,0:T(8,128)(2,1)S(1)}, u32[]{:S(2)}, u32[]{:S(2)}) collective-permute-start(bf16[7,256,128]{2,1,0:T(8,128)(2,1)S(1)} %constant_dynamic-update-slice_fusion.4.refs_4_), channel_id=1, source_target_pairs={{0,1},{1,0},{2,3},{3,2},{4,5},{5,4},{6,7},{7,6},{8,9},{9,8},{10,11... | collective-permute-start | bytes 1376264 | tf_op jit(solution)/shard_map/ppermute | solution.py:144
  36.6 13.3 %collective-permute-start.7 = (bf16[7,264,128]{2,1,0:T(8,128)(2,1)S(1)}, bf16[7,264,128]{2,1,0:T(8,128)(2,1)S(1)}, u32[]{:S(2)}, u32[]{:S(2)}) collective-permute-start(bf16[7,264,128]{2,1,0:T(8,128)(2,1)S(1)} %constant_dynamic-update-slice_fusion.refs_3_), channel_id=1, source_target_pairs={{0,2},{1,3},{2,0},{3,1},{4,6},{5,7},{6,4},{7,5},{8,10},{9,11},{10,... | collective-permute-start | bytes 1419272 | tf_op jit(solution)/shard_map/ppermute | solution.py:144
  40.4 10.0 %collective-permute-start.12 = (bf16[7,264,128]{2,1,0:T(8,128)(2,1)S(1)}, bf16[7,264,128]{2,1,0:T(8,128)(2,1)S(1)}, u32[]{:S(2)}, u32[]{:S(2)}) collective-permute-start(bf16[7,264,128]{2,1,0:T(8,128)(2,1)S(1)} %constant_dynamic-update-slice_fusion.refs_3_), channel_id=1, source_target_pairs={{0,1},{1,0},{2,3},{3,2},{4,5},{5,4},{6,7},{7,6},{8,9},{9,8},{10,11... | collective-permute-start | bytes 1419272 | tf_op jit(solution)/shard_map/ppermute | solution.py:144
  40.6 17.7 %collective-permute-start.18 = (bf16[3,384,384]{2,1,0:T(8,128)(2,1)S(1)}, bf16[3,384,384]{2,1,0:T(8,128)(2,1)S(1)}, u32[]{:S(2)}, u32[]{:S(2)}) collective-permute-start(bf16[3,384,384]{2,1,0:T(8,128)(2,1)S(1)} %convert_element_type.47.refs_0_), channel_id=1, source_target_pairs={{0,1},{1,0},{2,3},{3,2},{4,5},{5,4},{6,7},{7,6},{8,9},{9,8},{10,11... | collective-permute-start | bytes 2654216 | tf_op jit(solution)/shard_map/ppermute | solution.py:144
  100.0 17.8 %collective-permute-start.28 = (bf16[16,120,384]{2,1,0:T(8,128)(2,1)S(1)}, bf16[16,120,384]{2,1,0:T(8,128)(2,1)S(1)}, u32[]{:S(2)}, u32[]{:S(2)}) collective-permute-start(bf16[16,120,384]{2,1,0:T(8,128)(2,1)S(1)} %get-tuple-element.121), channel_id=1, source_target_pairs={{0,1},{1,0},{2,3},{3,2},{4,5},{5,4},{6,7},{7,6},{8,9},{9,8},{10,11... | collective-permute-start | bytes 4423688 | tf_op jit(solution)/shard_map/ppermute | solution.py:144
  118.7 11.5 %collective-permute-start.29 = (bf16[4,120,384]{2,1,0:T(8,128)(2,1)S(1)}, bf16[4,120,384]{2,1,0:T(8,128)(2,1)S(1)}, u32[]{:S(2)}, u32[]{:S(2)}) collective-permute-start(bf16[4,120,384]{2,1,0:T(8,128)(2,1)S(1)} %get-tuple-element.123), channel_id=1, source_target_pairs={{0,4},{1,5},{2,6},{3,7},{4,0},{5,1},{6,2},{7,3},{8,12},{9,13},{10,... | collective-permute-start | bytes 1105928 | tf_op jit(solution)/shard_map/ppermute | solution.py:144
  120.3 19.4 %collective-permute-start.30 = (bf16[4,120,384]{2,1,0:T(8,128)(2,1)S(1)}, bf16[4,120,384]{2,1,0:T(8,128)(2,1)S(1)}, u32[]{:S(2)}, u32[]{:S(2)}) collective-permute-start(bf16[4,120,384]{2,1,0:T(8,128)(2,1)S(1)} %get-tuple-element.124), channel_id=1, source_target_pairs={{0,2},{1,3},{2,0},{3,1},{4,6},{5,7},{6,4},{7,5},{8,10},{9,11},{10,... | collective-permute-start | bytes 1105928 | tf_op jit(solution)/shard_map/ppermute | solution.py:144
  121.8 17.9 %collective-permute-start.31 = (bf16[4,120,384]{2,1,0:T(8,128)(2,1)S(1)}, bf16[4,120,384]{2,1,0:T(8,128)(2,1)S(1)}, u32[]{:S(2)}, u32[]{:S(2)}) collective-permute-start(bf16[4,120,384]{2,1,0:T(8,128)(2,1)S(1)} %get-tuple-element.125), channel_id=1, source_target_pairs={{0,6},{1,7},{2,4},{3,5},{4,2},{5,3},{6,0},{7,1},{8,14},{9,15},{10,... | collective-permute-start | bytes 1105928 | tf_op jit(solution)/shard_map/ppermute | solution.py:144
  123.0 18.4 %collective-permute-start.22 = (bf16[4,48,384]{2,1,0:T(8,128)(2,1)S(1)}, bf16[4,48,384]{2,1,0:T(8,128)(2,1)S(1)}, u32[]{:S(2)}, u32[]{:S(2)}) collective-permute-start(bf16[4,48,384]{2,1,0:T(8,128)(2,1)S(1)} %get-tuple-element.113), channel_id=1, source_target_pairs={{0,4},{1,5},{2,6},{3,7},{4,0},{5,1},{6,2},{7,3},{8,12},{9,13},{10,... | collective-permute-start | bytes 442376 | tf_op jit(solution)/shard_map/ppermute | solution.py:144
  124.5 20.7 %collective-permute-start.23 = (bf16[4,48,384]{2,1,0:T(8,128)(2,1)S(1)}, bf16[4,48,384]{2,1,0:T(8,128)(2,1)S(1)}, u32[]{:S(2)}, u32[]{:S(2)}) collective-permute-start(bf16[4,48,384]{2,1,0:T(8,128)(2,1)S(1)} %get-tuple-element.114), channel_id=1, source_target_pairs={{0,2},{1,3},{2,0},{3,1},{4,6},{5,7},{6,4},{7,5},{8,10},{9,11},{10,... | collective-permute-start | bytes 442376 | tf_op jit(solution)/shard_map/ppermute | solution.py:144
  130.2 15.0 %collective-permute-start.24 = (bf16[4,48,384]{2,1,0:T(8,128)(2,1)S(1)}, bf16[4,48,384]{2,1,0:T(8,128)(2,1)S(1)}, u32[]{:S(2)}, u32[]{:S(2)}) collective-permute-start(bf16[4,48,384]{2,1,0:T(8,128)(2,1)S(1)} %get-tuple-element.115), channel_id=1, source_target_pairs={{0,6},{1,7},{2,4},{3,5},{4,2},{5,3},{6,0},{7,1},{8,14},{9,15},{10,... | collective-permute-start | bytes 442376 | tf_op jit(solution)/shard_map/ppermute | solution.py:144
  145.8 11.3 %collective-permute-start.25 = (bf16[48,384]{1,0:T(8,128)(2,1)S(1)}, bf16[48,384]{1,0:T(8,128)(2,1)S(1)}, u32[]{:S(2)}, u32[]{:S(2)}) collective-permute-start(bf16[48,384]{1,0:T(8,128)(2,1)S(1)} %get-tuple-element.117), channel_id=1, source_target_pairs={{0,8},{1,9},{2,10},{3,11},{4,12},{5,13},{6,14},{7,15},{8,16},{9,17... | collective-permute-start | bytes 110600 | tf_op jit(solution)/shard_map/ppermute | solution.py:144
  151.3 11.0 %collective-permute-start.45 = (bf16[64,384]{1,0:T(8,128)(2,1)S(1)}, bf16[64,384]{1,0:T(8,128)(2,1)S(1)}, u32[]{:S(2)}, u32[]{:S(2)}) collective-permute-start(bf16[64,384]{1,0:T(8,128)(2,1)S(1)} %get-tuple-element.147), channel_id=1, source_target_pairs={{0,8},{1,9},{2,10},{3,11},{4,12},{5,13},{6,14},{7,15},{8,16},{9,17... | collective-permute-start | bytes 147464 | tf_op jit(solution)/shard_map/ppermute | solution.py:144
  162.3 22.8 %collective-permute-start.48 = (bf16[4,64,384]{2,1,0:T(8,128)(2,1)S(1)}, bf16[4,64,384]{2,1,0:T(8,128)(2,1)S(1)}, u32[]{:S(2)}, u32[]{:S(2)}) collective-permute-start(bf16[4,64,384]{2,1,0:T(8,128)(2,1)S(1)} %pad_maximum_fusion.3.refs_0_), channel_id=1, source_target_pairs={{0,4},{1,5},{2,6},{3,7},{4,0},{5,1},{6,2},{7,3},{8,12},{9,13},{10,... | collective-permute-start | bytes 589832 | tf_op jit(solution)/shard_map/ppermute | solution.py:144
  163.9 21.7 %collective-permute-start.49 = (bf16[4,64,384]{2,1,0:T(8,128)(2,1)S(1)}, bf16[4,64,384]{2,1,0:T(8,128)(2,1)S(1)}, u32[]{:S(2)}, u32[]{:S(2)}) collective-permute-start(bf16[4,64,384]{2,1,0:T(8,128)(2,1)S(1)} %pad_maximum_fusion.3.refs_0_), channel_id=1, source_target_pairs={{0,2},{1,3},{2,0},{3,1},{4,6},{5,7},{6,4},{7,5},{8,10},{9,11},{10,... | collective-permute-start | bytes 589832 | tf_op jit(solution)/shard_map/ppermute | solution.py:144
  164.4 21.3 %collective-permute-start.50 = (bf16[4,64,384]{2,1,0:T(8,128)(2,1)S(1)}, bf16[4,64,384]{2,1,0:T(8,128)(2,1)S(1)}, u32[]{:S(2)}, u32[]{:S(2)}) collective-permute-start(bf16[4,64,384]{2,1,0:T(8,128)(2,1)S(1)} %pad_maximum_fusion.3.refs_0_), channel_id=1, source_target_pairs={{0,6},{1,7},{2,4},{3,5},{4,2},{5,3},{6,0},{7,1},{8,14},{9,15},{10,... | collective-permute-start | bytes 589832 | tf_op jit(solution)/shard_map/ppermute | solution.py:144
  165.9 11.1 %collective-permute-start.36 = (bf16[3,24,384]{2,1,0:T(8,128)(2,1)S(1)}, bf16[3,24,384]{2,1,0:T(8,128)(2,1)S(1)}, u32[]{:S(2)}, u32[]{:S(2)}) collective-permute-start(bf16[3,24,384]{2,1,0:T(8,128)(2,1)S(1)} %get-tuple-element.132), channel_id=1, source_target_pairs={{0,2},{1,3},{2,0},{3,1},{4,6},{5,7},{6,4},{7,5},{8,10},{9,11},{10,... | collective-permute-start | bytes 165896 | tf_op jit(solution)/shard_map/ppermute | solution.py:144
  178.0 10.7 %collective-permute-start.39 = (bf16[2,3,24,384]{3,2,1,0:T(8,128)(2,1)S(1)}, bf16[2,3,24,384]{3,2,1,0:T(8,128)(2,1)S(1)}, u32[]{:S(2)}, u32[]{:S(2)}) collective-permute-start(bf16[2,3,24,384]{3,2,1,0:T(8,128)(2,1)S(1)} %join.1.refs_0_), channel_id=1, source_target_pairs={{0,16},{1,17},{2,18},{3,19},{4,20},{5,21},{6,22},{7,23},{8,24},{9,... | collective-permute-start | bytes 331784 | tf_op jit(solution)/shard_map/ppermute | solution.py:144
  185.1 10.4 %collective-permute-start.52 = (bf16[4,64,384]{2,1,0:T(8,128)(2,1)S(1)}, bf16[4,64,384]{2,1,0:T(8,128)(2,1)S(1)}, u32[]{:S(2)}, u32[]{:S(2)}) collective-permute-start(bf16[4,64,384]{2,1,0:T(8,128)(2,1)S(1)} %collective-permute-done.48.refs_1_), channel_id=1, source_target_pairs={{0,1},{1,0},{2,3},{3,2},{4,5},{5,4},{6,7},{7,6},{8,9},{9,8},{10,11... | collective-permute-start | bytes 589832 | tf_op jit(solution)/shard_map/ppermute | solution.py:144
  185.6 10.6 %collective-permute-start.53 = (bf16[4,64,384]{2,1,0:T(8,128)(2,1)S(1)}, bf16[4,64,384]{2,1,0:T(8,128)(2,1)S(1)}, u32[]{:S(2)}, u32[]{:S(2)}) collective-permute-start(bf16[4,64,384]{2,1,0:T(8,128)(2,1)S(1)} %collective-permute-done.49.refs_2_), channel_id=1, source_target_pairs={{0,1},{1,0},{2,3},{3,2},{4,5},{5,4},{6,7},{7,6},{8,9},{9,8},{10,11... | collective-permute-start | bytes 589832 | tf_op jit(solution)/shard_map/ppermute | solution.py:144
  185.7 11.8 %collective-permute-start.54 = (bf16[4,64,384]{2,1,0:T(8,128)(2,1)S(1)}, bf16[4,64,384]{2,1,0:T(8,128)(2,1)S(1)}, u32[]{:S(2)}, u32[]{:S(2)}) collective-permute-start(bf16[4,64,384]{2,1,0:T(8,128)(2,1)S(1)} %collective-permute-done.50.refs_3_), channel_id=1, source_target_pairs={{0,1},{1,0},{2,3},{3,2},{4,5},{5,4},{6,7},{7,6},{8,9},{9,8},{10,11... | collective-permute-start | bytes 589832 | tf_op jit(solution)/shard_map/ppermute | solution.py:144
  (39 other events, 521.4 us)
where the time goes:
time: 211 us; the launch traced here: 210 us
  Pallas kernels  73.3 us (35%)
  waiting for transfers between devices  69.5 us (33%)
  starting transfers between devices  52.5 us (25%)
  local copies, waits for them, and re-layouts  9.78 us (5%)
  other arithmetic  4.13 us (2%)
    ppermute x55, waiting for transfers between devices, send(): return lax.ppermute(value, AXES, pairs)  69.5 us
    ppermute x55, starting transfers between devices, send(): return lax.ppermute(value, AXES, pairs)  52.5 us
    pallas_call x1, Pallas kernels, middle(): pl.pallas_call(functools.partial(middle_kernel, images, total_img), name=...  24.9 us
    pallas_call x2, Pallas kernels, attention_back(): pl.pallas_call(functools.partial(back_kernel, first), name='attention_bac...  14.7 us
    pallas_call x1, Pallas kernels, front(): pl.pallas_call(front_kernel, name='front', grid=(images,), out_shape=(sha...  14.1 us
    pallas_call x1, Pallas kernels, shampoo(): pl.pallas_call(functools.partial(shampoo_kernel, near), name='shampoo', g...  6.41 us
    unnamed x40, local copies, waits for them, and re-layouts  6.15 us
  transfers between devices with their start and end apart: 55, of which 21 were waited for; matrix products, arithmetic and copies ran while one was open for 4% of the time, Pallas kernels for 13%

commit v1 on v0

--- a/solution.py
+++ b/solution.py
@@ -166,7 +166,7 @@
     second = jnp.stack([t[cut:] for t in turned])
     first_x = send(first, TO_X)
     second_y = send(second, TO_Y)
-    first_x, second_y, ready = lax.optimization_barrier((first_x, second_y, ready))
+    second_y, ready = lax.optimization_barrier((second_y, ready))
     first = jnp.concatenate([own_x[None, :cut], first, first_x])
     second = jnp.concatenate([own_y[None, cut:], second, second_y])
     far = [send(first, TO_Y), send(second, TO_X)]
@@ -200,11 +200,15 @@
     return places
 
 
-def gather_rows(keep, away):
+def gather_rows(away, keep, column, finish):
     turned = [send(v, TO_Z[d + 1]) for d, v in enumerate(away)]
-    column = jnp.stack([keep] + turned)
-    plane = [column] + send_plane(column)
-    return plane + [send(p, TO_C) for p in plane]
+    column = column()
+    turned, column[1] = lax.optimization_barrier((turned, column[1]))
+    plane = jnp.stack([keep] + turned)
+    plane = [plane] + send_plane(plane)
+    column = finish(column)
+    plane, column[4] = lax.optimization_barrier((plane, column[4]))
+    return plane + [send(p, TO_C) for p in plane], column
 
 
 def read_coordinates(ref):
@@ -306,26 +310,28 @@
     return [mine, near, far, send(mine, TO_C), send(near, TO_C), send(far, TO_C)]
 
 
-def fetch_blocks(at, own_ref, refs, out_ref, sems):
-    if len(refs) == 1:
-        return [pltpu.make_async_copy(refs[0], out_ref, sems.at[0])]
-    z, _, y, c = at
-    copies = []
-    odd = lax.rem(z, 2)
-    for dc in range(2):
-        core = flip(c, dc)
+def place_blocks_kernel(at_ref, own_ref, mine_ref, near_ref, far_ref, mine_c_ref, near_c_ref, far_c_ref, out_ref):
+    z, _, y, c = read_coordinates(at_ref)
+    for core, mine, near, far in ((c, mine_ref, near_ref, far_ref), (1 - c, mine_c_ref, near_c_ref, far_c_ref)):
         for t in range(3):
-            mine, near, far = refs[3 * dc : 3 * dc + 3]
-            here = own_ref[3 * (2 * y + core) + t]
+            out_ref[own_ref[3 * (2 * y + core) + t]] = mine[t]
             there = own_ref[3 * (2 * (1 - y) + core) + t]
-            for source, block, rows in (
-                (mine.at[t], here, None),
-                (near.at[t], there, pl.ds(pl.multiple_of(192 * odd, 16), 192)),
-                (far.at[t], there, pl.ds(pl.multiple_of(192 * (1 - odd), 16), 192)),
-            ):
-                target = out_ref.at[block] if rows is None else out_ref.at[block, rows]
-                copies.append(pltpu.make_async_copy(source, target, sems.at[len(copies)]))
-    return copies
+            odd = pl.multiple_of(192 * lax.rem(z, 2), 16)
+            even = pl.multiple_of(192 * (1 - lax.rem(z, 2)), 16)
+            out_ref[there, pl.ds(odd, 192), :] = near[t]
+            out_ref[there, pl.ds(even, 192), :] = far[t]
+
+
+def place_blocks(at, owner_map, parts):
+    return pl.pallas_call(
+        place_blocks_kernel,
+        name="place_blocks",
+        out_shape=shape((NBLK, D, D), BF),
+        in_specs=[SM, SM] + [VM] * 6,
+        out_specs=VM,
+        compiler_params=room(12),
+        cost_estimate=cost(1e6, 7e6),
+    )(at, owner_map, *parts)
 
 
 UNIT = 24
@@ -397,7 +403,7 @@
     out_ref[1] = near_ref[...] + far_ref[...]
 
 
-def gather_owned(at, late, early, owner_map):
+def turn_owned(at, late, early, owner_map):
     piece = (3, UNIT, D)
     own, to_c, to_y, to_cy = pl.pallas_call(
         owner_kernel,
@@ -419,7 +425,10 @@
         compiler_params=room(8),
         cost_estimate=cost(1e6, 1e6),
     )(own, pair, near, far)
-    column = [both] + [send(both, TO_Z[d]) for d in (1, 2, 3)]
+    return [both] + [send(both, TO_Z[d]) for d in (1, 2, 3)]
+
+
+def cross_owned(column):
     return column + [send(v, TO_X) for v in column]
 
 
@@ -688,19 +697,9 @@
         other_ref[u, 24 * j : 24 * j + 24, :] = other[rows]
 
 
-def front_kernel(at_ref, own_ref, noisy_ref, mods_ref, bias_ref, patch_ref, pos_ref, *refs):
-    h0_ref, qkv_ref, att_ref, h1_ref, all_ref, w_ref, in_sems, out_sem = refs[-8:]
+def front_kernel(noisy_ref, mods_ref, bias_ref, patch_ref, pos_ref, w_ref,
+                 h0_ref, qkv_ref, att_ref, h1_ref):
     i = pl.program_id(0)
-    fetch = fetch_blocks(read_coordinates(at_ref), own_ref, refs[:-8], w_ref, in_sems)
-    keep = pltpu.make_async_copy(w_ref, all_ref, out_sem)
-
-    @pl.when(i == 0)
-    def _():
-        for copy in fetch:
-            copy.start()
-        for copy in fetch:
-            copy.wait()
-        keep.start()
 
     def mod(t):
         return mods_ref[pl.ds(i, 1), D * t : D * t + D]
@@ -715,24 +714,24 @@
     qkv_ref[0, :, 0:D] = q
     qkv_ref[0, :, D : 2 * D] = k
     qkv_ref[0, :, 2 * D :] = v
-    outs = []
-    for h in range(HEADS):
-        s = mm_nt(head(q, h), head(k, h)) * QK_SCALE
-        e = jnp.exp(s - jnp.max(s, axis=-1, keepdims=True))
-        p = e * (1.0 / jnp.sum(e, axis=-1, keepdims=True))
-        outs.append(mm(p.astype(BF), head(v, h)))
+    scores, probs, outs = [], [], []
+    for h in range(HEADS + 2):
+        if h < HEADS:
+            scores.append(mm_nt(head(q, h), head(k, h)))
+        if 1 <= h <= HEADS:
+            s = scores[h - 1] * QK_SCALE
+            e = jnp.exp(s - jnp.max(s, axis=-1, keepdims=True))
+            probs.append((e * (1.0 / jnp.sum(e, axis=-1, keepdims=True))).astype(BF))
+        if h >= 2:
+            outs.append(mm(probs[h - 2], head(v, h - 2)))
     att = jnp.concatenate(outs, axis=1).astype(BF)
     att_ref[0] = att
     h1_ref[0] = h0 + mod(2) * (mm(att, w_ref[3]) + bias_ref[3:4, :])
 
-    @pl.when(i == pl.num_programs(0) - 1)
-    def _():
-        keep.wait()
-
 
 def middle_kernel(images, total_img, at_ref, tw_ref, h1_ref, vel_ref, dino_ref, mods_ref, bias_ref, w_ref, aw_ref, fw_ref,
                   bh1_ref, gm_ref, mine_ref, other_ref, sums_ref,
-                  act2_s, gelu_s, slope_s, bi_s, bb2_s, h1_s, ba_s, act3_s, bo_s):
+                  act2_s, gelu_s, slope_s, bi_s, bb2_s, h1_s, ba_s, act3_s, bo_s, up_s):
     i = pl.program_id(0)
     rows = pl.ds(pl.multiple_of(i * SEQ, SEQ), SEQ)
 
@@ -742,22 +741,25 @@
     @pl.when(i == 0)
     def _():
         sums_ref[...] = jnp.zeros_like(sums_ref)
+        for j in range(4):
+            up_s[:, D * j : D * j + D] = w_ref[4 + j]
 
     h1 = h1_ref[0]
     n2, inv2 = norm_stats(h1)
     act2 = (n2 * (1.0 + mod(4)) + mod(3)).astype(BF)
     act2_s[rows, :] = act2
     branch = jnp.zeros((SEQ, D), F32) + bias_ref[8:9, :]
-    for j in range(4):
-        lanes = slice(D * j, D * j + D)
-        x = mm(act2, w_ref[4 + j]) + bias_ref[4 + j : 5 + j, :]
+    for j in range(2):
+        lanes = slice(2 * D * j, 2 * D * j + 2 * D)
+        bias = jnp.concatenate([bias_ref[4 + 2 * j : 5 + 2 * j, :], bias_ref[5 + 2 * j : 6 + 2 * j, :]], axis=1)
+        x = mm(act2, up_s[:, lanes]) + bias
         xx = x * x
         t = jnp.tanh(x * (GELU_C + (GELU_C * GELU_D) * xx))
         half = 0.5 + 0.5 * t
         g = (x * half).astype(BF)
         slope_s[:, lanes] = half + (0.5 * x) * (1.0 - t * t) * (GELU_C + (3.0 * GELU_C * GELU_D) * xx)
         gelu_s[rows, lanes] = g
-        branch = branch + mm(g, w_ref[8 + j])
+        branch = branch + mm(g, w_ref[8 + 2 * j : 10 + 2 * j].reshape(2 * D, D))
     h2 = h1 + mod(5) * branch
     n3, inv3 = norm_stats(h2)
     act3 = (n3 * (1.0 + mod(7)) + mod(6)).astype(BF)
@@ -790,12 +792,14 @@
     bb2 = (bh2 * mod(5)).astype(BF)
     bb2_s[rows, :] = bb2
     b2 = jnp.zeros((SEQ, D), F32)
-    for j in range(4):
-        lanes = slice(D * j, D * j + D)
-        bi = (mm_nt(bb2, w_ref[8 + j]) * slope_s[:, lanes]).astype(BF)
+    for j in range(2):
+        lanes = slice(2 * D * j, 2 * D * j + 2 * D)
+        bi = (mm_nt(bb2, w_ref[8 + 2 * j : 10 + 2 * j].reshape(2 * D, D)) * slope_s[:, lanes]).astype(BF)
         bi_s[rows, lanes] = bi
-        sums_ref[16 + j : 17 + j, :] += column_sum(bi.astype(F32))
-        b2 = b2 + mm_nt(bi, w_ref[4 + j])
+        bi_sum = column_sum(bi.astype(F32))
+        sums_ref[16 + 2 * j : 17 + 2 * j, :] += bi_sum[:, :D]
+        sums_ref[17 + 2 * j : 18 + 2 * j, :] += bi_sum[:, D:]
+        b2 = b2 + mm_nt(bi, up_s[:, lanes])
     sums_ref[20:21, :] += column_sum(bb2.astype(F32))
     ba_sum = column_sum(ba.astype(F32))
     sums_ref[21:22, :] += ba_sum[:, :D]
@@ -813,10 +817,14 @@
     @pl.when(i == images - 1)
     def _():
         put = functools.partial(put_pair, at_ref[3], mine_ref, other_ref)
-        for j in range(4):
-            lanes = slice(D * j, D * j + D)
-            put(j, mm_tn(act2_s[...], bi_s[:, lanes]), mm_tn(gelu_s[:, lanes], bb2_s[...]))
-        put(4, mm_tn(h1_s[...], ba_s[:, 0:D]), mm_tn(h1_s[...], ba_s[:, D:]))
+        for j in range(2):
+            lanes = slice(2 * D * j, 2 * D * j + 2 * D)
+            up = mm_tn(act2_s[...], bi_s[:, lanes]).astype(BF)
+            down = mm_tn(bb2_s[...], gelu_s[:, lanes]).astype(BF)
+            put(2 * j, up[:, :D], down[:, :D].T)
+            put(2 * j + 1, up[:, D:], down[:, D:].T)
+        align = mm_tn(h1_s[...], ba_s[...])
+        put(4, align[:, :D], align[:, D:])
         g = mm_tn(act3_s[...], bo_s[...]).astype(BF)
         spread = (lax.broadcasted_iota(jnp.int32, (128, 128), 1) % PD
                   == lax.broadcasted_iota(jnp.int32, (128, 128), 0)).astype(F32).astype(BF)
@@ -843,17 +851,21 @@
     gm_ref[0, 2:3, :] = column_sum(bh1 * (mm(att, w_ref[3]) + bias_ref[3:4, :]))
     batt = mm_nt(bb1, w_ref[3]).astype(BF)
     q, k, v = qkv_ref[0, :, 0:D], qkv_ref[0, :, D : 2 * D], qkv_ref[0, :, 2 * D :]
-    gq, gk, gv = [], [], []
-    for h in range(HEADS):
-        qh, kh, vh, bh = head(q, h), head(k, h), head(v, h), head(batt, h)
-        s = mm_nt(kh, qh) * QK_SCALE
-        e = jnp.exp(s - jnp.max(s, axis=0, keepdims=True))
-        p = e * (1.0 / column_sum(e))
-        dp = mm_nt(vh, bh)
-        ds = (p * (dp - column_sum(dp * p))).astype(BF)
-        gv.append(mm(p.astype(BF), bh))
-        gk.append(mm(ds, qh))
-        gq.append(mm_tn(ds, kh))
+    ready, halves, gq, gk, gv = [], [], [], [], []
+    for h in range(HEADS + 2):
+        if h < HEADS:
+            ready.append((mm_nt(head(k, h), head(q, h)), mm_nt(head(v, h), head(batt, h))))
+        if 1 <= h <= HEADS:
+            s, dp = ready[h - 1]
+            s = s * QK_SCALE
+            e = jnp.exp(s - jnp.max(s, axis=0, keepdims=True))
+            p = e * (1.0 / column_sum(e))
+            halves.append((p.astype(BF), (p * (dp - column_sum(dp * p))).astype(BF)))
+        if h >= 2:
+            p, ds = halves[h - 2]
+            gv.append(mm(p, head(batt, h - 2)))
+            gk.append(mm(ds, head(q, h - 2)))
+            gq.append(mm_tn(ds, head(k, h - 2)))
     bq = (jnp.concatenate(gq, axis=1) * QK_SCALE).astype(BF)
     bk = (jnp.concatenate(gk, axis=1) * QK_SCALE).astype(BF)
     bv = jnp.concatenate(gv, axis=1).astype(BF)
@@ -973,22 +985,20 @@
     return pl.BlockSpec((1,) + dims, lambda i: (i + first,) + (0,) * len(dims))
 
 
-def front(at, owner_map, noisy, mods, bias, patch_low, pos, pieces):
+def front(noisy, mods, bias, patch_low, pos, blocks):
     images = noisy.shape[0]
     each = functools.partial(rows_each, 0)
-    anywhere = pl.BlockSpec(memory_space=pl.ANY)
     return pl.pallas_call(
         front_kernel,
         name="front",
         grid=(images,),
         out_shape=(shape((images, SEQ, D)), shape((images, SEQ, 3 * D), BF),
-                   shape((images, SEQ, D), BF), shape((images, SEQ, D)), shape((NBLK, D, D), BF)),
-        in_specs=[SM, SM, each(PD, SEQ), VM, VM, VM, VM] + [anywhere] * len(pieces),
-        out_specs=[each(SEQ, D), each(SEQ, 3 * D), each(SEQ, D), each(SEQ, D), anywhere],
-        scratch_shapes=[pltpu.VMEM((NBLK, D, D), BF), pltpu.SemaphoreType.DMA((18,)), pltpu.SemaphoreType.DMA(())],
+                   shape((images, SEQ, D), BF), shape((images, SEQ, D))),
+        in_specs=[each(PD, SEQ), VM, VM, VM, VM, VM],
+        out_specs=[each(SEQ, D), each(SEQ, 3 * D), each(SEQ, D), each(SEQ, D)],
         compiler_params=room(24),
         cost_estimate=cost(2.2e9, 1.2e7),
-    )(at, owner_map, noisy, mods, bias, patch_low, pos, *pieces)
+    )(noisy, mods, bias, patch_low, pos, blocks)
 
 
 def middle(total_img, at, time_weight, h1, velocity, dino, mods, bias, blocks, align_low, final_low):
@@ -1004,7 +1014,7 @@
         in_specs=[SM, SM, each(SEQ, D), each(PD, SEQ), each(SEQ, DINO), VM, VM, VM, VM, VM],
         out_specs=[each(SEQ, D), each(8, D), VM, VM, VM],
         scratch_shapes=[full(D), full(F), pltpu.VMEM((SEQ, F), F32), full(F), full(D), full(D),
-                        full(DINO), full(D), full(128)],
+                        full(DINO), full(D), full(128), pltpu.VMEM((D, F), BF)],
         compiler_params=room(40),
         cost_estimate=cost(9e9, 1.4e7),
     )(at, time_weight, h1, velocity, dino, mods, bias, blocks, align_low, final_low)
@@ -1108,6 +1118,7 @@
         block_parts = gather_blocks(blocks_w.astype(BF))
         pieces, (at, features, pos) = gather_flat(mine, cut, (at, features, pos))
         places = flat_places(cut)
+        blocks = place_blocks(at, owner_map, block_parts)
     else:
         pieces = [lax.all_gather(mine, AXES, axis=0, tiled=True)[None]]
         places = [(0, lambda i, at: 0)]
@@ -1116,10 +1127,10 @@
         slot_of = jnp.sum(
             block_ids[:, None] * (owner_map[:, None] == block_ids[None, :]).astype(jnp.int32), axis=0
         )
-        block_parts = [jnp.take(slot_low, slot_of, axis=0)]
+        blocks = jnp.take(slot_low, slot_of, axis=0)
     (mods, pre, th, cond, mod_w, fmod_w, tout_w, align_low, bias, patch_low, final_low) = conditioning(
         at, class_ids, features, pieces, places, rows)
-    h0, qkv, att, h1, blocks = front(at, owner_map, noisy, mods, bias, patch_low, pos, block_parts)
+    h0, qkv, att, h1 = front(noisy, mods, bias, patch_low, pos, blocks)
     bh1, gm2, mine, other, sums = middle(
         total_img, at, time_weight, h1, velocity, dino, mods, bias, blocks, align_low, final_low)
     if near:
@@ -1135,8 +1146,8 @@
         images, at, class_ids, gm2, pre, th, cond, features, mod_w, fmod_w, tout_w, sums, aligns, gm3)
     if near:
         late = reduce_units(at, late_mine, late_other)
-        grads = gather_owned(at, late, early, owner_map)
-        parts = gather_rows(keep, away)
+        parts, grads = gather_rows(
+            away, keep, lambda: turn_owned(at, late, early, owner_map), cross_owned)
         loss, upd, new_m, new_v = adam_near(at, parts, flat_w, flat_m, flat_v)
         *grads, loss, upd, new_m, new_v = lax.optimization_barrier((*grads, loss, upd, new_m, new_v))
     else:

time: 211 us -> 192 us (0.910)
  Pallas kernels: 73.3 us -> 60.2 us
  starting transfers between devices: 52.5 us -> 49.1 us
  local copies, waits for them, and re-layouts: 9.78 us -> 7.24 us
    pallas_call x1, Pallas kernels: 14.1 us -> 8.9 us  [front(): pl.pallas_call(front_kernel, name='front', grid=(images,), out_shape=(sha...]
    pallas_call x1, Pallas kernels: 24.9 us -> 20 us  [middle(): pl.pallas_call(functools.partial(middle_kernel, images, total_img), name=...]
    pallas_call x2, Pallas kernels: 14.7 us -> 10.9 us  [attention_back(): pl.pallas_call(functools.partial(back_kernel, first), name='attention_bac...]
    ppermute x55, starting transfers between devices: 52.5 us -> 49.1 us  [send(): return lax.ppermute(value, AXES, pairs)]
    unnamed x40 -> x36, local copies, waits for them, and re-layouts: 6.15 us -> 3.61 us
  transfers between devices with their start and end apart: 55 -> 55, of which waited for: 21 -> 23; matrix products, arithmetic and copies ran while one was open for 4% -> 5% of each run, Pallas kernels for 13% -> 12%
where the time goes in v1:
time: 192 us
  waiting for transfers between devices  69.6 us (36%)
  Pallas kernels  60.2 us (31%)
  starting transfers between devices  49.1 us (26%)
  local copies, waits for them, and re-layouts  7.24 us (4%)
  other arithmetic  4.13 us (2%)
    ppermute x55, waiting for transfers between devices, send(): return lax.ppermute(value, AXES, pairs)  69.6 us
    ppermute x55, starting transfers between devices, send(): return lax.ppermute(value, AXES, pairs)  49.1 us
    pallas_call x1, Pallas kernels, middle(): pl.pallas_call(functools.partial(middle_kernel, images, total_img), name=...  20 us
    pallas_call x2, Pallas kernels, attention_back(): pl.pallas_call(functools.partial(back_kernel, first), name='attention_bac...  10.9 us
    pallas_call x1, Pallas kernels, front(): pl.pallas_call(front_kernel, name='front', grid=(images,), out_shape=(sha...  8.9 us
    pallas_call x1, Pallas kernels, shampoo(): pl.pallas_call(functools.partial(shampoo_kernel, near), name='shampoo', g...  6.47 us
  transfers between devices with their start and end apart: 55, of which 23 were waited for; matrix products, arithmetic and copies ran while one was open for 5% of the time, Pallas kernels for 12%

profile of v1, /device:TPU:0, one launch (start us, length us, event | category | flops | bytes accessed | tf_op | source)
XLA Modules:
  0.0 191.5 jit_solution(16428756889681768065)
XLA Ops:
  0.6 1.9 convert_bitcast_fusion
  2.5 5.1 %collective-permute-start.2 = (bf16[520,128]{1,0:T(8,128)(2,1)}, bf16[520,128]{1,0:T(8,128)(2,1)S(1)}, u32[]{:S(2)}, u32[]{:S(2)}) collective-permute-start(bf16[520,128]{1,0:T(8,128)(2,1)} %get-tuple-element.184), channel_id=1, source_target_pairs={{0,24},{1,25},{2,26},{3,27},{4,28},{5,29},{6,30},{7,31},{8,0},{9,1... | collective-permute-start | bytes 399368 | tf_op jit(solution)/shard_map/ppermute | solution.py:144
  14.0 5.1 %collective-permute-done.1 = bf16[520,128]{1,0:T(8,128)(2,1)S(1)} collective-permute-done((bf16[520,128]{1,0:T(8,128)(2,1)}, bf16[520,128]{1,0:T(8,128)(2,1)S(1)}, u32[]{:S(2)}, u32[]{:S(2)}) %collective-permute-start.1) | collective-permute-done | bytes 133152 | tf_op jit(solution)/shard_map/ppermute | solution.py:144
  29.1 5.7 %collective-permute-done.3 = bf16[3,256,128]{2,1,0:T(8,128)(2,1)S(1)} collective-permute-done((bf16[3,256,128]{2,1,0:T(8,128)(2,1)S(1)}, bf16[3,256,128]{2,1,0:T(8,128)(2,1)S(1)}, u32[]{:S(2)}, u32[]{:S(2)}) %collective-permute-start.3) | collective-permute-done | bytes 196640 | tf_op jit(solution)/shard_map/ppermute | solution.py:144
  36.6 1.6 collective-permute-start.7
  40.9 5.0 %collective-permute-done.8.refs_6_ = bf16[7,256,128]{2,1,0:T(8,128)(2,1)S(1)} collective-permute-done((bf16[7,256,128]{2,1,0:T(8,128)(2,1)S(1)}, bf16[7,256,128]{2,1,0:T(8,128)(2,1)S(1)}, u32[]{:S(2)}, u32[]{:S(2)}) %collective-permute-start.8) | collective-permute-done | bytes 458784 | tf_op jit(solution)/shard_map/ppermute | solution.py:144
  45.9 4.0 %collective-permute-done.7.refs_5_ = bf16[7,264,128]{2,1,0:T(8,128)(2,1)S(1)} collective-permute-done((bf16[7,264,128]{2,1,0:T(8,128)(2,1)S(1)}, bf16[7,264,128]{2,1,0:T(8,128)(2,1)S(1)}, u32[]{:S(2)}, u32[]{:S(2)}) %collective-permute-start.7) | collective-permute-done | bytes 473120 | tf_op jit(solution)/shard_map/ppermute | solution.py:144
  50.5 5.2 %collective-permute-done.17.far_ref = bf16[3,192,384]{2,1,0:T(8,128)(2,1)S(1)} collective-permute-done((bf16[3,192,384]{2,1,0:T(8,128)(2,1)S(1)}, bf16[3,192,384]{2,1,0:T(8,128)(2,1)S(1)}, u32[]{:S(2)}, u32[]{:S(2)}) %collective-permute-start.17) | collective-permute-done | bytes 442400 | tf_op jit(solution)/shard_map/ppermute | solution.py:144
  55.7 2.6 %conditioning.1 = (f32[8,3072]{1,0:T(8,128)S(1)}, f32[8,384]{1,0:T(8,128)S(1)}, f32[8,384]{1,0:T(8,128)S(1)}, f32[8,384]{1,0:T(8,128)S(1)}, bf16[384,2304]{1,0:T...) custom-call(s32[4]{0:T(128)S(1)} %pad_add_fusion.at_ref, ...), custom_call_target="tpu_custom_call" | custom-call | flops 1000000000 | bytes 10000000 | tf_op jit(solution)/shard_map/conditioning/pallas_call | solution.py:291
  59.3 8.9 %front.1 = (f32[4,256,384]{2,1,0:T(8,128)S(1)}, bf16[4,256,1152]{2,1,0:T(8,128)(2,1)S(1)}, bf16[4,256,384]{2,1,0:T(8,128)(2,1)S(1)}, f32[4,256,384]{2,1,0:T(8,128)S(1)}) custom-call(f32[4,16,256]{2,1,0:T(8,128)S(1)} %bitcast.76, f32[8,3072]{1,0:T(8,128)S(1)} %get-tuple-element.98.mods_ref, f32[16,384]{1,0:T(8,128)S(1)} %get-tuple-element.99.bias_ref, ...), custom_call_target="tpu_custom_call" | custom-call | flops 2200000000 | bytes 12000000 | tf_op jit(solution)/shard_map/front/pallas_call | solution.py:991
  68.2 20.0 %middle.1 = (f32[4,256,384]{2,1,0:T(8,128)S(1)}, f32[4,8,384]{2,1,0:T(8,128)S(1)}, bf16[16,120,384]{2,1,0:T(8,128)(2,1)S(1)}, bf16[16,120,384]{2,1,0:T(8,128)(2,1)S(1)}, f32[24,384]{1,0:T(8,128)S(1)}) custom-call(s32[4]{0:T(128)S(1)} %pad_add_fusion.at_ref, f32[4]{0:T(128)S(1)} %copy-done.13, f32[4,256,384]{2,1,0:T(8,128)S(1)} %get-tuple-element.103.h1_ref, ...), custom_call_target="tpu_custom_call" | custom-call | flops 8999999488 | bytes 14000000 | tf_op jit(solution)/shard_map/middle/pallas_call | solution.py:1008
  88.8 2.7 %attention_back.2 = (bf16[1,256,384]{2,1,0:T(8,128)(2,1)S(1)}, bf16[1,256,1152]{2,1,0:T(8,128)(2,1)S(1)}, bf16[1,256,384]{2,1,0:T(8,128)(2,1)S(1)}, f32[1,8,384]{2,1,0:T(8,128)S(1)}, f32[1,16,384]{2,1,0:T(8,128)S(1)}) custom-call(f32[4,256,384]{2,1,0:T(8,128)S(1)} %get-tuple-element.106.bh1_ref, f32[4,256,384]{2,1,0:T(8,128)S(1)} %get-tuple-element.107.h0_ref, ...), custom_call_target="tpu_custom_call" | custom-call | flops 1200000000 | bytes 3000000 | tf_op jit(solution)/shard_map/attention_back/pallas_call | solution.py:1026
  91.5 8.2 %attention_back.3 = (bf16[3,256,384]{2,1,0:T(8,128)(2,1)S(1)}, bf16[3,256,1152]{2,1,0:T(8,128)(2,1)S(1)}, bf16[3,256,384]{2,1,0:T(8,128)(2,1)S(1)}, f32[3,8,384]{2,1,0:T(8,128)S(1)}, f32[3,16,384]{2,1,0:T(8,128)S(1)}) custom-call(f32[4,256,384]{2,1,0:T(8,128)S(1)} %get-tuple-element.106.bh1_ref, f32[4,256,384]{2,1,0:T(8,128)S(1)} %get-tuple-element.107.h0_ref, ...), custom_call_target="tpu_custom_call" | custom-call | flops 3600000000 | bytes 9000000 | tf_op jit(solution)/shard_map/attention_back/pallas_call | solution.py:1026
  99.7 2.4 %last_gradients.1 = (bf16[16,48,384]{2,1,0:T(8,128)(2,1)S(1)}, bf16[16,48,384]{2,1,0:T(8,128)(2,1)S(1)}) custom-call(s32[4]{0:T(128)S(1)} %pad_add_fusion.at_ref, bf16[1024,384]{1,0:T(8,128)(2,1)S(1)} %bitcast.66, bf16[256,384]{1,0:T(8,128)(2,1)S(1)} %bitcast.73, bf16[256,1152]{1,0:T(8,128)(2,1)S(1)} %bitcast.68, bf16[256,384]{1,0:T(8,128)(2,1)S(1)} %bitcast.72, ...), custom_call_target="tpu_custom_call" | custom-call | flops 1200000000 | bytes 9000000 | tf_op jit(solution)/shard_map/last_gradients/pallas_call | solution.py:1043
  110.4 4.2 %collective-permute-done.29.refs_1_ = bf16[4,120,384]{2,1,0:T(8,128)(2,1)S(1)} collective-permute-done((bf16[4,120,384]{2,1,0:T(8,128)(2,1)S(1)}, bf16[4,120,384]{2,1,0:T(8,128)(2,1)S(1)}, u32[]{:S(2)}, u32[]{:S(2)}) %collective-permute-start.29) | collective-permute-done | bytes 368672 | tf_op jit(solution)/shard_map/ppermute | solution.py:144
  114.6 2.5 %collective-permute-start.24 = (bf16[4,48,384]{2,1,0:T(8,128)(2,1)S(1)}, bf16[4,48,384]{2,1,0:T(8,128)(2,1)S(1)}, u32[]{:S(2)}, u32[]{:S(2)}) collective-permute-start(bf16[4,48,384]{2,1,0:T(8,128)(2,1)S(1)} %get-tuple-element.120), channel_id=1, source_target_pairs={{0,6},{1,7},{2,4},{3,5},{4,2},{5,3},{6,0},{7,1},{8,14},{9,15},{10,... | collective-permute-start | bytes 442376 | tf_op jit(solution)/shard_map/ppermute | solution.py:144
  117.1 7.0 %collective-permute-done.30.refs_2_ = bf16[4,120,384]{2,1,0:T(8,128)(2,1)S(1)} collective-permute-done((bf16[4,120,384]{2,1,0:T(8,128)(2,1)S(1)}, bf16[4,120,384]{2,1,0:T(8,128)(2,1)S(1)}, u32[]{:S(2)}, u32[]{:S(2)}) %collective-permute-start.30) | collective-permute-done | bytes 368672 | tf_op jit(solution)/shard_map/ppermute | solution.py:144
  125.7 2.9 %collective-permute-start.34 = (bf16[120,384]{1,0:T(8,128)(2,1)S(1)}, bf16[120,384]{1,0:T(8,128)(2,1)S(1)}, u32[]{:S(2)}, u32[]{:S(2)}) collective-permute-start(bf16[120,384]{1,0:T(8,128)(2,1)S(1)} %get-tuple-element.134), channel_id=1, source_target_pairs={{0,24},{1,25},{2,26},{3,27},{4,28},{5,29},{6,30},{7,31},{8,0},{9,1... | collective-permute-start | bytes 276488 | tf_op jit(solution)/shard_map/ppermute | solution.py:144
  131.5 4.7 %collective-permute-done.25.refs_1_ = bf16[48,384]{1,0:T(8,128)(2,1)S(1)} collective-permute-done((bf16[48,384]{1,0:T(8,128)(2,1)S(1)}, bf16[48,384]{1,0:T(8,128)(2,1)S(1)}, u32[]{:S(2)}, u32[]{:S(2)}) %collective-permute-start.25) | collective-permute-done | bytes 36896 | tf_op jit(solution)/shard_map/ppermute | solution.py:144
  136.1 1.7 collective-permute-done.26.refs_2_
  137.8 2.3 %collective-permute-done.27.refs_3_ = bf16[48,384]{1,0:T(8,128)(2,1)S(1)} collective-permute-done((bf16[48,384]{1,0:T(8,128)(2,1)S(1)}, bf16[48,384]{1,0:T(8,128)(2,1)S(1)}, u32[]{:S(2)}, u32[]{:S(2)}) %collective-permute-start.27) | collective-permute-done | bytes 36896 | tf_op jit(solution)/shard_map/ppermute | solution.py:144
  140.9 1.6 collective-permute-start.36
  142.7 2.4 %collective-permute-done.36.near_ref = bf16[3,24,384]{2,1,0:T(8,128)(2,1)S(1)} collective-permute-done((bf16[3,24,384]{2,1,0:T(8,128)(2,1)S(1)}, bf16[3,24,384]{2,1,0:T(8,128)(2,1)S(1)}, u32[]{:S(2)}, u32[]{:S(2)}) %collective-permute-start.36) | collective-permute-done | bytes 55328 | tf_op jit(solution)/shard_map/ppermute | solution.py:144
  146.4 1.7 cond_back.1
  149.6 3.0 %collective-permute-start.39 = (bf16[64,384]{1,0:T(8,128)(2,1)S(1)}, bf16[64,384]{1,0:T(8,128)(2,1)S(1)}, u32[]{:S(2)}, u32[]{:S(2)}) collective-permute-start(bf16[64,384]{1,0:T(8,128)(2,1)S(1)} %get-tuple-element.152), channel_id=1, source_target_pairs={{0,16},{1,17},{2,18},{3,19},{4,20},{5,21},{6,22},{7,23},{8,24},{9,... | collective-permute-start | bytes 147464 | tf_op jit(solution)/shard_map/ppermute | solution.py:144
  153.4 1.6 collective-permute-done.38
  158.9 1.7 collective-permute-start.46
  162.0 8.0 %collective-permute-done.47.refs_4_ = bf16[2,3,24,384]{3,2,1,0:T(8,128)(2,1)S(1)} collective-permute-done((bf16[2,3,24,384]{3,2,1,0:T(8,128)(2,1)S(1)}, bf16[2,3,24,384]{3,2,1,0:T(8,128)(2,1)S(1)}, u32[]{:S(2)}, u32[]{:S(2)}) %collective-permute-start.47) | collective-permute-done | bytes 110624 | tf_op jit(solution)/shard_map/ppermute | solution.py:144
  172.1 4.0 %collective-permute-done.43.refs_3_ = bf16[2,3,24,384]{3,2,1,0:T(8,128)(2,1)S(1)} collective-permute-done((bf16[2,3,24,384]{3,2,1,0:T(8,128)(2,1)S(1)}, bf16[2,3,24,384]{3,2,1,0:T(8,128)(2,1)S(1)}, u32[]{:S(2)}, u32[]{:S(2)}) %collective-permute-start.43) | collective-permute-done | bytes 110624 | tf_op jit(solution)/shard_map/ppermute | solution.py:144
  179.2 2.8 %adam.1 = (f32[1,1]{1,0:T(1,128)}, f32[520,128]{1,0:T(8,128)}, f32[520,128]{1,0:T(8,128)}, f32[520,128]{1,0:T(8,128)}) custom-call(s32[4]{0:T(128)S(1)} %pad_add_fusion.at_ref, bf16[4,64,384]{2,1,0:T(8,128)(2,1)S(1)} %pad_maximum_fusion.3.refs_0_, bf16[4,64,384]{2,1,0:T(8,128)(2,1)S(1)} %collective-permute-done.44.refs_1_, ...), custom_call_target="tpu_custom_call" | custom-call | flops 1000000000 | bytes 10000000 | tf_op jit(solution)/shard_map/adam/pallas_call | solution.py:581
  182.0 1.8 collective-permute-done.49.refs_6_
  185.1 6.5 %shampoo.1 = (f32[3,384,384]{2,1,0:T(8,128)}, f32[3,384,384]{2,1,0:T(8,128)}, f32[3,384,384]{2,1,0:T(8,128)}) custom-call(s32[4]{0:T(128)S(1)} %pad_add_fusion.at_ref, bf16[2,3,24,384]{3,2,1,0:T(8,128)(2,1)S(1)} %join.1.refs_0_, bf16[2,3,24,384]{3,2,1,0:T(8,128)(2,1)S(1)} %collective-permute-done.41.refs_1_, ...), custom_call_target="tpu_custom_call" | custom-call | flops 3000000000 | bytes 15000000 | tf_op jit(solution)/shard_map/shampoo/pallas_call | solution.py:651
  (155 shorter events, 51.8 us)
Async XLA Ops:
  2.5 11.4 %collective-permute-start.2 = (bf16[520,128]{1,0:T(8,128)(2,1)}, bf16[520,128]{1,0:T(8,128)(2,1)S(1)}, u32[]{:S(2)}, u32[]{:S(2)}) collective-permute-start(bf16[520,128]{1,0:T(8,128)(2,1)} %get-tuple-element.184), channel_id=1, source_target_pairs={{0,24},{1,25},{2,26},{3,27},{4,28},{5,29},{6,30},{7,31},{8,0},{9,1... | collective-permute-start | bytes 399368 | tf_op jit(solution)/shard_map/ppermute | solution.py:144
  7.6 11.6 %collective-permute-start.1 = (bf16[520,128]{1,0:T(8,128)(2,1)}, bf16[520,128]{1,0:T(8,128)(2,1)S(1)}, u32[]{:S(2)}, u32[]{:S(2)}) collective-permute-start(bf16[520,128]{1,0:T(8,128)(2,1)} %get-tuple-element.184), channel_id=1, source_target_pairs={{0,16},{1,17},{2,18},{3,19},{4,20},{5,21},{6,22},{7,23},{8,24},{9,... | collective-permute-start | bytes 399368 | tf_op jit(solution)/shard_map/ppermute | solution.py:144
  7.6 13.1 %collective-permute-start = (bf16[520,128]{1,0:T(8,128)(2,1)}, bf16[520,128]{1,0:T(8,128)(2,1)}, u32[]{:S(2)}, u32[]{:S(2)}) collective-permute-start(bf16[520,128]{1,0:T(8,128)(2,1)} %get-tuple-element.184), channel_id=1, source_target_pairs={{0,8},{1,9},{2,10},{3,11},{4,12},{5,13},{6,14},{7,15},{8,16},{9,17... | collective-permute-start | bytes 399368 | tf_op jit(solution)/shard_map/ppermute | solution.py:144
  8.6 17.8 %collective-permute-start.5 = (bf16[520,128]{1,0:T(8,128)(2,1)}, bf16[520,128]{1,0:T(8,128)(2,1)}, u32[]{:S(2)}, u32[]{:S(2)}) collective-permute-start(bf16[520,128]{1,0:T(8,128)(2,1)} %get-tuple-element.184), channel_id=1, source_target_pairs={{0,2},{1,3},{2,0},{3,1},{4,6},{5,7},{6,4},{7,5},{8,10},{9,11},{10,... | collective-permute-start | bytes 399368 | tf_op jit(solution)/shard_map/ppermute | solution.py:144
  10.1 12.9 %collective-permute-start.4 = (bf16[520,128]{1,0:T(8,128)(2,1)}, bf16[520,128]{1,0:T(8,128)(2,1)}, u32[]{:S(2)}, u32[]{:S(2)}) collective-permute-start(bf16[520,128]{1,0:T(8,128)(2,1)} %get-tuple-element.184), channel_id=1, source_target_pairs={{0,4},{1,5},{2,6},{3,7},{4,0},{5,1},{6,2},{7,3},{8,12},{9,13},{10,... | collective-permute-start | bytes 399368 | tf_op jit(solution)/shard_map/ppermute | solution.py:144
  13.9 22.6 %collective-permute-start.9 = (bf16[520,128]{1,0:T(8,128)(2,1)}, bf16[520,128]{1,0:T(8,128)(2,1)S(1)}, u32[]{:S(2)}, u32[]{:S(2)}) collective-permute-start(bf16[520,128]{1,0:T(8,128)(2,1)} %get-tuple-element.184), channel_id=1, source_target_pairs={{0,1},{1,0},{2,3},{3,2},{4,5},{5,4},{6,7},{7,6},{8,9},{9,8},{10,11... | collective-permute-start | bytes 399368 | tf_op jit(solution)/shard_map/ppermute | solution.py:144
  19.2 21.5 %collective-permute-start.16 = (bf16[3,192,384]{2,1,0:T(8,128)(2,1)S(1)}, bf16[3,192,384]{2,1,0:T(8,128)(2,1)S(1)}, u32[]{:S(2)}, u32[]{:S(2)}) collective-permute-start(bf16[3,192,384]{2,1,0:T(8,128)(2,1)S(1)} %constant_dynamic-slice_fusion), channel_id=1, source_target_pairs={{0,2},{1,3},{2,0},{3,1},{4,6},{5,7},{6,4},{7,5},{8,10},{9,11},{10,... | collective-permute-start | bytes 1327112 | tf_op jit(solution)/shard_map/ppermute | solution.py:144
  21.6 13.3 %collective-permute-start.3 = (bf16[3,256,128]{2,1,0:T(8,128)(2,1)S(1)}, bf16[3,256,128]{2,1,0:T(8,128)(2,1)S(1)}, u32[]{:S(2)}, u32[]{:S(2)}) collective-permute-start(bf16[3,256,128]{2,1,0:T(8,128)(2,1)S(1)} %pad_maximum_fusion.2), channel_id=1, source_target_pairs={{0,2},{1,3},{2,0},{3,1},{4,6},{5,7},{6,4},{7,5},{8,10},{9,11},{10,... | collective-permute-start | bytes 589832 | tf_op jit(solution)/shard_map/ppermute | solution.py:144
  23.1 13.4 %collective-permute-start.6 = (bf16[3,264,128]{2,1,0:T(8,128)(2,1)S(1)}, bf16[3,264,128]{2,1,0:T(8,128)(2,1)S(1)}, u32[]{:S(2)}, u32[]{:S(2)}) collective-permute-start(bf16[3,264,128]{2,1,0:T(8,128)(2,1)S(1)} %pad_maximum_fusion.1), channel_id=1, source_target_pairs={{0,4},{1,5},{2,6},{3,7},{4,0},{5,1},{6,2},{7,3},{8,12},{9,13},{10,... | collective-permute-start | bytes 608264 | tf_op jit(solution)/shard_map/ppermute | solution.py:144
  26.4 12.7 %collective-permute-start.10 = (bf16[256,128]{1,0:T(8,128)(2,1)S(1)}, bf16[256,128]{1,0:T(8,128)(2,1)S(1)}, u32[]{:S(2)}, u32[]{:S(2)}) collective-permute-start(bf16[256,128]{1,0:T(8,128)(2,1)S(1)} %get-tuple-element.187), channel_id=1, source_target_pairs={{0,1},{1,0},{2,3},{3,2},{4,5},{5,4},{6,7},{7,6},{8,9},{9,8},{10,11... | collective-permute-start | bytes 196616 | tf_op jit(solution)/shard_map/ppermute | solution.py:144
  34.9 11.0 %collective-permute-start.8 = (bf16[7,256,128]{2,1,0:T(8,128)(2,1)S(1)}, bf16[7,256,128]{2,1,0:T(8,128)(2,1)S(1)}, u32[]{:S(2)}, u32[]{:S(2)}) collective-permute-start(bf16[7,256,128]{2,1,0:T(8,128)(2,1)S(1)} %constant_dynamic-update-slice_fusion.4.refs_4_), channel_id=1, source_target_pairs={{0,4},{1,5},{2,6},{3,7},{4,0},{5,1},{6,2},{7,3},{8,12},{9,13},{10,... | collective-permute-start | bytes 1376264 | tf_op jit(solution)/shard_map/ppermute | solution.py:144
  36.5 13.4 %collective-permute-start.13 = (bf16[7,256,128]{2,1,0:T(8,128)(2,1)S(1)}, bf16[7,256,128]{2,1,0:T(8,128)(2,1)S(1)}, u32[]{:S(2)}, u32[]{:S(2)}) collective-permute-start(bf16[7,256,128]{2,1,0:T(8,128)(2,1)S(1)} %constant_dynamic-update-slice_fusion.4.refs_4_), channel_id=1, source_target_pairs={{0,1},{1,0},{2,3},{3,2},{4,5},{5,4},{6,7},{7,6},{8,9},{9,8},{10,11... | collective-permute-start | bytes 1376264 | tf_op jit(solution)/shard_map/ppermute | solution.py:144
  36.6 13.3 %collective-permute-start.7 = (bf16[7,264,128]{2,1,0:T(8,128)(2,1)S(1)}, bf16[7,264,128]{2,1,0:T(8,128)(2,1)S(1)}, u32[]{:S(2)}, u32[]{:S(2)}) collective-permute-start(bf16[7,264,128]{2,1,0:T(8,128)(2,1)S(1)} %constant_dynamic-update-slice_fusion.refs_3_), channel_id=1, source_target_pairs={{0,2},{1,3},{2,0},{3,1},{4,6},{5,7},{6,4},{7,5},{8,10},{9,11},{10,... | collective-permute-start | bytes 1419272 | tf_op jit(solution)/shard_map/ppermute | solution.py:144
  40.4 10.0 %collective-permute-start.12 = (bf16[7,264,128]{2,1,0:T(8,128)(2,1)S(1)}, bf16[7,264,128]{2,1,0:T(8,128)(2,1)S(1)}, u32[]{:S(2)}, u32[]{:S(2)}) collective-permute-start(bf16[7,264,128]{2,1,0:T(8,128)(2,1)S(1)} %constant_dynamic-update-slice_fusion.refs_3_), channel_id=1, source_target_pairs={{0,1},{1,0},{2,3},{3,2},{4,5},{5,4},{6,7},{7,6},{8,9},{9,8},{10,11... | collective-permute-start | bytes 1419272 | tf_op jit(solution)/shard_map/ppermute | solution.py:144
  40.6 17.7 %collective-permute-start.18 = (bf16[3,384,384]{2,1,0:T(8,128)(2,1)S(1)}, bf16[3,384,384]{2,1,0:T(8,128)(2,1)S(1)}, u32[]{:S(2)}, u32[]{:S(2)}) collective-permute-start(bf16[3,384,384]{2,1,0:T(8,128)(2,1)S(1)} %convert_element_type.47.mine_ref), channel_id=1, source_target_pairs={{0,1},{1,0},{2,3},{3,2},{4,5},{5,4},{6,7},{7,6},{8,9},{9,8},{10,11... | collective-permute-start | bytes 2654216 | tf_op jit(solution)/shard_map/ppermute | solution.py:144
  45.9 9.8 %collective-permute-start.17 = (bf16[3,192,384]{2,1,0:T(8,128)(2,1)S(1)}, bf16[3,192,384]{2,1,0:T(8,128)(2,1)S(1)}, u32[]{:S(2)}, u32[]{:S(2)}) collective-permute-start(bf16[3,192,384]{2,1,0:T(8,128)(2,1)S(1)} %collective-permute-done.16.near_ref), channel_id=1, source_target_pairs={{0,8},{1,9},{2,10},{3,11},{4,12},{5,13},{6,14},{7,15},{8,0},{9,1},... | collective-permute-start | bytes 1327112 | tf_op jit(solution)/shard_map/ppermute | solution.py:144
  88.3 13.9 %collective-permute-start.28 = (bf16[16,120,384]{2,1,0:T(8,128)(2,1)S(1)}, bf16[16,120,384]{2,1,0:T(8,128)(2,1)S(1)}, u32[]{:S(2)}, u32[]{:S(2)}) collective-permute-start(bf16[16,120,384]{2,1,0:T(8,128)(2,1)S(1)} %get-tuple-element.126), channel_id=1, source_target_pairs={{0,1},{1,0},{2,3},{3,2},{4,5},{5,4},{6,7},{7,6},{8,9},{9,8},{10,11... | collective-permute-start | bytes 4423688 | tf_op jit(solution)/shard_map/ppermute | solution.py:144
  103.1 11.5 %collective-permute-start.29 = (bf16[4,120,384]{2,1,0:T(8,128)(2,1)S(1)}, bf16[4,120,384]{2,1,0:T(8,128)(2,1)S(1)}, u32[]{:S(2)}, u32[]{:S(2)}) collective-permute-start(bf16[4,120,384]{2,1,0:T(8,128)(2,1)S(1)} %get-tuple-element.128), channel_id=1, source_target_pairs={{0,4},{1,5},{2,6},{3,7},{4,0},{5,1},{6,2},{7,3},{8,12},{9,13},{10,... | collective-permute-start | bytes 1105928 | tf_op jit(solution)/shard_map/ppermute | solution.py:144
  104.7 19.4 %collective-permute-start.30 = (bf16[4,120,384]{2,1,0:T(8,128)(2,1)S(1)}, bf16[4,120,384]{2,1,0:T(8,128)(2,1)S(1)}, u32[]{:S(2)}, u32[]{:S(2)}) collective-permute-start(bf16[4,120,384]{2,1,0:T(8,128)(2,1)S(1)} %get-tuple-element.129), channel_id=1, source_target_pairs={{0,2},{1,3},{2,0},{3,1},{4,6},{5,7},{6,4},{7,5},{8,10},{9,11},{10,... | collective-permute-start | bytes 1105928 | tf_op jit(solution)/shard_map/ppermute | solution.py:144
  106.2 17.8 %collective-permute-start.31 = (bf16[4,120,384]{2,1,0:T(8,128)(2,1)S(1)}, bf16[4,120,384]{2,1,0:T(8,128)(2,1)S(1)}, u32[]{:S(2)}, u32[]{:S(2)}) collective-permute-start(bf16[4,120,384]{2,1,0:T(8,128)(2,1)S(1)} %get-tuple-element.130), channel_id=1, source_target_pairs={{0,6},{1,7},{2,4},{3,5},{4,2},{5,3},{6,0},{7,1},{8,14},{9,15},{10,... | collective-permute-start | bytes 1105928 | tf_op jit(solution)/shard_map/ppermute | solution.py:144
  107.3 18.4 %collective-permute-start.22 = (bf16[4,48,384]{2,1,0:T(8,128)(2,1)S(1)}, bf16[4,48,384]{2,1,0:T(8,128)(2,1)S(1)}, u32[]{:S(2)}, u32[]{:S(2)}) collective-permute-start(bf16[4,48,384]{2,1,0:T(8,128)(2,1)S(1)} %get-tuple-element.118), channel_id=1, source_target_pairs={{0,4},{1,5},{2,6},{3,7},{4,0},{5,1},{6,2},{7,3},{8,12},{9,13},{10,... | collective-permute-start | bytes 442376 | tf_op jit(solution)/shard_map/ppermute | solution.py:144
  108.9 20.7 %collective-permute-start.23 = (bf16[4,48,384]{2,1,0:T(8,128)(2,1)S(1)}, bf16[4,48,384]{2,1,0:T(8,128)(2,1)S(1)}, u32[]{:S(2)}, u32[]{:S(2)}) collective-permute-start(bf16[4,48,384]{2,1,0:T(8,128)(2,1)S(1)} %get-tuple-element.119), channel_id=1, source_target_pairs={{0,2},{1,3},{2,0},{3,1},{4,6},{5,7},{6,4},{7,5},{8,10},{9,11},{10,... | collective-permute-start | bytes 442376 | tf_op jit(solution)/shard_map/ppermute | solution.py:144
  114.6 15.0 %collective-permute-start.24 = (bf16[4,48,384]{2,1,0:T(8,128)(2,1)S(1)}, bf16[4,48,384]{2,1,0:T(8,128)(2,1)S(1)}, u32[]{:S(2)}, u32[]{:S(2)}) collective-permute-start(bf16[4,48,384]{2,1,0:T(8,128)(2,1)S(1)} %get-tuple-element.120), channel_id=1, source_target_pairs={{0,6},{1,7},{2,4},{3,5},{4,2},{5,3},{6,0},{7,1},{8,14},{9,15},{10,... | collective-permute-start | bytes 442376 | tf_op jit(solution)/shard_map/ppermute | solution.py:144
  124.8 15.3 %collective-permute-start.32 = (bf16[120,384]{1,0:T(8,128)(2,1)S(1)}, bf16[120,384]{1,0:T(8,128)(2,1)S(1)}, u32[]{:S(2)}, u32[]{:S(2)}) collective-permute-start(bf16[120,384]{1,0:T(8,128)(2,1)S(1)} %get-tuple-element.132), channel_id=1, source_target_pairs={{0,8},{1,9},{2,10},{3,11},{4,12},{5,13},{6,14},{7,15},{8,16},{9,17... | collective-permute-start | bytes 276488 | tf_op jit(solution)/shard_map/ppermute | solution.py:144
  125.1 15.0 %collective-permute-start.33 = (bf16[120,384]{1,0:T(8,128)(2,1)S(1)}, bf16[120,384]{1,0:T(8,128)(2,1)S(1)}, u32[]{:S(2)}, u32[]{:S(2)}) collective-permute-start(bf16[120,384]{1,0:T(8,128)(2,1)S(1)} %get-tuple-element.133), channel_id=1, source_target_pairs={{0,16},{1,17},{2,18},{3,19},{4,20},{5,21},{6,22},{7,23},{8,24},{9,... | collective-permute-start | bytes 276488 | tf_op jit(solution)/shard_map/ppermute | solution.py:144
  125.7 14.4 %collective-permute-start.34 = (bf16[120,384]{1,0:T(8,128)(2,1)S(1)}, bf16[120,384]{1,0:T(8,128)(2,1)S(1)}, u32[]{:S(2)}, u32[]{:S(2)}) collective-permute-start(bf16[120,384]{1,0:T(8,128)(2,1)S(1)} %get-tuple-element.134), channel_id=1, source_target_pairs={{0,24},{1,25},{2,26},{3,27},{4,28},{5,29},{6,30},{7,31},{8,0},{9,1... | collective-permute-start | bytes 276488 | tf_op jit(solution)/shard_map/ppermute | solution.py:144
  146.3 10.7 %collective-permute-start.41 = (bf16[2,3,24,384]{3,2,1,0:T(8,128)(2,1)S(1)}, bf16[2,3,24,384]{3,2,1,0:T(8,128)(2,1)S(1)}, u32[]{:S(2)}, u32[]{:S(2)}) collective-permute-start(bf16[2,3,24,384]{3,2,1,0:T(8,128)(2,1)S(1)} %join.1.refs_0_), channel_id=1, source_target_pairs={{0,8},{1,9},{2,10},{3,11},{4,12},{5,13},{6,14},{7,15},{8,16},{9,17... | collective-permute-start | bytes 331784 | tf_op jit(solution)/shard_map/ppermute | solution.py:144
  157.0 13.0 %collective-permute-start.44 = (bf16[4,64,384]{2,1,0:T(8,128)(2,1)S(1)}, bf16[4,64,384]{2,1,0:T(8,128)(2,1)S(1)}, u32[]{:S(2)}, u32[]{:S(2)}) collective-permute-start(bf16[4,64,384]{2,1,0:T(8,128)(2,1)S(1)} %pad_maximum_fusion.3.refs_0_), channel_id=1, source_target_pairs={{0,4},{1,5},{2,6},{3,7},{4,0},{5,1},{6,2},{7,3},{8,12},{9,13},{10,... | collective-permute-start | bytes 589832 | tf_op jit(solution)/shard_map/ppermute | solution.py:144
  158.1 11.9 %collective-permute-start.45 = (bf16[4,64,384]{2,1,0:T(8,128)(2,1)S(1)}, bf16[4,64,384]{2,1,0:T(8,128)(2,1)S(1)}, u32[]{:S(2)}, u32[]{:S(2)}) collective-permute-start(bf16[4,64,384]{2,1,0:T(8,128)(2,1)S(1)} %pad_maximum_fusion.3.refs_0_), channel_id=1, source_target_pairs={{0,2},{1,3},{2,0},{3,1},{4,6},{5,7},{6,4},{7,5},{8,10},{9,11},{10,... | collective-permute-start | bytes 589832 | tf_op jit(solution)/shard_map/ppermute | solution.py:144
  158.9 11.1 %collective-permute-start.46 = (bf16[4,64,384]{2,1,0:T(8,128)(2,1)S(1)}, bf16[4,64,384]{2,1,0:T(8,128)(2,1)S(1)}, u32[]{:S(2)}, u32[]{:S(2)}) collective-permute-start(bf16[4,64,384]{2,1,0:T(8,128)(2,1)S(1)} %pad_maximum_fusion.3.refs_0_), channel_id=1, source_target_pairs={{0,6},{1,7},{2,4},{3,5},{4,2},{5,3},{6,0},{7,1},{8,14},{9,15},{10,... | collective-permute-start | bytes 589832 | tf_op jit(solution)/shard_map/ppermute | solution.py:144
  160.6 9.4 %collective-permute-start.47 = (bf16[2,3,24,384]{3,2,1,0:T(8,128)(2,1)S(1)}, bf16[2,3,24,384]{3,2,1,0:T(8,128)(2,1)S(1)}, u32[]{:S(2)}, u32[]{:S(2)}) collective-permute-start(bf16[2,3,24,384]{3,2,1,0:T(8,128)(2,1)S(1)} %join.1.refs_0_), channel_id=1, source_target_pairs={{0,4},{1,5},{2,6},{3,7},{4,0},{5,1},{6,2},{7,3},{8,12},{9,13},{10,... | collective-permute-start | bytes 331784 | tf_op jit(solution)/shard_map/ppermute | solution.py:144
  161.5 9.5 %collective-permute-start.42 = (bf16[2,3,24,384]{3,2,1,0:T(8,128)(2,1)S(1)}, bf16[2,3,24,384]{3,2,1,0:T(8,128)(2,1)S(1)}, u32[]{:S(2)}, u32[]{:S(2)}) collective-permute-start(bf16[2,3,24,384]{3,2,1,0:T(8,128)(2,1)S(1)} %join.1.refs_0_), channel_id=1, source_target_pairs={{0,16},{1,17},{2,18},{3,19},{4,20},{5,21},{6,22},{7,23},{8,24},{9,... | collective-permute-start | bytes 331784 | tf_op jit(solution)/shard_map/ppermute | solution.py:144
  (37 other events, 429.2 us)

commit v2 on v1

--- a/solution.py
+++ b/solution.py
@@ -137,7 +137,7 @@
 TO_C = permutation(lambda z, x, y, c: (z, x, y, 1 - c))
 TO_Y = permutation(lambda z, x, y, c: (z, x, 1 - y, c))
 TO_X = permutation(lambda z, x, y, c: (z, 1 - x, y, c))
-TO_Z = [permutation(lambda z, x, y, c, d=d: ((z + d) % 4, x, y, c)) for d in range(4)]
+TO_Z = [permutation(lambda z, x, y, c, d=d: (z ^ d, x, y, c)) for d in range(4)]
 
 
 def send(value, pairs):
@@ -153,10 +153,6 @@
 TO_XY = permutation(lambda z, x, y, c: (z, 1 - x, 1 - y, c))
 TO_CY = permutation(lambda z, x, y, c: (z, x, 1 - y, 1 - c))
 TO_PAIR = permutation(lambda z, x, y, c: (z + 1 - 2 * (z % 2), x, y, c))
-
-
-def send_plane(value):
-    return [send(value, TO_X), send(value, TO_Y), send(value, TO_XY)]
 
 
 def gather_flat(piece, cut, ready):
@@ -189,7 +185,7 @@
             z, x, y, c = at
             dz, other = (0, 1) if i == 0 else ((i - 1) % 3 + 1, (i - 1) // 3)
             dx, dy = {0: (other, 0), 1: (0, other), 2: (other, 1), 3: (1, other)}[kind]
-            return place_of(lax.rem(z + 4 - dz, 4), flip(x, dx), flip(y, dy), flip(c, dc))
+            return place_of(z ^ dz, flip(x, dx), flip(y, dy), flip(c, dc))
 
         return entry
 
@@ -198,17 +194,6 @@
         places += [(0, near(dc, 0, 0)), (cut, near(dc, 1, 0)), (0, near(dc, 0, 1))]
         places += [((0, cut, 0, cut)[kind], far(dc, kind)) for kind in range(4)]
     return places
-
-
-def gather_rows(away, keep, column, finish):
-    turned = [send(v, TO_Z[d + 1]) for d, v in enumerate(away)]
-    column = column()
-    turned, column[1] = lax.optimization_barrier((turned, column[1]))
-    plane = jnp.stack([keep] + turned)
-    plane = [plane] + send_plane(plane)
-    column = finish(column)
-    plane, column[4] = lax.optimization_barrier((plane, column[4]))
-    return plane + [send(p, TO_C) for p in plane], column
 
 
 def read_coordinates(ref):
@@ -351,7 +336,7 @@
 def turn_kernel(at_ref, *refs):
     z, _, _, _ = read_coordinates(at_ref)
     for d, out_ref in enumerate(refs[4:]):
-        unit = lax.rem(z + d, 4)
+        unit = z ^ d
         out_ref[...] = sum(ref[unit].astype(F32) for ref in refs[:4]).astype(BF)
 
 
@@ -380,12 +365,25 @@
     return [own] + [send(v, TO_Z[d + 1]) for d, v in enumerate(away)]
 
 
+def rows_kernel(at_ref, pay_ref, *refs):
+    early, out_refs, total_ref = refs[:4], refs[4:8], refs[8]
+    total = sum(ref[...].astype(F32) for ref in early).astype(BF)
+    total_ref[...] = total
+    for d, out_ref in enumerate(out_refs):
+        plane = at_ref[0] ^ d
+        out_ref[...] = pay_ref[plane]
+
+        @pl.when(plane == 3)
+        def _():
+            out_ref[16:40, :] = total[4 * UNIT :]
+
+
 def owner_kernel(at_ref, own_ref, *refs):
-    late, early = refs[:4], refs[4:8]
-    out_refs, total = refs[8:12], refs[12]
+    late, early = refs[:4], refs[4]
+    out_refs, total = refs[5:9], refs[9]
     _, _, y, c = read_coordinates(at_ref)
     one = sum(ref[...].astype(F32) for ref in late)
-    two = sum(ref[0 : 4 * UNIT, :].astype(F32) for ref in early)
+    two = early[...].astype(F32)
     for k in range(6):
         total[k] = (one[UNIT * k : UNIT * k + UNIT] if k < 2 else two[UNIT * (k - 2) : UNIT * (k - 1)])
     for out_ref, (dy, dc) in zip(out_refs, ((0, 0), (0, 1), (1, 0), (1, 1))):
@@ -403,19 +401,32 @@
     out_ref[1] = near_ref[...] + far_ref[...]
 
 
-def turn_owned(at, late, early, owner_map):
+def exchange_gradients(at, owner_map, pay, late, early):
     piece = (3, UNIT, D)
+    keep, *away, early = pl.pallas_call(
+        rows_kernel,
+        name="pay_rows",
+        out_shape=(shape((PAY, D), BF),) * 4 + (shape((EARLY, D), BF),),
+        in_specs=[SM] + [VM] * 5,
+        out_specs=[VM] * 5,
+        compiler_params=room(8),
+        cost_estimate=cost(1e6, 1e6),
+    )(at, pay, *early)
+    turned = [send(v, TO_Z[d + 1]) for d, v in enumerate(away)]
     own, to_c, to_y, to_cy = pl.pallas_call(
         owner_kernel,
         name="owner_rows",
         out_shape=(shape(piece, BF),) * 4,
-        in_specs=[SM, SM] + [VM] * 8,
+        in_specs=[SM, SM] + [VM] * 5,
         out_specs=[VM] * 4,
         scratch_shapes=[pltpu.VMEM((6, UNIT, D), F32)],
         compiler_params=room(8),
         cost_estimate=cost(1e6, 1e6),
-    )(at, owner_map, *late, *early)
+    )(at, owner_map, *late, early)
     far, near, pair = send(to_cy, TO_CY), send(to_y, TO_Y), send(to_c, TO_C)
+    turned, pair = lax.optimization_barrier((turned, pair))
+    rows = jnp.stack([keep] + turned)
+    plane = [rows, send(rows, TO_X), send(rows, TO_Y)]
     both = pl.pallas_call(
         join_kernel,
         name="join",
@@ -425,11 +436,12 @@
         compiler_params=room(8),
         cost_estimate=cost(1e6, 1e6),
     )(own, pair, near, far)
-    return [both] + [send(both, TO_Z[d]) for d in (1, 2, 3)]
-
-
-def cross_owned(column):
-    return column + [send(v, TO_X) for v in column]
+    column = [both] + [send(both, TO_Z[d]) for d in (1, 2, 3)]
+    crossed = [send(both, TO_X)]
+    plane[1], column[1] = lax.optimization_barrier((plane[1], column[1]))
+    plane.append(send(plane[1], TO_Y))
+    slots = column + crossed + [send(v, TO_X) for v in column[1:]]
+    return slots, plane + [send(p, TO_C) for p in plane]
 
 
 def plane_gradient(plane, pay_ref, flat, rolled, align):
@@ -540,7 +552,7 @@
     for k, ref in enumerate(parts):
         dc, dy, dx = k // 4, k // 2 % 2, k % 2
         for dz in range(4):
-            there = (lax.rem(z + 4 - dz, 4), flip(x, dx), flip(y, dy), flip(c, dc))
+            there = (z ^ dz, flip(x, dx), flip(y, dy), flip(c, dc))
             value = ref[dz].astype(F32)
             pay[place_of(*there)] = value
             start = pl.multiple_of(unit_of(*there[:3]) * UNIT, 8)
@@ -626,7 +638,7 @@
         for dx in range(2):
             for dz in range(4):
                 for dy in range(2):
-                    unit = unit_of(lax.rem(z + 4 - dz, 4), flip(x, dx), flip(y, dy))
+                    unit = unit_of(z ^ dz, flip(x, dx), flip(y, dy))
                     rows = pl.ds(pl.multiple_of(unit * UNIT, 8), UNIT)
                     grad[rows, :] = parts[4 * dx + dz][dy, t].astype(F32)
         g = grad[...].astype(BF)
@@ -745,21 +757,53 @@
             up_s[:, D * j : D * j + D] = w_ref[4 + j]
 
     h1 = h1_ref[0]
+    h1_low = h1.astype(BF)
+    h1_s[rows, :] = h1_low
+    aligned = mm(h1_low, aw_ref[...])
     n2, inv2 = norm_stats(h1)
     act2 = (n2 * (1.0 + mod(4)) + mod(3)).astype(BF)
     act2_s[rows, :] = act2
-    branch = jnp.zeros((SEQ, D), F32) + bias_ref[8:9, :]
-    for j in range(2):
-        lanes = slice(2 * D * j, 2 * D * j + 2 * D)
-        bias = jnp.concatenate([bias_ref[4 + 2 * j : 5 + 2 * j, :], bias_ref[5 + 2 * j : 6 + 2 * j, :]], axis=1)
-        x = mm(act2, up_s[:, lanes]) + bias
+
+    def lanes_of(j):
+        return slice(2 * D * j, 2 * D * j + 2 * D)
+
+    def pair_row(j):
+        return jnp.concatenate([bias_ref[j : j + 1, :], bias_ref[j + 1 : j + 2, :]], axis=1)
+
+    def expand(j):
+        return mm(act2, up_s[:, lanes_of(j)])
+
+    def activate(j, x):
+        x = x + pair_row(4 + 2 * j)
         xx = x * x
         t = jnp.tanh(x * (GELU_C + (GELU_C * GELU_D) * xx))
         half = 0.5 + 0.5 * t
+        slope_s[:, lanes_of(j)] = half + (0.5 * x) * (1.0 - t * t) * (GELU_C + (3.0 * GELU_C * GELU_D) * xx)
         g = (x * half).astype(BF)
-        slope_s[:, lanes] = half + (0.5 * x) * (1.0 - t * t) * (GELU_C + (3.0 * GELU_C * GELU_D) * xx)
-        gelu_s[rows, lanes] = g
-        branch = branch + mm(g, w_ref[8 + 2 * j : 10 + 2 * j].reshape(2 * D, D))
+        gelu_s[rows, lanes_of(j)] = g
+        return g
+
+    def contract(j, g):
+        return mm(g, w_ref[8 + 2 * j : 10 + 2 * j].reshape(2 * D, D))
+
+    x_one = expand(0)
+    aligned = aligned + pair_row(9)
+    dino = dino_ref[0].astype(F32)
+    dot = jnp.sum(aligned * dino, axis=-1, keepdims=True)
+    ra = lax.rsqrt(jnp.sum(aligned * aligned, axis=-1, keepdims=True) + NORM_EPS)
+    rd = lax.rsqrt(jnp.sum(dino * dino, axis=-1, keepdims=True) + NORM_EPS)
+    x_two = expand(1)
+    g_one = activate(0, x_one)
+    scale = REPA_WEIGHT / (total_img * SEQ)
+    both = ra * rd
+    cosine = dot * both
+    ba = (dino * (both * -scale) + aligned * (cosine * (ra * ra) * scale)).astype(BF)
+    ba_s[rows, :] = ba
+    branch = contract(0, g_one)
+    g_two = activate(1, x_two)
+    through = mm_nt(ba, aw_ref[...])
+    branch = branch + contract(1, g_two) + bias_ref[8:9, :]
+    ba_sum = column_sum(ba.astype(F32))
     h2 = h1 + mod(5) * branch
     n3, inv3 = norm_stats(h2)
     act3 = (n3 * (1.0 + mod(7)) + mod(6)).astype(BF)
@@ -768,24 +812,10 @@
     err = out[:, :PD] - vel_ref[0].T
     weight = tw_ref[i]
     loss = jnp.sum(column_sum(err * err), axis=1, keepdims=True) * (weight / (total_img * SEQ * PD))
+    loss = loss - column_sum(cosine) * scale
     bo = jnp.concatenate([err * (2.0 * weight / (total_img * SEQ * PD)), jnp.zeros((SEQ, 128 - PD), F32)],
                          axis=1).astype(BF)
     bo_s[rows, :] = bo
-
-    h1_low = h1.astype(BF)
-    h1_s[rows, :] = h1_low
-    aligned = mm(h1_low, aw_ref[...]) + jnp.concatenate([bias_ref[9:10, :], bias_ref[10:11, :]], axis=1)
-    dino = dino_ref[0].astype(F32)
-    dot = jnp.sum(aligned * dino, axis=-1, keepdims=True)
-    ra = lax.rsqrt(jnp.sum(aligned * aligned, axis=-1, keepdims=True) + NORM_EPS)
-    rd = lax.rsqrt(jnp.sum(dino * dino, axis=-1, keepdims=True) + NORM_EPS)
-    scale = REPA_WEIGHT / (total_img * SEQ)
-    both = ra * rd
-    cosine = dot * both
-    loss = loss - column_sum(cosine) * scale
-    ba = (dino * (both * -scale) + aligned * (cosine * (ra * ra) * scale)).astype(BF)
-    ba_s[rows, :] = ba
-    through = mm_nt(ba, aw_ref[...])
 
     b3 = mm_nt(bo, fw_ref[...])
     bh2 = norm_back(b3 * (1.0 + mod(7)), n3, inv3)
@@ -801,7 +831,6 @@
         sums_ref[17 + 2 * j : 18 + 2 * j, :] += bi_sum[:, D:]
         b2 = b2 + mm_nt(bi, up_s[:, lanes])
     sums_ref[20:21, :] += column_sum(bb2.astype(F32))
-    ba_sum = column_sum(ba.astype(F32))
     sums_ref[21:22, :] += ba_sum[:, :D]
     sums_ref[22:23, :] += ba_sum[:, D:]
     sums_ref[23:24, 0:128] += column_sum(bo.astype(F32))
@@ -907,10 +936,9 @@
         att[first : first + bb1.shape[0], :], bb1[...])))
 
 
-def cond_back_kernel(images, aligns, at_ref, cls_ref, gm2_ref, pre_ref, th_ref, cond_ref, feat_ref, modw_ref, fmodw_ref,
+def cond_back_kernel(images, cls_ref, gm2_ref, pre_ref, th_ref, cond_ref, feat_ref, modw_ref, fmodw_ref,
                      tout_ref, sums_ref, *refs):
-    align_refs, refs = refs[:aligns], refs[aligns:]
-    out_refs, pay_ref, refs = refs[-5:-1], refs[-1], refs[:-5]
+    out_ref, pay_ref, refs = refs[-2], refs[-1], refs[:-2]
     gm3_refs, patch_refs = refs[::2], refs[1::2]
     none = jnp.zeros((4, D), F32)
     gm2 = [gm2_ref[m] for m in range(images)]
@@ -972,13 +1000,11 @@
     put_rows(2, 40, jnp.concatenate([over(4), over(5), over(6), sums[16:21]], axis=0))
     put(3, 0, act, act)
     put(3, 1, finals[0], finals[1])
-    put_rows(3, 16, sum(ref[4 * UNIT :, :].astype(F32) for ref in align_refs))
     put_rows(3, 40, sums[0:16])
     last = [[over(3)] + [row] * 6, [row] * 7, [row] * 7, [sums[23:24], sums[21:22], sums[22:23]] + [row] * 4]
     for plane in range(4):
         put_rows(plane, 56, jnp.concatenate(last[plane] + [loss], axis=0))
-    for d, out_ref in enumerate(out_refs):
-        out_ref[...] = pay_ref[lax.rem(at_ref[0] + d, 4)].astype(BF)
+    out_ref[...] = pay_ref[...].astype(BF)
 
 
 def rows_each(first, *dims):
@@ -1051,17 +1077,17 @@
     )(at, flat(att), *arrays)
 
 
-def cond_back(images, at, class_ids, gm2, pre, th, cond, features, mod_w, fmod_w, tout_w, sums, aligns, gm3):
+def cond_back(images, class_ids, gm2, pre, th, cond, features, mod_w, fmod_w, tout_w, sums, gm3):
     return pl.pallas_call(
-        functools.partial(cond_back_kernel, images, len(aligns)),
+        functools.partial(cond_back_kernel, images),
         name="cond_back",
-        out_shape=(shape((PAY, D), BF),) * 4,
-        in_specs=[SM, SM] + [VM] * (9 + len(aligns) + len(gm3)),
-        out_specs=[VM] * 4,
+        out_shape=shape((4, PAY, D), BF),
+        in_specs=[SM] + [VM] * (9 + len(gm3)),
+        out_specs=VM,
         scratch_shapes=[pltpu.VMEM((4, PAY, D), F32)],
         compiler_params=room(16),
         cost_estimate=cost(1e8, 4e6),
-    )(at, class_ids, gm2, pre, th, cond, features, mod_w, fmod_w, tout_w, sums, *aligns, *gm3)
+    )(class_ids, gm2, pre, th, cond, features, mod_w, fmod_w, tout_w, sums, *gm3)
 
 
 def position_table():
@@ -1141,15 +1167,13 @@
         parts.append((act, bp, bb1))
         gm3 += [gm, patch]
     late_mine, late_other = last_gradients(at, att, parts)
-    aligns = early if near else [jnp.zeros((EARLY, D), BF)]
-    keep, *away = cond_back(
-        images, at, class_ids, gm2, pre, th, cond, features, mod_w, fmod_w, tout_w, sums, aligns, gm3)
+    pay = cond_back(images, class_ids, gm2, pre, th, cond, features, mod_w, fmod_w, tout_w, sums, gm3)
     if near:
         late = reduce_units(at, late_mine, late_other)
-        parts, grads = gather_rows(
-            away, keep, lambda: turn_owned(at, late, early, owner_map), cross_owned)
+        grads, parts = exchange_gradients(at, owner_map, pay, late, early)
         loss, upd, new_m, new_v = adam_near(at, parts, flat_w, flat_m, flat_v)
         *grads, loss, upd, new_m, new_v = lax.optimization_barrier((*grads, loss, upd, new_m, new_v))
+        updates = shampoo(at, grads, blocks_w, stat_left, stat_right, root_left, root_right)
     else:
         core = at[3]
 
@@ -1161,16 +1185,14 @@
         early, late = by_part(mine, other), by_part(late_mine, late_other)
         late = jnp.stack([late[0, 0], late[0, 1], late[1, 0], late[1, 1]])
         grad_model = jnp.concatenate([late, early[:, :4].reshape(8, D, D)])
-        planes = jnp.take(jnp.stack([keep, *away]), (jnp.arange(4) - at[0]) % 4, axis=0)
-        pays = lax.all_gather(planes, AXES, axis=0, tiled=False)
+        pays = lax.all_gather(pay, AXES, axis=0, tiled=False)
         align_sum = lax.psum(early[:, 4].astype(F32), AXES)
         loss, upd, new_m, new_v = adam_wide(pays, align_sum, flat_w, flat_m, flat_v)
         slots = jnp.take(grad_model, owner_map, axis=0)
         owned = lax.psum_scatter(slots, "shard", scatter_dimension=0, tiled=True)
         grads = [lax.psum(owned.astype(F32), "dp").astype(BF)]
-    block_update, new_left, new_right = shampoo(
-        at, grads, blocks_w, stat_left, stat_right, root_left, root_right)
-    return (loss, block_update, new_left, new_right,
+        updates = shampoo(at, grads, blocks_w, stat_left, stat_right, root_left, root_right)
+    return (loss, *updates,
             upd.reshape(-1), new_m.reshape(-1), new_v.reshape(-1))
 
 

time: 192 us -> 191 us (level)
  starting transfers between devices: 49.1 us -> 54.3 us
  waiting for transfers between devices: 69.6 us -> 64.4 us
    ppermute x55, starting transfers between devices: 49.1 us -> 54.3 us  [send(): return lax.ppermute(value, AXES, pairs)]
    ppermute x55, waiting for transfers between devices: 69.6 us -> 64.4 us  [send(): return lax.ppermute(value, AXES, pairs)]
  transfers between devices with their start and end apart: 55 -> 55, of which waited for: 23 -> 21; matrix products, arithmetic and copies ran while one was open for 5% -> 5% of each run, Pallas kernels for 12% -> 13%
where the time goes in v2:
time: 191 us
  waiting for transfers between devices  64.4 us (34%)
  Pallas kernels  59.3 us (31%)
  starting transfers between devices  54.3 us (28%)
  local copies, waits for them, and re-layouts  7.23 us (4%)
  other arithmetic  4.13 us (2%)
    ppermute x55, waiting for transfers between devices, send(): return lax.ppermute(value, AXES, pairs)  64.4 us
    ppermute x55, starting transfers between devices, send(): return lax.ppermute(value, AXES, pairs)  54.3 us
    pallas_call x1, Pallas kernels, middle(): pl.pallas_call(functools.partial(middle_kernel, images, total_img), name=...  18.6 us
    pallas_call x2, Pallas kernels, attention_back(): pl.pallas_call(functools.partial(back_kernel, first), name='attention_bac...  10.9 us
    pallas_call x1, Pallas kernels, front(): pl.pallas_call(front_kernel, name='front', grid=(images,), out_shape=(sha...  8.89 us
    pallas_call x1, Pallas kernels, shampoo(): pl.pallas_call(functools.partial(shampoo_kernel, near), name='shampoo', g...  6.39 us
  transfers between devices with their start and end apart: 55, of which 21 were waited for; matrix products, arithmetic and copies ran while one was open for 5% of the time, Pallas kernels for 13%

profile of v2, /device:TPU:0, one launch (start us, length us, event | category | flops | bytes accessed | tf_op | source)
XLA Modules:
  0.0 190.6 jit_solution(13995716720816228393)
XLA Ops:
  0.6 1.9 convert_bitcast_fusion
  2.5 5.1 %collective-permute-start.2 = (bf16[520,128]{1,0:T(8,128)(2,1)}, bf16[520,128]{1,0:T(8,128)(2,1)S(1)}, u32[]{:S(2)}, u32[]{:S(2)}) collective-permute-start(bf16[520,128]{1,0:T(8,128)(2,1)} %get-tuple-element.180), channel_id=1, source_target_pairs={{0,24},{1,25},{2,26},{3,27},{4,28},{5,29},{6,30},{7,31},{8,16},{9,... | collective-permute-start | bytes 399368 | tf_op jit(solution)/shard_map/ppermute | solution.py:144
  8.1 1.7 collective-permute-start.5
  13.8 5.2 %collective-permute-done.1 = bf16[520,128]{1,0:T(8,128)(2,1)S(1)} collective-permute-done((bf16[520,128]{1,0:T(8,128)(2,1)}, bf16[520,128]{1,0:T(8,128)(2,1)S(1)}, u32[]{:S(2)}, u32[]{:S(2)}) %collective-permute-start.1) | collective-permute-done | bytes 133152 | tf_op jit(solution)/shard_map/ppermute | solution.py:144
  29.0 5.5 %collective-permute-done.3 = bf16[3,256,128]{2,1,0:T(8,128)(2,1)S(1)} collective-permute-done((bf16[3,256,128]{2,1,0:T(8,128)(2,1)S(1)}, bf16[3,256,128]{2,1,0:T(8,128)(2,1)S(1)}, u32[]{:S(2)}, u32[]{:S(2)}) %collective-permute-start.3) | collective-permute-done | bytes 196640 | tf_op jit(solution)/shard_map/ppermute | solution.py:144
  36.2 1.6 collective-permute-start.7
  40.6 4.8 %collective-permute-done.8.refs_6_ = bf16[7,256,128]{2,1,0:T(8,128)(2,1)S(1)} collective-permute-done((bf16[7,256,128]{2,1,0:T(8,128)(2,1)S(1)}, bf16[7,256,128]{2,1,0:T(8,128)(2,1)S(1)}, u32[]{:S(2)}, u32[]{:S(2)}) %collective-permute-start.8) | collective-permute-done | bytes 458784 | tf_op jit(solution)/shard_map/ppermute | solution.py:144
  45.7 3.8 %collective-permute-done.7.refs_5_ = bf16[7,264,128]{2,1,0:T(8,128)(2,1)S(1)} collective-permute-done((bf16[7,264,128]{2,1,0:T(8,128)(2,1)S(1)}, bf16[7,264,128]{2,1,0:T(8,128)(2,1)S(1)}, u32[]{:S(2)}, u32[]{:S(2)}) %collective-permute-start.7) | collective-permute-done | bytes 473120 | tf_op jit(solution)/shard_map/ppermute | solution.py:144
  50.1 4.7 %collective-permute-done.17.far_ref = bf16[3,192,384]{2,1,0:T(8,128)(2,1)S(1)} collective-permute-done((bf16[3,192,384]{2,1,0:T(8,128)(2,1)S(1)}, bf16[3,192,384]{2,1,0:T(8,128)(2,1)S(1)}, u32[]{:S(2)}, u32[]{:S(2)}) %collective-permute-start.17) | collective-permute-done | bytes 442400 | tf_op jit(solution)/shard_map/ppermute | solution.py:144
  54.9 2.6 %conditioning.1 = (f32[8,3072]{1,0:T(8,128)S(1)}, f32[8,384]{1,0:T(8,128)S(1)}, f32[8,384]{1,0:T(8,128)S(1)}, f32[8,384]{1,0:T(8,128)S(1)}, bf16[384,2304]{1,0:T...) custom-call(s32[4]{0:T(128)S(1)} %pad_add_fusion.at_ref, ...), custom_call_target="tpu_custom_call" | custom-call | flops 1000000000 | bytes 10000000 | tf_op jit(solution)/shard_map/conditioning/pallas_call | solution.py:276
  58.4 8.9 %front.1 = (f32[4,256,384]{2,1,0:T(8,128)S(1)}, bf16[4,256,1152]{2,1,0:T(8,128)(2,1)S(1)}, bf16[4,256,384]{2,1,0:T(8,128)(2,1)S(1)}, f32[4,256,384]{2,1,0:T(8,128)S(1)}) custom-call(f32[4,16,256]{2,1,0:T(8,128)S(1)} %bitcast.76, f32[8,3072]{1,0:T(8,128)S(1)} %get-tuple-element.96.mods_ref, f32[16,384]{1,0:T(8,128)S(1)} %get-tuple-element.97.bias_ref, ...), custom_call_target="tpu_custom_call" | custom-call | flops 2200000000 | bytes 12000000 | tf_op jit(solution)/shard_map/front/pallas_call | solution.py:1017
  67.4 18.6 %middle.1 = (f32[4,256,384]{2,1,0:T(8,128)S(1)}, f32[4,8,384]{2,1,0:T(8,128)S(1)}, bf16[16,120,384]{2,1,0:T(8,128)(2,1)S(1)}, bf16[16,120,384]{2,1,0:T(8,128)(2,1)S(1)}, f32[24,384]{1,0:T(8,128)S(1)}) custom-call(s32[4]{0:T(128)S(1)} %pad_add_fusion.at_ref, f32[4]{0:T(128)S(1)} %copy-done.13, f32[4,256,384]{2,1,0:T(8,128)S(1)} %get-tuple-element.101.h1_ref, ...), custom_call_target="tpu_custom_call" | custom-call | flops 8999999488 | bytes 14000000 | tf_op jit(solution)/shard_map/middle/pallas_call | solution.py:1034
  86.6 2.7 %attention_back.2 = (bf16[1,256,384]{2,1,0:T(8,128)(2,1)S(1)}, bf16[1,256,1152]{2,1,0:T(8,128)(2,1)S(1)}, bf16[1,256,384]{2,1,0:T(8,128)(2,1)S(1)}, f32[1,8,384]{2,1,0:T(8,128)S(1)}, f32[1,16,384]{2,1,0:T(8,128)S(1)}) custom-call(f32[4,256,384]{2,1,0:T(8,128)S(1)} %get-tuple-element.104.bh1_ref, f32[4,256,384]{2,1,0:T(8,128)S(1)} %get-tuple-element.105.h0_ref, ...), custom_call_target="tpu_custom_call" | custom-call | flops 1200000000 | bytes 3000000 | tf_op jit(solution)/shard_map/attention_back/pallas_call | solution.py:1052
  89.3 8.2 %attention_back.3 = (bf16[3,256,384]{2,1,0:T(8,128)(2,1)S(1)}, bf16[3,256,1152]{2,1,0:T(8,128)(2,1)S(1)}, bf16[3,256,384]{2,1,0:T(8,128)(2,1)S(1)}, f32[3,8,384]{2,1,0:T(8,128)S(1)}, f32[3,16,384]{2,1,0:T(8,128)S(1)}) custom-call(f32[4,256,384]{2,1,0:T(8,128)S(1)} %get-tuple-element.104.bh1_ref, f32[4,256,384]{2,1,0:T(8,128)S(1)} %get-tuple-element.105.h0_ref, ...), custom_call_target="tpu_custom_call" | custom-call | flops 3600000000 | bytes 9000000 | tf_op jit(solution)/shard_map/attention_back/pallas_call | solution.py:1052
  97.5 2.4 %last_gradients.1 = (bf16[16,48,384]{2,1,0:T(8,128)(2,1)S(1)}, bf16[16,48,384]{2,1,0:T(8,128)(2,1)S(1)}) custom-call(s32[4]{0:T(128)S(1)} %pad_add_fusion.at_ref, bf16[1024,384]{1,0:T(8,128)(2,1)S(1)} %bitcast.66, bf16[256,384]{1,0:T(8,128)(2,1)S(1)} %bitcast.73, bf16[256,1152]{1,0:T(8,128)(2,1)S(1)} %bitcast.68, bf16[256,384]{1,0:T(8,128)(2,1)S(1)} %bitcast.72, ...), custom_call_target="tpu_custom_call" | custom-call | flops 1200000000 | bytes 9000000 | tf_op jit(solution)/shard_map/last_gradients/pallas_call | solution.py:1069
  108.2 4.2 %collective-permute-done.29.refs_1_ = bf16[4,120,384]{2,1,0:T(8,128)(2,1)S(1)} collective-permute-done((bf16[4,120,384]{2,1,0:T(8,128)(2,1)S(1)}, bf16[4,120,384]{2,1,0:T(8,128)(2,1)S(1)}, u32[]{:S(2)}, u32[]{:S(2)}) %collective-permute-start.29) | collective-permute-done | bytes 368672 | tf_op jit(solution)/shard_map/ppermute | solution.py:144
  112.4 2.4 %collective-permute-start.24 = (bf16[4,48,384]{2,1,0:T(8,128)(2,1)S(1)}, bf16[4,48,384]{2,1,0:T(8,128)(2,1)S(1)}, u32[]{:S(2)}, u32[]{:S(2)}) collective-permute-start(bf16[4,48,384]{2,1,0:T(8,128)(2,1)S(1)} %get-tuple-element.118), channel_id=1, source_target_pairs={{0,6},{1,7},{2,4},{3,5},{4,2},{5,3},{6,0},{7,1},{8,14},{9,15},{10,... | collective-permute-start | bytes 442376 | tf_op jit(solution)/shard_map/ppermute | solution.py:144
  114.8 7.0 %collective-permute-done.30.refs_2_ = bf16[4,120,384]{2,1,0:T(8,128)(2,1)S(1)} collective-permute-done((bf16[4,120,384]{2,1,0:T(8,128)(2,1)S(1)}, bf16[4,120,384]{2,1,0:T(8,128)(2,1)S(1)}, u32[]{:S(2)}, u32[]{:S(2)}) %collective-permute-start.30) | collective-permute-done | bytes 368672 | tf_op jit(solution)/shard_map/ppermute | solution.py:144
  123.3 3.5 %collective-permute-start.33 = (bf16[120,384]{1,0:T(8,128)(2,1)S(1)}, bf16[120,384]{1,0:T(8,128)(2,1)S(1)}, u32[]{:S(2)}, u32[]{:S(2)}) collective-permute-start(bf16[120,384]{1,0:T(8,128)(2,1)S(1)} %get-tuple-element.143), channel_id=1, source_target_pairs={{0,16},{1,17},{2,18},{3,19},{4,20},{5,21},{6,22},{7,23},{8,24},{9,... | collective-permute-start | bytes 276488 | tf_op jit(solution)/shard_map/ppermute | solution.py:144
  129.3 3.0 %collective-permute-start.26 = (bf16[48,384]{1,0:T(8,128)(2,1)S(1)}, bf16[48,384]{1,0:T(8,128)(2,1)S(1)}, u32[]{:S(2)}, u32[]{:S(2)}) collective-permute-start(bf16[48,384]{1,0:T(8,128)(2,1)S(1)} %get-tuple-element.121), channel_id=1, source_target_pairs={{0,16},{1,17},{2,18},{3,19},{4,20},{5,21},{6,22},{7,23},{8,24},{9,... | collective-permute-start | bytes 110600 | tf_op jit(solution)/shard_map/ppermute | solution.py:144
  133.5 1.7 cond_back.1.pay_ref
  135.8 1.7 collective-permute-done.26.refs_2_
  139.7 2.1 %collective-permute-start.36 = (bf16[64,384]{1,0:T(8,128)(2,1)S(1)}, bf16[64,384]{1,0:T(8,128)(2,1)S(1)}, u32[]{:S(2)}, u32[]{:S(2)}) collective-permute-start(bf16[64,384]{1,0:T(8,128)(2,1)S(1)} %get-tuple-element.148), channel_id=1, source_target_pairs={{0,16},{1,17},{2,18},{3,19},{4,20},{5,21},{6,22},{7,23},{8,24},{9,... | collective-permute-start | bytes 147464 | tf_op jit(solution)/shard_map/ppermute | solution.py:144
  143.3 2.7 %collective-permute-done.36 = bf16[64,384]{1,0:T(8,128)(2,1)S(1)} collective-permute-done((bf16[64,384]{1,0:T(8,128)(2,1)S(1)}, bf16[64,384]{1,0:T(8,128)(2,1)S(1)}, u32[]{:S(2)}, u32[]{:S(2)}) %collective-permute-start.36) | collective-permute-done | bytes 49184 | tf_op jit(solution)/shard_map/ppermute | solution.py:144
  146.0 1.7 collective-permute-done.37
  149.8 3.7 %collective-permute-done.39.near_ref = bf16[3,24,384]{2,1,0:T(8,128)(2,1)S(1)} collective-permute-done((bf16[3,24,384]{2,1,0:T(8,128)(2,1)S(1)}, bf16[3,24,384]{2,1,0:T(8,128)(2,1)S(1)}, u32[]{:S(2)}, u32[]{:S(2)}) %collective-permute-start.39) | collective-permute-done | bytes 55328 | tf_op jit(solution)/shard_map/ppermute | solution.py:144
  155.9 3.4 %collective-permute-done.42.refs_1_ = bf16[2,3,24,384]{3,2,1,0:T(8,128)(2,1)S(1)} collective-permute-done((bf16[2,3,24,384]{3,2,1,0:T(8,128)(2,1)S(1)}, bf16[2,3,24,384]{3,2,1,0:T(8,128)(2,1)S(1)}, u32[]{:S(2)}, u32[]{:S(2)}) %collective-permute-start.42) | collective-permute-done | bytes 110624 | tf_op jit(solution)/shard_map/ppermute | solution.py:144
  161.9 3.7 %collective-permute-done.50.refs_3_ = bf16[4,64,384]{2,1,0:T(8,128)(2,1)S(1)} collective-permute-done((bf16[4,64,384]{2,1,0:T(8,128)(2,1)S(1)}, bf16[4,64,384]{2,1,0:T(8,128)(2,1)S(1)}, u32[]{:S(2)}, u32[]{:S(2)}) %collective-permute-start.50) | collective-permute-done | bytes 196640 | tf_op jit(solution)/shard_map/ppermute | solution.py:144
  165.6 1.8 collective-permute-done.43.refs_2_
  169.0 5.1 %collective-permute-done.44.refs_3_ = bf16[2,3,24,384]{3,2,1,0:T(8,128)(2,1)S(1)} collective-permute-done((bf16[2,3,24,384]{3,2,1,0:T(8,128)(2,1)S(1)}, bf16[2,3,24,384]{3,2,1,0:T(8,128)(2,1)S(1)}, u32[]{:S(2)}, u32[]{:S(2)}) %collective-permute-start.44) | collective-permute-done | bytes 110624 | tf_op jit(solution)/shard_map/ppermute | solution.py:144
  178.2 2.8 %adam.1 = (f32[1,1]{1,0:T(1,128)}, f32[520,128]{1,0:T(8,128)}, f32[520,128]{1,0:T(8,128)}, f32[520,128]{1,0:T(8,128)}) custom-call(s32[4]{0:T(128)S(1)} %pad_add_fusion.at_ref, bf16[4,64,384]{2,1,0:T(8,128)(2,1)S(1)} %pad_maximum_fusion.3.refs_0_, bf16[4,64,384]{2,1,0:T(8,128)(2,1)S(1)} %collective-permute-done.41.refs_1_, ...), custom_call_target="tpu_custom_call" | custom-call | flops 1000000000 | bytes 10000000 | tf_op jit(solution)/shard_map/adam/pallas_call | solution.py:593
  184.2 6.4 %shampoo.1 = (f32[3,384,384]{2,1,0:T(8,128)}, f32[3,384,384]{2,1,0:T(8,128)}, f32[3,384,384]{2,1,0:T(8,128)}) custom-call(s32[4]{0:T(128)S(1)} %pad_add_fusion.at_ref, bf16[2,3,24,384]{3,2,1,0:T(8,128)(2,1)S(1)} %join.1.refs_0_, bf16[2,3,24,384]{3,2,1,0:T(8,128)(2,1)S(1)} %collective-permute-done.42.refs_1_, ...), custom_call_target="tpu_custom_call" | custom-call | flops 3000000000 | bytes 15000000 | tf_op jit(solution)/shard_map/shampoo/pallas_call | solution.py:663
  (156 shorter events, 55.0 us)
Async XLA Ops:
  2.5 11.2 %collective-permute-start.2 = (bf16[520,128]{1,0:T(8,128)(2,1)}, bf16[520,128]{1,0:T(8,128)(2,1)S(1)}, u32[]{:S(2)}, u32[]{:S(2)}) collective-permute-start(bf16[520,128]{1,0:T(8,128)(2,1)} %get-tuple-element.180), channel_id=1, source_target_pairs={{0,24},{1,25},{2,26},{3,27},{4,28},{5,29},{6,30},{7,31},{8,16},{9,... | collective-permute-start | bytes 399368 | tf_op jit(solution)/shard_map/ppermute | solution.py:144
  7.6 11.5 %collective-permute-start.1 = (bf16[520,128]{1,0:T(8,128)(2,1)}, bf16[520,128]{1,0:T(8,128)(2,1)S(1)}, u32[]{:S(2)}, u32[]{:S(2)}) collective-permute-start(bf16[520,128]{1,0:T(8,128)(2,1)} %get-tuple-element.180), channel_id=1, source_target_pairs={{0,16},{1,17},{2,18},{3,19},{4,20},{5,21},{6,22},{7,23},{8,24},{9,... | collective-permute-start | bytes 399368 | tf_op jit(solution)/shard_map/ppermute | solution.py:144
  7.6 13.0 %collective-permute-start = (bf16[520,128]{1,0:T(8,128)(2,1)}, bf16[520,128]{1,0:T(8,128)(2,1)}, u32[]{:S(2)}, u32[]{:S(2)}) collective-permute-start(bf16[520,128]{1,0:T(8,128)(2,1)} %get-tuple-element.180), channel_id=1, source_target_pairs={{0,8},{1,9},{2,10},{3,11},{4,12},{5,13},{6,14},{7,15},{8,0},{9,1},... | collective-permute-start | bytes 399368 | tf_op jit(solution)/shard_map/ppermute | solution.py:144
  8.1 18.1 %collective-permute-start.5 = (bf16[520,128]{1,0:T(8,128)(2,1)}, bf16[520,128]{1,0:T(8,128)(2,1)}, u32[]{:S(2)}, u32[]{:S(2)}) collective-permute-start(bf16[520,128]{1,0:T(8,128)(2,1)} %get-tuple-element.180), channel_id=1, source_target_pairs={{0,2},{1,3},{2,0},{3,1},{4,6},{5,7},{6,4},{7,5},{8,10},{9,11},{10,... | collective-permute-start | bytes 399368 | tf_op jit(solution)/shard_map/ppermute | solution.py:144
  9.9 13.1 %collective-permute-start.4 = (bf16[520,128]{1,0:T(8,128)(2,1)}, bf16[520,128]{1,0:T(8,128)(2,1)}, u32[]{:S(2)}, u32[]{:S(2)}) collective-permute-start(bf16[520,128]{1,0:T(8,128)(2,1)} %get-tuple-element.180), channel_id=1, source_target_pairs={{0,4},{1,5},{2,6},{3,7},{4,0},{5,1},{6,2},{7,3},{8,12},{9,13},{10,... | collective-permute-start | bytes 399368 | tf_op jit(solution)/shard_map/ppermute | solution.py:144
  13.7 22.5 %collective-permute-start.9 = (bf16[520,128]{1,0:T(8,128)(2,1)}, bf16[520,128]{1,0:T(8,128)(2,1)S(1)}, u32[]{:S(2)}, u32[]{:S(2)}) collective-permute-start(bf16[520,128]{1,0:T(8,128)(2,1)} %get-tuple-element.180), channel_id=1, source_target_pairs={{0,1},{1,0},{2,3},{3,2},{4,5},{5,4},{6,7},{7,6},{8,9},{9,8},{10,11... | collective-permute-start | bytes 399368 | tf_op jit(solution)/shard_map/ppermute | solution.py:144
  19.0 21.2 %collective-permute-start.16 = (bf16[3,192,384]{2,1,0:T(8,128)(2,1)S(1)}, bf16[3,192,384]{2,1,0:T(8,128)(2,1)S(1)}, u32[]{:S(2)}, u32[]{:S(2)}) collective-permute-start(bf16[3,192,384]{2,1,0:T(8,128)(2,1)S(1)} %constant_dynamic-slice_fusion), channel_id=1, source_target_pairs={{0,2},{1,3},{2,0},{3,1},{4,6},{5,7},{6,4},{7,5},{8,10},{9,11},{10,... | collective-permute-start | bytes 1327112 | tf_op jit(solution)/shard_map/ppermute | solution.py:144
  21.4 13.0 %collective-permute-start.3 = (bf16[3,256,128]{2,1,0:T(8,128)(2,1)S(1)}, bf16[3,256,128]{2,1,0:T(8,128)(2,1)S(1)}, u32[]{:S(2)}, u32[]{:S(2)}) collective-permute-start(bf16[3,256,128]{2,1,0:T(8,128)(2,1)S(1)} %pad_maximum_fusion.2), channel_id=1, source_target_pairs={{0,2},{1,3},{2,0},{3,1},{4,6},{5,7},{6,4},{7,5},{8,10},{9,11},{10,... | collective-permute-start | bytes 589832 | tf_op jit(solution)/shard_map/ppermute | solution.py:144
  22.9 13.1 %collective-permute-start.6 = (bf16[3,264,128]{2,1,0:T(8,128)(2,1)S(1)}, bf16[3,264,128]{2,1,0:T(8,128)(2,1)S(1)}, u32[]{:S(2)}, u32[]{:S(2)}) collective-permute-start(bf16[3,264,128]{2,1,0:T(8,128)(2,1)S(1)} %pad_maximum_fusion.1), channel_id=1, source_target_pairs={{0,4},{1,5},{2,6},{3,7},{4,0},{5,1},{6,2},{7,3},{8,12},{9,13},{10,... | collective-permute-start | bytes 608264 | tf_op jit(solution)/shard_map/ppermute | solution.py:144
  26.3 12.5 %collective-permute-start.10 = (bf16[256,128]{1,0:T(8,128)(2,1)S(1)}, bf16[256,128]{1,0:T(8,128)(2,1)S(1)}, u32[]{:S(2)}, u32[]{:S(2)}) collective-permute-start(bf16[256,128]{1,0:T(8,128)(2,1)S(1)} %get-tuple-element.183), channel_id=1, source_target_pairs={{0,1},{1,0},{2,3},{3,2},{4,5},{5,4},{6,7},{7,6},{8,9},{9,8},{10,11... | collective-permute-start | bytes 196616 | tf_op jit(solution)/shard_map/ppermute | solution.py:144
  34.5 10.8 %collective-permute-start.8 = (bf16[7,256,128]{2,1,0:T(8,128)(2,1)S(1)}, bf16[7,256,128]{2,1,0:T(8,128)(2,1)S(1)}, u32[]{:S(2)}, u32[]{:S(2)}) collective-permute-start(bf16[7,256,128]{2,1,0:T(8,128)(2,1)S(1)} %constant_dynamic-update-slice_fusion.4.refs_4_), channel_id=1, source_target_pairs={{0,4},{1,5},{2,6},{3,7},{4,0},{5,1},{6,2},{7,3},{8,12},{9,13},{10,... | collective-permute-start | bytes 1376264 | tf_op jit(solution)/shard_map/ppermute | solution.py:144
  36.1 13.4 %collective-permute-start.13 = (bf16[7,256,128]{2,1,0:T(8,128)(2,1)S(1)}, bf16[7,256,128]{2,1,0:T(8,128)(2,1)S(1)}, u32[]{:S(2)}, u32[]{:S(2)}) collective-permute-start(bf16[7,256,128]{2,1,0:T(8,128)(2,1)S(1)} %constant_dynamic-update-slice_fusion.4.refs_4_), channel_id=1, source_target_pairs={{0,1},{1,0},{2,3},{3,2},{4,5},{5,4},{6,7},{7,6},{8,9},{9,8},{10,11... | collective-permute-start | bytes 1376264 | tf_op jit(solution)/shard_map/ppermute | solution.py:144
  36.2 13.3 %collective-permute-start.7 = (bf16[7,264,128]{2,1,0:T(8,128)(2,1)S(1)}, bf16[7,264,128]{2,1,0:T(8,128)(2,1)S(1)}, u32[]{:S(2)}, u32[]{:S(2)}) collective-permute-start(bf16[7,264,128]{2,1,0:T(8,128)(2,1)S(1)} %constant_dynamic-update-slice_fusion.refs_3_), channel_id=1, source_target_pairs={{0,2},{1,3},{2,0},{3,1},{4,6},{5,7},{6,4},{7,5},{8,10},{9,11},{10,... | collective-permute-start | bytes 1419272 | tf_op jit(solution)/shard_map/ppermute | solution.py:144
  40.0 10.0 %collective-permute-start.12 = (bf16[7,264,128]{2,1,0:T(8,128)(2,1)S(1)}, bf16[7,264,128]{2,1,0:T(8,128)(2,1)S(1)}, u32[]{:S(2)}, u32[]{:S(2)}) collective-permute-start(bf16[7,264,128]{2,1,0:T(8,128)(2,1)S(1)} %constant_dynamic-update-slice_fusion.refs_3_), channel_id=1, source_target_pairs={{0,1},{1,0},{2,3},{3,2},{4,5},{5,4},{6,7},{7,6},{8,9},{9,8},{10,11... | collective-permute-start | bytes 1419272 | tf_op jit(solution)/shard_map/ppermute | solution.py:144
  40.3 17.2 %collective-permute-start.18 = (bf16[3,384,384]{2,1,0:T(8,128)(2,1)S(1)}, bf16[3,384,384]{2,1,0:T(8,128)(2,1)S(1)}, u32[]{:S(2)}, u32[]{:S(2)}) collective-permute-start(bf16[3,384,384]{2,1,0:T(8,128)(2,1)S(1)} %convert_element_type.47.mine_ref), channel_id=1, source_target_pairs={{0,1},{1,0},{2,3},{3,2},{4,5},{5,4},{6,7},{7,6},{8,9},{9,8},{10,11... | collective-permute-start | bytes 2654216 | tf_op jit(solution)/shard_map/ppermute | solution.py:144
  45.3 9.5 %collective-permute-start.17 = (bf16[3,192,384]{2,1,0:T(8,128)(2,1)S(1)}, bf16[3,192,384]{2,1,0:T(8,128)(2,1)S(1)}, u32[]{:S(2)}, u32[]{:S(2)}) collective-permute-start(bf16[3,192,384]{2,1,0:T(8,128)(2,1)S(1)} %collective-permute-done.16.near_ref), channel_id=1, source_target_pairs={{0,8},{1,9},{2,10},{3,11},{4,12},{5,13},{6,14},{7,15},{8,0},{9,1},... | collective-permute-start | bytes 1327112 | tf_op jit(solution)/shard_map/ppermute | solution.py:144
  86.0 13.9 %collective-permute-start.28 = (bf16[16,120,384]{2,1,0:T(8,128)(2,1)S(1)}, bf16[16,120,384]{2,1,0:T(8,128)(2,1)S(1)}, u32[]{:S(2)}, u32[]{:S(2)}) collective-permute-start(bf16[16,120,384]{2,1,0:T(8,128)(2,1)S(1)} %get-tuple-element.136), channel_id=1, source_target_pairs={{0,1},{1,0},{2,3},{3,2},{4,5},{5,4},{6,7},{7,6},{8,9},{9,8},{10,11... | collective-permute-start | bytes 4423688 | tf_op jit(solution)/shard_map/ppermute | solution.py:144
  100.8 11.5 %collective-permute-start.29 = (bf16[4,120,384]{2,1,0:T(8,128)(2,1)S(1)}, bf16[4,120,384]{2,1,0:T(8,128)(2,1)S(1)}, u32[]{:S(2)}, u32[]{:S(2)}) collective-permute-start(bf16[4,120,384]{2,1,0:T(8,128)(2,1)S(1)} %get-tuple-element.138), channel_id=1, source_target_pairs={{0,4},{1,5},{2,6},{3,7},{4,0},{5,1},{6,2},{7,3},{8,12},{9,13},{10,... | collective-permute-start | bytes 1105928 | tf_op jit(solution)/shard_map/ppermute | solution.py:144
  102.4 19.4 %collective-permute-start.30 = (bf16[4,120,384]{2,1,0:T(8,128)(2,1)S(1)}, bf16[4,120,384]{2,1,0:T(8,128)(2,1)S(1)}, u32[]{:S(2)}, u32[]{:S(2)}) collective-permute-start(bf16[4,120,384]{2,1,0:T(8,128)(2,1)S(1)} %get-tuple-element.139), channel_id=1, source_target_pairs={{0,2},{1,3},{2,0},{3,1},{4,6},{5,7},{6,4},{7,5},{8,10},{9,11},{10,... | collective-permute-start | bytes 1105928 | tf_op jit(solution)/shard_map/ppermute | solution.py:144
  103.9 17.8 %collective-permute-start.31 = (bf16[4,120,384]{2,1,0:T(8,128)(2,1)S(1)}, bf16[4,120,384]{2,1,0:T(8,128)(2,1)S(1)}, u32[]{:S(2)}, u32[]{:S(2)}) collective-permute-start(bf16[4,120,384]{2,1,0:T(8,128)(2,1)S(1)} %get-tuple-element.140), channel_id=1, source_target_pairs={{0,6},{1,7},{2,4},{3,5},{4,2},{5,3},{6,0},{7,1},{8,14},{9,15},{10,... | collective-permute-start | bytes 1105928 | tf_op jit(solution)/shard_map/ppermute | solution.py:144
  105.1 21.7 %collective-permute-start.22 = (bf16[4,48,384]{2,1,0:T(8,128)(2,1)S(1)}, bf16[4,48,384]{2,1,0:T(8,128)(2,1)S(1)}, u32[]{:S(2)}, u32[]{:S(2)}) collective-permute-start(bf16[4,48,384]{2,1,0:T(8,128)(2,1)S(1)} %get-tuple-element.116), channel_id=1, source_target_pairs={{0,4},{1,5},{2,6},{3,7},{4,0},{5,1},{6,2},{7,3},{8,12},{9,13},{10,... | collective-permute-start | bytes 442376 | tf_op jit(solution)/shard_map/ppermute | solution.py:144
  106.7 21.3 %collective-permute-start.23 = (bf16[4,48,384]{2,1,0:T(8,128)(2,1)S(1)}, bf16[4,48,384]{2,1,0:T(8,128)(2,1)S(1)}, u32[]{:S(2)}, u32[]{:S(2)}) collective-permute-start(bf16[4,48,384]{2,1,0:T(8,128)(2,1)S(1)} %get-tuple-element.117), channel_id=1, source_target_pairs={{0,2},{1,3},{2,0},{3,1},{4,6},{5,7},{6,4},{7,5},{8,10},{9,11},{10,... | collective-permute-start | bytes 442376 | tf_op jit(solution)/shard_map/ppermute | solution.py:144
  112.4 15.6 %collective-permute-start.24 = (bf16[4,48,384]{2,1,0:T(8,128)(2,1)S(1)}, bf16[4,48,384]{2,1,0:T(8,128)(2,1)S(1)}, u32[]{:S(2)}, u32[]{:S(2)}) collective-permute-start(bf16[4,48,384]{2,1,0:T(8,128)(2,1)S(1)} %get-tuple-element.118), channel_id=1, source_target_pairs={{0,6},{1,7},{2,4},{3,5},{4,2},{5,3},{6,0},{7,1},{8,14},{9,15},{10,... | collective-permute-start | bytes 442376 | tf_op jit(solution)/shard_map/ppermute | solution.py:144
  122.5 9.7 %collective-permute-start.32 = (bf16[120,384]{1,0:T(8,128)(2,1)S(1)}, bf16[120,384]{1,0:T(8,128)(2,1)S(1)}, u32[]{:S(2)}, u32[]{:S(2)}) collective-permute-start(bf16[120,384]{1,0:T(8,128)(2,1)S(1)} %get-tuple-element.142), channel_id=1, source_target_pairs={{0,8},{1,9},{2,10},{3,11},{4,12},{5,13},{6,14},{7,15},{8,0},{9,1},... | collective-permute-start | bytes 276488 | tf_op jit(solution)/shard_map/ppermute | solution.py:144
  123.3 11.9 %collective-permute-start.33 = (bf16[120,384]{1,0:T(8,128)(2,1)S(1)}, bf16[120,384]{1,0:T(8,128)(2,1)S(1)}, u32[]{:S(2)}, u32[]{:S(2)}) collective-permute-start(bf16[120,384]{1,0:T(8,128)(2,1)S(1)} %get-tuple-element.143), channel_id=1, source_target_pairs={{0,16},{1,17},{2,18},{3,19},{4,20},{5,21},{6,22},{7,23},{8,24},{9,... | collective-permute-start | bytes 276488 | tf_op jit(solution)/shard_map/ppermute | solution.py:144
  126.8 8.4 %collective-permute-start.34 = (bf16[120,384]{1,0:T(8,128)(2,1)S(1)}, bf16[120,384]{1,0:T(8,128)(2,1)S(1)}, u32[]{:S(2)}, u32[]{:S(2)}) collective-permute-start(bf16[120,384]{1,0:T(8,128)(2,1)S(1)} %get-tuple-element.144), channel_id=1, source_target_pairs={{0,24},{1,25},{2,26},{3,27},{4,28},{5,29},{6,30},{7,31},{8,16},{9,... | collective-permute-start | bytes 276488 | tf_op jit(solution)/shard_map/ppermute | solution.py:144
  138.8 9.0 %collective-permute-start.38 = (bf16[3,24,384]{2,1,0:T(8,128)(2,1)S(1)}, bf16[3,24,384]{2,1,0:T(8,128)(2,1)S(1)}, u32[]{:S(2)}, u32[]{:S(2)}) collective-permute-start(bf16[3,24,384]{2,1,0:T(8,128)(2,1)S(1)} %get-tuple-element.150), channel_id=1, source_target_pairs={{0,1},{1,0},{2,3},{3,2},{4,5},{5,4},{6,7},{7,6},{8,9},{9,8},{10,11... | collective-permute-start | bytes 165896 | tf_op jit(solution)/shard_map/ppermute | solution.py:144
  147.8 11.5 %collective-permute-start.41 = (bf16[4,64,384]{2,1,0:T(8,128)(2,1)S(1)}, bf16[4,64,384]{2,1,0:T(8,128)(2,1)S(1)}, u32[]{:S(2)}, u32[]{:S(2)}) collective-permute-start(bf16[4,64,384]{2,1,0:T(8,128)(2,1)S(1)} %pad_maximum_fusion.3.refs_0_), channel_id=1, source_target_pairs={{0,4},{1,5},{2,6},{3,7},{4,0},{5,1},{6,2},{7,3},{8,12},{9,13},{10,... | collective-permute-start | bytes 589832 | tf_op jit(solution)/shard_map/ppermute | solution.py:144
  161.4 13.8 %collective-permute-start.51 = (bf16[4,64,384]{2,1,0:T(8,128)(2,1)S(1)}, bf16[4,64,384]{2,1,0:T(8,128)(2,1)S(1)}, u32[]{:S(2)}, u32[]{:S(2)}) collective-permute-start(bf16[4,64,384]{2,1,0:T(8,128)(2,1)S(1)} %pad_maximum_fusion.3.refs_0_), channel_id=1, source_target_pairs={{0,1},{1,0},{2,3},{3,2},{4,5},{5,4},{6,7},{7,6},{8,9},{9,8},{10,11... | collective-permute-start | bytes 589832 | tf_op jit(solution)/shard_map/ppermute | solution.py:144
  161.4 14.7 %collective-permute-start.52 = (bf16[4,64,384]{2,1,0:T(8,128)(2,1)S(1)}, bf16[4,64,384]{2,1,0:T(8,128)(2,1)S(1)}, u32[]{:S(2)}, u32[]{:S(2)}) collective-permute-start(bf16[4,64,384]{2,1,0:T(8,128)(2,1)S(1)} %collective-permute-done.41.refs_1_), channel_id=1, source_target_pairs={{0,1},{1,0},{2,3},{3,2},{4,5},{5,4},{6,7},{7,6},{8,9},{9,8},{10,11... | collective-permute-start | bytes 589832 | tf_op jit(solution)/shard_map/ppermute | solution.py:144
  161.9 15.3 %collective-permute-start.53 = (bf16[4,64,384]{2,1,0:T(8,128)(2,1)S(1)}, bf16[4,64,384]{2,1,0:T(8,128)(2,1)S(1)}, u32[]{:S(2)}, u32[]{:S(2)}) collective-permute-start(bf16[4,64,384]{2,1,0:T(8,128)(2,1)S(1)} %collective-permute-done.49.refs_2_), channel_id=1, source_target_pairs={{0,1},{1,0},{2,3},{3,2},{4,5},{5,4},{6,7},{7,6},{8,9},{9,8},{10,11... | collective-permute-start | bytes 589832 | tf_op jit(solution)/shard_map/ppermute | solution.py:144
  165.6 12.5 %collective-permute-start.54 = (bf16[4,64,384]{2,1,0:T(8,128)(2,1)S(1)}, bf16[4,64,384]{2,1,0:T(8,128)(2,1)S(1)}, u32[]{:S(2)}, u32[]{:S(2)}) collective-permute-start(bf16[4,64,384]{2,1,0:T(8,128)(2,1)S(1)} %collective-permute-done.50.refs_3_), channel_id=1, source_target_pairs={{0,1},{1,0},{2,3},{3,2},{4,5},{5,4},{6,7},{7,6},{8,9},{9,8},{10,11... | collective-permute-start | bytes 589832 | tf_op jit(solution)/shard_map/ppermute | solution.py:144
  (37 other events, 458.0 us)

commit v3 on v2

--- a/solution.py
+++ b/solution.py
@@ -440,7 +440,9 @@
     crossed = [send(both, TO_X)]
     plane[1], column[1] = lax.optimization_barrier((plane[1], column[1]))
     plane.append(send(plane[1], TO_Y))
-    slots = column + crossed + [send(v, TO_X) for v in column[1:]]
+    crossed.append(send(column[1], TO_X))
+    crossed[1], column[2], column[3] = lax.optimization_barrier((crossed[1], column[2], column[3]))
+    slots = column + crossed + [send(v, TO_X) for v in column[2:]]
     return slots, plane + [send(p, TO_C) for p in plane]
 
 
@@ -648,9 +650,8 @@
     nl_ref[0] = STAT_BETA * sl_ref[t] + (1.0 - STAT_BETA) * mm_nt(g, g)
     nr_ref[0] = STAT_BETA * sr_ref[t] + (1.0 - STAT_BETA) * mm_tn(g, g)
     left = mm(jnp.concatenate(split2(rl_ref[t]), axis=1), jnp.concatenate([g, g], axis=0))
-    l_one, l_two = split2(left)
-    r_one, r_two = split2(rr_ref[t])
-    p = mm(jnp.concatenate([l_one, l_two, l_one], axis=1), jnp.concatenate([r_one, r_one, r_two], axis=0))
+    left = left.astype(BF)
+    p = mm(jnp.concatenate([left, left], axis=1), jnp.concatenate(split2(rr_ref[t]), axis=0))
     mean = jnp.sum(jnp.sum(p * p, axis=1, keepdims=True), axis=0, keepdims=True) * (1.0 / (D * D))
     root = jnp.sqrt(mean)
     upd_ref[0] = -SHAMPOO_RATE * (p / (root + RMS_EPS) + DECAY_RATE * w_ref[t])
@@ -797,13 +798,14 @@
     scale = REPA_WEIGHT / (total_img * SEQ)
     both = ra * rd
     cosine = dot * both
-    ba = (dino * (both * -scale) + aligned * (cosine * (ra * ra) * scale)).astype(BF)
+    ba = dino * (both * -scale) + aligned * (cosine * (ra * ra) * scale)
+    ba_sum = column_sum(ba)
+    ba = ba.astype(BF)
     ba_s[rows, :] = ba
     branch = contract(0, g_one)
     g_two = activate(1, x_two)
     through = mm_nt(ba, aw_ref[...])
     branch = branch + contract(1, g_two) + bias_ref[8:9, :]
-    ba_sum = column_sum(ba.astype(F32))
     h2 = h1 + mod(5) * branch
     n3, inv3 = norm_stats(h2)
     act3 = (n3 * (1.0 + mod(7)) + mod(6)).astype(BF)
@@ -824,9 +826,10 @@
     b2 = jnp.zeros((SEQ, D), F32)
     for j in range(2):
         lanes = slice(2 * D * j, 2 * D * j + 2 * D)
-        bi = (mm_nt(bb2, w_ref[8 + 2 * j : 10 + 2 * j].reshape(2 * D, D)) * slope_s[:, lanes]).astype(BF)
+        bi = mm_nt(bb2, w_ref[8 + 2 * j : 10 + 2 * j].reshape(2 * D, D)) * slope_s[:, lanes]
+        bi_sum = column_sum(bi)
+        bi = bi.astype(BF)
         bi_s[rows, lanes] = bi
-        bi_sum = column_sum(bi.astype(F32))
         sums_ref[16 + 2 * j : 17 + 2 * j, :] += bi_sum[:, :D]
         sums_ref[17 + 2 * j : 18 + 2 * j, :] += bi_sum[:, D:]
         b2 = b2 + mm_nt(bi, up_s[:, lanes])

time: 191 us -> 192 us (level)
  transfers between devices with their start and end apart: 55 -> 55, of which waited for: 21 -> 19; matrix products, arithmetic and copies ran while one was open for 5% -> 5% of each run, Pallas kernels for 13% -> 12%
where the time goes in v3:
time: 192 us; the launch traced here: 191 us
  waiting for transfers between devices  64.8 us (34%)
  Pallas kernels  58.7 us (31%)
  starting transfers between devices  55.4 us (29%)
  local copies, waits for them, and re-layouts  7.23 us (4%)
  other arithmetic  4.13 us (2%)
    ppermute x55, waiting for transfers between devices, send(): return lax.ppermute(value, AXES, pairs)  64.8 us
    ppermute x55, starting transfers between devices, send(): return lax.ppermute(value, AXES, pairs)  55.4 us
    pallas_call x1, Pallas kernels, middle(): pl.pallas_call(functools.partial(middle_kernel, images, total_img), name=...  18.6 us
    pallas_call x2, Pallas kernels, attention_back(): pl.pallas_call(functools.partial(back_kernel, first), name='attention_bac...  10.9 us
    pallas_call x1, Pallas kernels, front(): pl.pallas_call(front_kernel, name='front', grid=(images,), out_shape=(sha...  8.89 us
    pallas_call x1, Pallas kernels, shampoo(): pl.pallas_call(functools.partial(shampoo_kernel, near), name='shampoo', g...  5.82 us
  transfers between devices with their start and end apart: 55, of which 19 were waited for; matrix products, arithmetic and copies ran while one was open for 5% of the time, Pallas kernels for 12%

profile of v3, /device:TPU:0, one launch (start us, length us, event | category | flops | bytes accessed | tf_op | source)
XLA Modules:
  0.0 191.5 jit_solution(1460837095299256353)
XLA Ops:
  0.6 1.9 convert_bitcast_fusion
  2.5 5.1 %collective-permute-start.2 = (bf16[520,128]{1,0:T(8,128)(2,1)}, bf16[520,128]{1,0:T(8,128)(2,1)S(1)}, u32[]{:S(2)}, u32[]{:S(2)}) collective-permute-start(bf16[520,128]{1,0:T(8,128)(2,1)} %get-tuple-element.186), channel_id=1, source_target_pairs={{0,24},{1,25},{2,26},{3,27},{4,28},{5,29},{6,30},{7,31},{8,16},{9,... | collective-permute-start | bytes 399368 | tf_op jit(solution)/shard_map/ppermute | solution.py:144
  8.1 1.7 collective-permute-start.5
  13.8 5.2 %collective-permute-done.1 = bf16[520,128]{1,0:T(8,128)(2,1)S(1)} collective-permute-done((bf16[520,128]{1,0:T(8,128)(2,1)}, bf16[520,128]{1,0:T(8,128)(2,1)S(1)}, u32[]{:S(2)}, u32[]{:S(2)}) %collective-permute-start.1) | collective-permute-done | bytes 133152 | tf_op jit(solution)/shard_map/ppermute | solution.py:144
  29.0 5.5 %collective-permute-done.3 = bf16[3,256,128]{2,1,0:T(8,128)(2,1)S(1)} collective-permute-done((bf16[3,256,128]{2,1,0:T(8,128)(2,1)S(1)}, bf16[3,256,128]{2,1,0:T(8,128)(2,1)S(1)}, u32[]{:S(2)}, u32[]{:S(2)}) %collective-permute-start.3) | collective-permute-done | bytes 196640 | tf_op jit(solution)/shard_map/ppermute | solution.py:144
  40.6 4.8 %collective-permute-done.8.refs_6_ = bf16[7,256,128]{2,1,0:T(8,128)(2,1)S(1)} collective-permute-done((bf16[7,256,128]{2,1,0:T(8,128)(2,1)S(1)}, bf16[7,256,128]{2,1,0:T(8,128)(2,1)S(1)}, u32[]{:S(2)}, u32[]{:S(2)}) %collective-permute-start.8) | collective-permute-done | bytes 458784 | tf_op jit(solution)/shard_map/ppermute | solution.py:144
  45.7 3.8 %collective-permute-done.7.refs_5_ = bf16[7,264,128]{2,1,0:T(8,128)(2,1)S(1)} collective-permute-done((bf16[7,264,128]{2,1,0:T(8,128)(2,1)S(1)}, bf16[7,264,128]{2,1,0:T(8,128)(2,1)S(1)}, u32[]{:S(2)}, u32[]{:S(2)}) %collective-permute-start.7) | collective-permute-done | bytes 473120 | tf_op jit(solution)/shard_map/ppermute | solution.py:144
  50.1 4.7 %collective-permute-done.17.far_ref = bf16[3,192,384]{2,1,0:T(8,128)(2,1)S(1)} collective-permute-done((bf16[3,192,384]{2,1,0:T(8,128)(2,1)S(1)}, bf16[3,192,384]{2,1,0:T(8,128)(2,1)S(1)}, u32[]{:S(2)}, u32[]{:S(2)}) %collective-permute-start.17) | collective-permute-done | bytes 442400 | tf_op jit(solution)/shard_map/ppermute | solution.py:144
  54.9 2.6 %conditioning.1 = (f32[8,3072]{1,0:T(8,128)S(1)}, f32[8,384]{1,0:T(8,128)S(1)}, f32[8,384]{1,0:T(8,128)S(1)}, f32[8,384]{1,0:T(8,128)S(1)}, bf16[384,2304]{1,0:T...) custom-call(s32[4]{0:T(128)S(1)} %pad_add_fusion.at_ref, ...), custom_call_target="tpu_custom_call" | custom-call | flops 1000000000 | bytes 10000000 | tf_op jit(solution)/shard_map/conditioning/pallas_call | solution.py:276
  58.4 8.9 %front.1 = (f32[4,256,384]{2,1,0:T(8,128)S(1)}, bf16[4,256,1152]{2,1,0:T(8,128)(2,1)S(1)}, bf16[4,256,384]{2,1,0:T(8,128)(2,1)S(1)}, f32[4,256,384]{2,1,0:T(8,128)S(1)}) custom-call(f32[4,16,256]{2,1,0:T(8,128)S(1)} %bitcast.76, f32[8,3072]{1,0:T(8,128)S(1)} %get-tuple-element.99.mods_ref, f32[16,384]{1,0:T(8,128)S(1)} %get-tuple-element.100.bias_ref, ...), custom_call_target="tpu_custom_call" | custom-call | flops 2200000000 | bytes 12000000 | tf_op jit(solution)/shard_map/front/pallas_call | solution.py:1020
  67.4 18.6 %middle.1 = (f32[4,256,384]{2,1,0:T(8,128)S(1)}, f32[4,8,384]{2,1,0:T(8,128)S(1)}, bf16[16,120,384]{2,1,0:T(8,128)(2,1)S(1)}, bf16[16,120,384]{2,1,0:T(8,128)(2,1)S(1)}, f32[24,384]{1,0:T(8,128)S(1)}) custom-call(s32[4]{0:T(128)S(1)} %pad_add_fusion.at_ref, f32[4]{0:T(128)S(1)} %copy-done.13, f32[4,256,384]{2,1,0:T(8,128)S(1)} %get-tuple-element.104.h1_ref, ...), custom_call_target="tpu_custom_call" | custom-call | flops 8999999488 | bytes 14000000 | tf_op jit(solution)/shard_map/middle/pallas_call | solution.py:1037
  86.5 2.7 %attention_back.2 = (bf16[1,256,384]{2,1,0:T(8,128)(2,1)S(1)}, bf16[1,256,1152]{2,1,0:T(8,128)(2,1)S(1)}, bf16[1,256,384]{2,1,0:T(8,128)(2,1)S(1)}, f32[1,8,384]{2,1,0:T(8,128)S(1)}, f32[1,16,384]{2,1,0:T(8,128)S(1)}) custom-call(f32[4,256,384]{2,1,0:T(8,128)S(1)} %get-tuple-element.107.bh1_ref, f32[4,256,384]{2,1,0:T(8,128)S(1)} %get-tuple-element.108.h0_ref, ...), custom_call_target="tpu_custom_call" | custom-call | flops 1200000000 | bytes 3000000 | tf_op jit(solution)/shard_map/attention_back/pallas_call | solution.py:1055
  89.2 8.2 %attention_back.3 = (bf16[3,256,384]{2,1,0:T(8,128)(2,1)S(1)}, bf16[3,256,1152]{2,1,0:T(8,128)(2,1)S(1)}, bf16[3,256,384]{2,1,0:T(8,128)(2,1)S(1)}, f32[3,8,384]{2,1,0:T(8,128)S(1)}, f32[3,16,384]{2,1,0:T(8,128)S(1)}) custom-call(f32[4,256,384]{2,1,0:T(8,128)S(1)} %get-tuple-element.107.bh1_ref, f32[4,256,384]{2,1,0:T(8,128)S(1)} %get-tuple-element.108.h0_ref, ...), custom_call_target="tpu_custom_call" | custom-call | flops 3600000000 | bytes 9000000 | tf_op jit(solution)/shard_map/attention_back/pallas_call | solution.py:1055
  97.4 2.4 %last_gradients.1 = (bf16[16,48,384]{2,1,0:T(8,128)(2,1)S(1)}, bf16[16,48,384]{2,1,0:T(8,128)(2,1)S(1)}) custom-call(s32[4]{0:T(128)S(1)} %pad_add_fusion.at_ref, bf16[1024,384]{1,0:T(8,128)(2,1)S(1)} %bitcast.66, bf16[256,384]{1,0:T(8,128)(2,1)S(1)} %bitcast.73, bf16[256,1152]{1,0:T(8,128)(2,1)S(1)} %bitcast.68, bf16[256,384]{1,0:T(8,128)(2,1)S(1)} %bitcast.72, ...), custom_call_target="tpu_custom_call" | custom-call | flops 1200000000 | bytes 9000000 | tf_op jit(solution)/shard_map/last_gradients/pallas_call | solution.py:1072
  108.1 4.2 %collective-permute-done.29.refs_1_ = bf16[4,120,384]{2,1,0:T(8,128)(2,1)S(1)} collective-permute-done((bf16[4,120,384]{2,1,0:T(8,128)(2,1)S(1)}, bf16[4,120,384]{2,1,0:T(8,128)(2,1)S(1)}, u32[]{:S(2)}, u32[]{:S(2)}) %collective-permute-start.29) | collective-permute-done | bytes 368672 | tf_op jit(solution)/shard_map/ppermute | solution.py:144
  112.3 2.4 %collective-permute-start.24 = (bf16[4,48,384]{2,1,0:T(8,128)(2,1)S(1)}, bf16[4,48,384]{2,1,0:T(8,128)(2,1)S(1)}, u32[]{:S(2)}, u32[]{:S(2)}) collective-permute-start(bf16[4,48,384]{2,1,0:T(8,128)(2,1)S(1)} %get-tuple-element.121), channel_id=1, source_target_pairs={{0,6},{1,7},{2,4},{3,5},{4,2},{5,3},{6,0},{7,1},{8,14},{9,15},{10,... | collective-permute-start | bytes 442376 | tf_op jit(solution)/shard_map/ppermute | solution.py:144
  114.7 7.0 %collective-permute-done.30.refs_2_ = bf16[4,120,384]{2,1,0:T(8,128)(2,1)S(1)} collective-permute-done((bf16[4,120,384]{2,1,0:T(8,128)(2,1)S(1)}, bf16[4,120,384]{2,1,0:T(8,128)(2,1)S(1)}, u32[]{:S(2)}, u32[]{:S(2)}) %collective-permute-start.30) | collective-permute-done | bytes 368672 | tf_op jit(solution)/shard_map/ppermute | solution.py:144
  123.2 3.5 %collective-permute-start.33 = (bf16[120,384]{1,0:T(8,128)(2,1)S(1)}, bf16[120,384]{1,0:T(8,128)(2,1)S(1)}, u32[]{:S(2)}, u32[]{:S(2)}) collective-permute-start(bf16[120,384]{1,0:T(8,128)(2,1)S(1)} %get-tuple-element.146), channel_id=1, source_target_pairs={{0,16},{1,17},{2,18},{3,19},{4,20},{5,21},{6,22},{7,23},{8,24},{9,... | collective-permute-start | bytes 276488 | tf_op jit(solution)/shard_map/ppermute | solution.py:144
  129.2 3.0 %collective-permute-start.26 = (bf16[48,384]{1,0:T(8,128)(2,1)S(1)}, bf16[48,384]{1,0:T(8,128)(2,1)S(1)}, u32[]{:S(2)}, u32[]{:S(2)}) collective-permute-start(bf16[48,384]{1,0:T(8,128)(2,1)S(1)} %get-tuple-element.124), channel_id=1, source_target_pairs={{0,16},{1,17},{2,18},{3,19},{4,20},{5,21},{6,22},{7,23},{8,24},{9,... | collective-permute-start | bytes 110600 | tf_op jit(solution)/shard_map/ppermute | solution.py:144
  133.4 1.7 cond_back.1.pay_ref
  135.7 1.7 collective-permute-done.26.refs_2_
  139.6 2.1 %collective-permute-start.36 = (bf16[64,384]{1,0:T(8,128)(2,1)S(1)}, bf16[64,384]{1,0:T(8,128)(2,1)S(1)}, u32[]{:S(2)}, u32[]{:S(2)}) collective-permute-start(bf16[64,384]{1,0:T(8,128)(2,1)S(1)} %get-tuple-element.151), channel_id=1, source_target_pairs={{0,16},{1,17},{2,18},{3,19},{4,20},{5,21},{6,22},{7,23},{8,24},{9,... | collective-permute-start | bytes 147464 | tf_op jit(solution)/shard_map/ppermute | solution.py:144
  143.2 2.7 %collective-permute-done.36 = bf16[64,384]{1,0:T(8,128)(2,1)S(1)} collective-permute-done((bf16[64,384]{1,0:T(8,128)(2,1)S(1)}, bf16[64,384]{1,0:T(8,128)(2,1)S(1)}, u32[]{:S(2)}, u32[]{:S(2)}) %collective-permute-start.36) | collective-permute-done | bytes 49184 | tf_op jit(solution)/shard_map/ppermute | solution.py:144
  145.9 1.7 collective-permute-done.37
  149.8 3.7 %collective-permute-done.39.near_ref = bf16[3,24,384]{2,1,0:T(8,128)(2,1)S(1)} collective-permute-done((bf16[3,24,384]{2,1,0:T(8,128)(2,1)S(1)}, bf16[3,24,384]{2,1,0:T(8,128)(2,1)S(1)}, u32[]{:S(2)}, u32[]{:S(2)}) %collective-permute-start.39) | collective-permute-done | bytes 55328 | tf_op jit(solution)/shard_map/ppermute | solution.py:144
  155.8 3.4 %collective-permute-done.42.refs_1_ = bf16[2,3,24,384]{3,2,1,0:T(8,128)(2,1)S(1)} collective-permute-done((bf16[2,3,24,384]{3,2,1,0:T(8,128)(2,1)S(1)}, bf16[2,3,24,384]{3,2,1,0:T(8,128)(2,1)S(1)}, u32[]{:S(2)}, u32[]{:S(2)}) %collective-permute-start.42) | collective-permute-done | bytes 110624 | tf_op jit(solution)/shard_map/ppermute | solution.py:144
  161.3 1.9 %collective-permute-start.45 = (bf16[2,3,24,384]{3,2,1,0:T(8,128)(2,1)S(1)}, bf16[2,3,24,384]{3,2,1,0:T(8,128)(2,1)S(1)}, u32[]{:S(2)}, u32[]{:S(2)}) collective-permute-start(bf16[2,3,24,384]{3,2,1,0:T(8,128)(2,1)S(1)} %join.1.refs_0_), channel_id=1, source_target_pairs={{0,24},{1,25},{2,26},{3,27},{4,28},{5,29},{6,30},{7,31},{8,16},{9,... | collective-permute-start | bytes 331784 | tf_op jit(solution)/shard_map/ppermute | solution.py:144
  163.2 7.1 %collective-permute-done.44.refs_2_ = bf16[2,3,24,384]{3,2,1,0:T(8,128)(2,1)S(1)} collective-permute-done((bf16[2,3,24,384]{3,2,1,0:T(8,128)(2,1)S(1)}, bf16[2,3,24,384]{3,2,1,0:T(8,128)(2,1)S(1)}, u32[]{:S(2)}, u32[]{:S(2)}) %collective-permute-start.44) | collective-permute-done | bytes 110624 | tf_op jit(solution)/shard_map/ppermute | solution.py:144
  172.3 4.1 %collective-permute-done.43.refs_5_ = bf16[2,3,24,384]{3,2,1,0:T(8,128)(2,1)S(1)} collective-permute-done((bf16[2,3,24,384]{3,2,1,0:T(8,128)(2,1)S(1)}, bf16[2,3,24,384]{3,2,1,0:T(8,128)(2,1)S(1)}, u32[]{:S(2)}, u32[]{:S(2)}) %collective-permute-start.43) | collective-permute-done | bytes 110624 | tf_op jit(solution)/shard_map/ppermute | solution.py:144
  179.8 2.8 %adam.1 = (f32[1,1]{1,0:T(1,128)}, f32[520,128]{1,0:T(8,128)}, f32[520,128]{1,0:T(8,128)}, f32[520,128]{1,0:T(8,128)}) custom-call(s32[4]{0:T(128)S(1)} %pad_add_fusion.at_ref, bf16[4,64,384]{2,1,0:T(8,128)(2,1)S(1)} %pad_maximum_fusion.3.refs_0_, bf16[4,64,384]{2,1,0:T(8,128)(2,1)S(1)} %collective-permute-done.41.refs_1_, ...), custom_call_target="tpu_custom_call" | custom-call | flops 1000000000 | bytes 10000000 | tf_op jit(solution)/shard_map/adam/pallas_call | solution.py:595
  182.5 1.9 collective-permute-done.47.refs_6_
  185.6 5.8 %shampoo.1 = (f32[3,384,384]{2,1,0:T(8,128)}, f32[3,384,384]{2,1,0:T(8,128)}, f32[3,384,384]{2,1,0:T(8,128)}) custom-call(s32[4]{0:T(128)S(1)} %pad_add_fusion.at_ref, bf16[2,3,24,384]{3,2,1,0:T(8,128)(2,1)S(1)} %join.1.refs_0_, bf16[2,3,24,384]{3,2,1,0:T(8,128)(2,1)S(1)} %collective-permute-done.42.refs_1_, ...), custom_call_target="tpu_custom_call" | custom-call | flops 3000000000 | bytes 15000000 | tf_op jit(solution)/shard_map/shampoo/pallas_call | solution.py:664
  (156 shorter events, 53.7 us)
Async XLA Ops:
  2.5 11.2 %collective-permute-start.2 = (bf16[520,128]{1,0:T(8,128)(2,1)}, bf16[520,128]{1,0:T(8,128)(2,1)S(1)}, u32[]{:S(2)}, u32[]{:S(2)}) collective-permute-start(bf16[520,128]{1,0:T(8,128)(2,1)} %get-tuple-element.186), channel_id=1, source_target_pairs={{0,24},{1,25},{2,26},{3,27},{4,28},{5,29},{6,30},{7,31},{8,16},{9,... | collective-permute-start | bytes 399368 | tf_op jit(solution)/shard_map/ppermute | solution.py:144
  7.6 11.5 %collective-permute-start.1 = (bf16[520,128]{1,0:T(8,128)(2,1)}, bf16[520,128]{1,0:T(8,128)(2,1)S(1)}, u32[]{:S(2)}, u32[]{:S(2)}) collective-permute-start(bf16[520,128]{1,0:T(8,128)(2,1)} %get-tuple-element.186), channel_id=1, source_target_pairs={{0,16},{1,17},{2,18},{3,19},{4,20},{5,21},{6,22},{7,23},{8,24},{9,... | collective-permute-start | bytes 399368 | tf_op jit(solution)/shard_map/ppermute | solution.py:144
  7.6 13.0 %collective-permute-start = (bf16[520,128]{1,0:T(8,128)(2,1)}, bf16[520,128]{1,0:T(8,128)(2,1)}, u32[]{:S(2)}, u32[]{:S(2)}) collective-permute-start(bf16[520,128]{1,0:T(8,128)(2,1)} %get-tuple-element.186), channel_id=1, source_target_pairs={{0,8},{1,9},{2,10},{3,11},{4,12},{5,13},{6,14},{7,15},{8,0},{9,1},... | collective-permute-start | bytes 399368 | tf_op jit(solution)/shard_map/ppermute | solution.py:144
  8.1 18.1 %collective-permute-start.5 = (bf16[520,128]{1,0:T(8,128)(2,1)}, bf16[520,128]{1,0:T(8,128)(2,1)}, u32[]{:S(2)}, u32[]{:S(2)}) collective-permute-start(bf16[520,128]{1,0:T(8,128)(2,1)} %get-tuple-element.186), channel_id=1, source_target_pairs={{0,2},{1,3},{2,0},{3,1},{4,6},{5,7},{6,4},{7,5},{8,10},{9,11},{10,... | collective-permute-start | bytes 399368 | tf_op jit(solution)/shard_map/ppermute | solution.py:144
  9.9 13.1 %collective-permute-start.4 = (bf16[520,128]{1,0:T(8,128)(2,1)}, bf16[520,128]{1,0:T(8,128)(2,1)}, u32[]{:S(2)}, u32[]{:S(2)}) collective-permute-start(bf16[520,128]{1,0:T(8,128)(2,1)} %get-tuple-element.186), channel_id=1, source_target_pairs={{0,4},{1,5},{2,6},{3,7},{4,0},{5,1},{6,2},{7,3},{8,12},{9,13},{10,... | collective-permute-start | bytes 399368 | tf_op jit(solution)/shard_map/ppermute | solution.py:144
  13.7 22.5 %collective-permute-start.9 = (bf16[520,128]{1,0:T(8,128)(2,1)}, bf16[520,128]{1,0:T(8,128)(2,1)S(1)}, u32[]{:S(2)}, u32[]{:S(2)}) collective-permute-start(bf16[520,128]{1,0:T(8,128)(2,1)} %get-tuple-element.186), channel_id=1, source_target_pairs={{0,1},{1,0},{2,3},{3,2},{4,5},{5,4},{6,7},{7,6},{8,9},{9,8},{10,11... | collective-permute-start | bytes 399368 | tf_op jit(solution)/shard_map/ppermute | solution.py:144
  19.0 21.2 %collective-permute-start.16 = (bf16[3,192,384]{2,1,0:T(8,128)(2,1)S(1)}, bf16[3,192,384]{2,1,0:T(8,128)(2,1)S(1)}, u32[]{:S(2)}, u32[]{:S(2)}) collective-permute-start(bf16[3,192,384]{2,1,0:T(8,128)(2,1)S(1)} %constant_dynamic-slice_fusion), channel_id=1, source_target_pairs={{0,2},{1,3},{2,0},{3,1},{4,6},{5,7},{6,4},{7,5},{8,10},{9,11},{10,... | collective-permute-start | bytes 1327112 | tf_op jit(solution)/shard_map/ppermute | solution.py:144
  21.4 13.0 %collective-permute-start.3 = (bf16[3,256,128]{2,1,0:T(8,128)(2,1)S(1)}, bf16[3,256,128]{2,1,0:T(8,128)(2,1)S(1)}, u32[]{:S(2)}, u32[]{:S(2)}) collective-permute-start(bf16[3,256,128]{2,1,0:T(8,128)(2,1)S(1)} %pad_maximum_fusion.2), channel_id=1, source_target_pairs={{0,2},{1,3},{2,0},{3,1},{4,6},{5,7},{6,4},{7,5},{8,10},{9,11},{10,... | collective-permute-start | bytes 589832 | tf_op jit(solution)/shard_map/ppermute | solution.py:144
  22.9 13.1 %collective-permute-start.6 = (bf16[3,264,128]{2,1,0:T(8,128)(2,1)S(1)}, bf16[3,264,128]{2,1,0:T(8,128)(2,1)S(1)}, u32[]{:S(2)}, u32[]{:S(2)}) collective-permute-start(bf16[3,264,128]{2,1,0:T(8,128)(2,1)S(1)} %pad_maximum_fusion.1), channel_id=1, source_target_pairs={{0,4},{1,5},{2,6},{3,7},{4,0},{5,1},{6,2},{7,3},{8,12},{9,13},{10,... | collective-permute-start | bytes 608264 | tf_op jit(solution)/shard_map/ppermute | solution.py:144
  26.3 12.5 %collective-permute-start.10 = (bf16[256,128]{1,0:T(8,128)(2,1)S(1)}, bf16[256,128]{1,0:T(8,128)(2,1)S(1)}, u32[]{:S(2)}, u32[]{:S(2)}) collective-permute-start(bf16[256,128]{1,0:T(8,128)(2,1)S(1)} %get-tuple-element.189), channel_id=1, source_target_pairs={{0,1},{1,0},{2,3},{3,2},{4,5},{5,4},{6,7},{7,6},{8,9},{9,8},{10,11... | collective-permute-start | bytes 196616 | tf_op jit(solution)/shard_map/ppermute | solution.py:144
  34.5 10.8 %collective-permute-start.8 = (bf16[7,256,128]{2,1,0:T(8,128)(2,1)S(1)}, bf16[7,256,128]{2,1,0:T(8,128)(2,1)S(1)}, u32[]{:S(2)}, u32[]{:S(2)}) collective-permute-start(bf16[7,256,128]{2,1,0:T(8,128)(2,1)S(1)} %constant_dynamic-update-slice_fusion.4.refs_4_), channel_id=1, source_target_pairs={{0,4},{1,5},{2,6},{3,7},{4,0},{5,1},{6,2},{7,3},{8,12},{9,13},{10,... | collective-permute-start | bytes 1376264 | tf_op jit(solution)/shard_map/ppermute | solution.py:144
  36.1 13.4 %collective-permute-start.13 = (bf16[7,256,128]{2,1,0:T(8,128)(2,1)S(1)}, bf16[7,256,128]{2,1,0:T(8,128)(2,1)S(1)}, u32[]{:S(2)}, u32[]{:S(2)}) collective-permute-start(bf16[7,256,128]{2,1,0:T(8,128)(2,1)S(1)} %constant_dynamic-update-slice_fusion.4.refs_4_), channel_id=1, source_target_pairs={{0,1},{1,0},{2,3},{3,2},{4,5},{5,4},{6,7},{7,6},{8,9},{9,8},{10,11... | collective-permute-start | bytes 1376264 | tf_op jit(solution)/shard_map/ppermute | solution.py:144
  36.2 13.3 %collective-permute-start.7 = (bf16[7,264,128]{2,1,0:T(8,128)(2,1)S(1)}, bf16[7,264,128]{2,1,0:T(8,128)(2,1)S(1)}, u32[]{:S(2)}, u32[]{:S(2)}) collective-permute-start(bf16[7,264,128]{2,1,0:T(8,128)(2,1)S(1)} %constant_dynamic-update-slice_fusion.refs_3_), channel_id=1, source_target_pairs={{0,2},{1,3},{2,0},{3,1},{4,6},{5,7},{6,4},{7,5},{8,10},{9,11},{10,... | collective-permute-start | bytes 1419272 | tf_op jit(solution)/shard_map/ppermute | solution.py:144
  40.0 10.0 %collective-permute-start.12 = (bf16[7,264,128]{2,1,0:T(8,128)(2,1)S(1)}, bf16[7,264,128]{2,1,0:T(8,128)(2,1)S(1)}, u32[]{:S(2)}, u32[]{:S(2)}) collective-permute-start(bf16[7,264,128]{2,1,0:T(8,128)(2,1)S(1)} %constant_dynamic-update-slice_fusion.refs_3_), channel_id=1, source_target_pairs={{0,1},{1,0},{2,3},{3,2},{4,5},{5,4},{6,7},{7,6},{8,9},{9,8},{10,11... | collective-permute-start | bytes 1419272 | tf_op jit(solution)/shard_map/ppermute | solution.py:144
  40.3 17.2 %collective-permute-start.18 = (bf16[3,384,384]{2,1,0:T(8,128)(2,1)S(1)}, bf16[3,384,384]{2,1,0:T(8,128)(2,1)S(1)}, u32[]{:S(2)}, u32[]{:S(2)}) collective-permute-start(bf16[3,384,384]{2,1,0:T(8,128)(2,1)S(1)} %convert_element_type.47.mine_ref), channel_id=1, source_target_pairs={{0,1},{1,0},{2,3},{3,2},{4,5},{5,4},{6,7},{7,6},{8,9},{9,8},{10,11... | collective-permute-start | bytes 2654216 | tf_op jit(solution)/shard_map/ppermute | solution.py:144
  45.3 9.5 %collective-permute-start.17 = (bf16[3,192,384]{2,1,0:T(8,128)(2,1)S(1)}, bf16[3,192,384]{2,1,0:T(8,128)(2,1)S(1)}, u32[]{:S(2)}, u32[]{:S(2)}) collective-permute-start(bf16[3,192,384]{2,1,0:T(8,128)(2,1)S(1)} %collective-permute-done.16.near_ref), channel_id=1, source_target_pairs={{0,8},{1,9},{2,10},{3,11},{4,12},{5,13},{6,14},{7,15},{8,0},{9,1},... | collective-permute-start | bytes 1327112 | tf_op jit(solution)/shard_map/ppermute | solution.py:144
  85.9 13.9 %collective-permute-start.28 = (bf16[16,120,384]{2,1,0:T(8,128)(2,1)S(1)}, bf16[16,120,384]{2,1,0:T(8,128)(2,1)S(1)}, u32[]{:S(2)}, u32[]{:S(2)}) collective-permute-start(bf16[16,120,384]{2,1,0:T(8,128)(2,1)S(1)} %get-tuple-element.139), channel_id=1, source_target_pairs={{0,1},{1,0},{2,3},{3,2},{4,5},{5,4},{6,7},{7,6},{8,9},{9,8},{10,11... | collective-permute-start | bytes 4423688 | tf_op jit(solution)/shard_map/ppermute | solution.py:144
  100.8 11.5 %collective-permute-start.29 = (bf16[4,120,384]{2,1,0:T(8,128)(2,1)S(1)}, bf16[4,120,384]{2,1,0:T(8,128)(2,1)S(1)}, u32[]{:S(2)}, u32[]{:S(2)}) collective-permute-start(bf16[4,120,384]{2,1,0:T(8,128)(2,1)S(1)} %get-tuple-element.141), channel_id=1, source_target_pairs={{0,4},{1,5},{2,6},{3,7},{4,0},{5,1},{6,2},{7,3},{8,12},{9,13},{10,... | collective-permute-start | bytes 1105928 | tf_op jit(solution)/shard_map/ppermute | solution.py:144
  102.3 19.4 %collective-permute-start.30 = (bf16[4,120,384]{2,1,0:T(8,128)(2,1)S(1)}, bf16[4,120,384]{2,1,0:T(8,128)(2,1)S(1)}, u32[]{:S(2)}, u32[]{:S(2)}) collective-permute-start(bf16[4,120,384]{2,1,0:T(8,128)(2,1)S(1)} %get-tuple-element.142), channel_id=1, source_target_pairs={{0,2},{1,3},{2,0},{3,1},{4,6},{5,7},{6,4},{7,5},{8,10},{9,11},{10,... | collective-permute-start | bytes 1105928 | tf_op jit(solution)/shard_map/ppermute | solution.py:144
  103.8 17.8 %collective-permute-start.31 = (bf16[4,120,384]{2,1,0:T(8,128)(2,1)S(1)}, bf16[4,120,384]{2,1,0:T(8,128)(2,1)S(1)}, u32[]{:S(2)}, u32[]{:S(2)}) collective-permute-start(bf16[4,120,384]{2,1,0:T(8,128)(2,1)S(1)} %get-tuple-element.143), channel_id=1, source_target_pairs={{0,6},{1,7},{2,4},{3,5},{4,2},{5,3},{6,0},{7,1},{8,14},{9,15},{10,... | collective-permute-start | bytes 1105928 | tf_op jit(solution)/shard_map/ppermute | solution.py:144
  105.0 21.7 %collective-permute-start.22 = (bf16[4,48,384]{2,1,0:T(8,128)(2,1)S(1)}, bf16[4,48,384]{2,1,0:T(8,128)(2,1)S(1)}, u32[]{:S(2)}, u32[]{:S(2)}) collective-permute-start(bf16[4,48,384]{2,1,0:T(8,128)(2,1)S(1)} %get-tuple-element.119), channel_id=1, source_target_pairs={{0,4},{1,5},{2,6},{3,7},{4,0},{5,1},{6,2},{7,3},{8,12},{9,13},{10,... | collective-permute-start | bytes 442376 | tf_op jit(solution)/shard_map/ppermute | solution.py:144
  106.6 21.3 %collective-permute-start.23 = (bf16[4,48,384]{2,1,0:T(8,128)(2,1)S(1)}, bf16[4,48,384]{2,1,0:T(8,128)(2,1)S(1)}, u32[]{:S(2)}, u32[]{:S(2)}) collective-permute-start(bf16[4,48,384]{2,1,0:T(8,128)(2,1)S(1)} %get-tuple-element.120), channel_id=1, source_target_pairs={{0,2},{1,3},{2,0},{3,1},{4,6},{5,7},{6,4},{7,5},{8,10},{9,11},{10,... | collective-permute-start | bytes 442376 | tf_op jit(solution)/shard_map/ppermute | solution.py:144
  112.3 15.6 %collective-permute-start.24 = (bf16[4,48,384]{2,1,0:T(8,128)(2,1)S(1)}, bf16[4,48,384]{2,1,0:T(8,128)(2,1)S(1)}, u32[]{:S(2)}, u32[]{:S(2)}) collective-permute-start(bf16[4,48,384]{2,1,0:T(8,128)(2,1)S(1)} %get-tuple-element.121), channel_id=1, source_target_pairs={{0,6},{1,7},{2,4},{3,5},{4,2},{5,3},{6,0},{7,1},{8,14},{9,15},{10,... | collective-permute-start | bytes 442376 | tf_op jit(solution)/shard_map/ppermute | solution.py:144
  122.4 9.7 %collective-permute-start.32 = (bf16[120,384]{1,0:T(8,128)(2,1)S(1)}, bf16[120,384]{1,0:T(8,128)(2,1)S(1)}, u32[]{:S(2)}, u32[]{:S(2)}) collective-permute-start(bf16[120,384]{1,0:T(8,128)(2,1)S(1)} %get-tuple-element.145), channel_id=1, source_target_pairs={{0,8},{1,9},{2,10},{3,11},{4,12},{5,13},{6,14},{7,15},{8,0},{9,1},... | collective-permute-start | bytes 276488 | tf_op jit(solution)/shard_map/ppermute | solution.py:144
  123.2 11.9 %collective-permute-start.33 = (bf16[120,384]{1,0:T(8,128)(2,1)S(1)}, bf16[120,384]{1,0:T(8,128)(2,1)S(1)}, u32[]{:S(2)}, u32[]{:S(2)}) collective-permute-start(bf16[120,384]{1,0:T(8,128)(2,1)S(1)} %get-tuple-element.146), channel_id=1, source_target_pairs={{0,16},{1,17},{2,18},{3,19},{4,20},{5,21},{6,22},{7,23},{8,24},{9,... | collective-permute-start | bytes 276488 | tf_op jit(solution)/shard_map/ppermute | solution.py:144
  147.7 11.5 %collective-permute-start.41 = (bf16[4,64,384]{2,1,0:T(8,128)(2,1)S(1)}, bf16[4,64,384]{2,1,0:T(8,128)(2,1)S(1)}, u32[]{:S(2)}, u32[]{:S(2)}) collective-permute-start(bf16[4,64,384]{2,1,0:T(8,128)(2,1)S(1)} %pad_maximum_fusion.3.refs_0_), channel_id=1, source_target_pairs={{0,4},{1,5},{2,6},{3,7},{4,0},{5,1},{6,2},{7,3},{8,12},{9,13},{10,... | collective-permute-start | bytes 589832 | tf_op jit(solution)/shard_map/ppermute | solution.py:144
  154.6 15.7 %collective-permute-start.49 = (bf16[4,64,384]{2,1,0:T(8,128)(2,1)S(1)}, bf16[4,64,384]{2,1,0:T(8,128)(2,1)S(1)}, u32[]{:S(2)}, u32[]{:S(2)}) collective-permute-start(bf16[4,64,384]{2,1,0:T(8,128)(2,1)S(1)} %pad_maximum_fusion.3.refs_0_), channel_id=1, source_target_pairs={{0,2},{1,3},{2,0},{3,1},{4,6},{5,7},{6,4},{7,5},{8,10},{9,11},{10,... | collective-permute-start | bytes 589832 | tf_op jit(solution)/shard_map/ppermute | solution.py:144
  159.2 11.7 %collective-permute-start.50 = (bf16[4,64,384]{2,1,0:T(8,128)(2,1)S(1)}, bf16[4,64,384]{2,1,0:T(8,128)(2,1)S(1)}, u32[]{:S(2)}, u32[]{:S(2)}) collective-permute-start(bf16[4,64,384]{2,1,0:T(8,128)(2,1)S(1)} %collective-permute-done.41.refs_1_), channel_id=1, source_target_pairs={{0,2},{1,3},{2,0},{3,1},{4,6},{5,7},{6,4},{7,5},{8,10},{9,11},{10,... | collective-permute-start | bytes 589832 | tf_op jit(solution)/shard_map/ppermute | solution.py:144
  160.2 10.2 %collective-permute-start.44 = (bf16[2,3,24,384]{3,2,1,0:T(8,128)(2,1)S(1)}, bf16[2,3,24,384]{3,2,1,0:T(8,128)(2,1)S(1)}, u32[]{:S(2)}, u32[]{:S(2)}) collective-permute-start(bf16[2,3,24,384]{3,2,1,0:T(8,128)(2,1)S(1)} %join.1.refs_0_), channel_id=1, source_target_pairs={{0,16},{1,17},{2,18},{3,19},{4,20},{5,21},{6,22},{7,23},{8,24},{9,... | collective-permute-start | bytes 331784 | tf_op jit(solution)/shard_map/ppermute | solution.py:144
  161.3 9.6 %collective-permute-start.45 = (bf16[2,3,24,384]{3,2,1,0:T(8,128)(2,1)S(1)}, bf16[2,3,24,384]{3,2,1,0:T(8,128)(2,1)S(1)}, u32[]{:S(2)}, u32[]{:S(2)}) collective-permute-start(bf16[2,3,24,384]{3,2,1,0:T(8,128)(2,1)S(1)} %join.1.refs_0_), channel_id=1, source_target_pairs={{0,24},{1,25},{2,26},{3,27},{4,28},{5,29},{6,30},{7,31},{8,16},{9,... | collective-permute-start | bytes 331784 | tf_op jit(solution)/shard_map/ppermute | solution.py:144
  163.2 14.5 %collective-permute-start.51 = (bf16[4,64,384]{2,1,0:T(8,128)(2,1)S(1)}, bf16[4,64,384]{2,1,0:T(8,128)(2,1)S(1)}, u32[]{:S(2)}, u32[]{:S(2)}) collective-permute-start(bf16[4,64,384]{2,1,0:T(8,128)(2,1)S(1)} %pad_maximum_fusion.3.refs_0_), channel_id=1, source_target_pairs={{0,1},{1,0},{2,3},{3,2},{4,5},{5,4},{6,7},{7,6},{8,9},{9,8},{10,11... | collective-permute-start | bytes 589832 | tf_op jit(solution)/shard_map/ppermute | solution.py:144
  170.3 9.4 %collective-permute-start.53 = (bf16[4,64,384]{2,1,0:T(8,128)(2,1)S(1)}, bf16[4,64,384]{2,1,0:T(8,128)(2,1)S(1)}, u32[]{:S(2)}, u32[]{:S(2)}) collective-permute-start(bf16[4,64,384]{2,1,0:T(8,128)(2,1)S(1)} %collective-permute-done.49.refs_2_), channel_id=1, source_target_pairs={{0,1},{1,0},{2,3},{3,2},{4,5},{5,4},{6,7},{7,6},{8,9},{9,8},{10,11... | collective-permute-start | bytes 589832 | tf_op jit(solution)/shard_map/ppermute | solution.py:144
  (37 other events, 470.5 us)

commit v4 on v3

--- a/solution.py
+++ b/solution.py
@@ -441,9 +441,9 @@
     plane[1], column[1] = lax.optimization_barrier((plane[1], column[1]))
     plane.append(send(plane[1], TO_Y))
     crossed.append(send(column[1], TO_X))
-    crossed[1], column[2], column[3] = lax.optimization_barrier((crossed[1], column[2], column[3]))
+    pairs = [send(p, TO_C) for p in plane[:3]]
     slots = column + crossed + [send(v, TO_X) for v in column[2:]]
-    return slots, plane + [send(p, TO_C) for p in plane]
+    return slots, plane + pairs + [send(plane[3], TO_C)]
 
 
 def plane_gradient(plane, pay_ref, flat, rolled, align):
@@ -727,22 +727,43 @@
     qkv_ref[0, :, 0:D] = q
     qkv_ref[0, :, D : 2 * D] = k
     qkv_ref[0, :, 2 * D :] = v
+    v_t = v.T
     scores, probs, outs = [], [], []
     for h in range(HEADS + 2):
         if h < HEADS:
-            scores.append(mm_nt(head(q, h), head(k, h)))
+            scores.append(mm_nt(head(k, h), head(q, h)))
         if 1 <= h <= HEADS:
             s = scores[h - 1] * QK_SCALE
-            e = jnp.exp(s - jnp.max(s, axis=-1, keepdims=True))
-            probs.append((e * (1.0 / jnp.sum(e, axis=-1, keepdims=True))).astype(BF))
+            e = jnp.exp(s - jnp.max(s, axis=0, keepdims=True))
+            probs.append((e * (1.0 / column_sum(e))).astype(BF))
         if h >= 2:
-            outs.append(mm(probs[h - 2], head(v, h - 2)))
-    att = jnp.concatenate(outs, axis=1).astype(BF)
+            outs.append(mm(v_t[HDIM * (h - 2) : HDIM * (h - 1), :], probs[h - 2]))
+    att = jnp.concatenate(outs, axis=0).astype(BF).T
     att_ref[0] = att
     h1_ref[0] = h0 + mod(2) * (mm(att, w_ref[3]) + bias_ref[3:4, :])
 
 
-def middle_kernel(images, total_img, at_ref, tw_ref, h1_ref, vel_ref, dino_ref, mods_ref, bias_ref, w_ref, aw_ref, fw_ref,
+def encoder_kernel(dino_ref, out_ref):
+    dino = dino_ref[0].astype(F32)
+    out_ref[0] = lax.rsqrt(jnp.sum(dino * dino, axis=-1, keepdims=True) + NORM_EPS)
+
+
+def encoder_norms(dino):
+    images = dino.shape[0]
+    each = functools.partial(rows_each, 0)
+    return pl.pallas_call(
+        encoder_kernel,
+        name="encoder_norms",
+        grid=(images,),
+        out_shape=shape((images, SEQ, 1)),
+        in_specs=[each(SEQ, DINO)],
+        out_specs=each(SEQ, 1),
+        compiler_params=room(8),
+        cost_estimate=cost(1e6, 2e6),
+    )(dino)
+
+
+def middle_kernel(images, total_img, at_ref, tw_ref, h1_ref, vel_ref, dino_ref, rd_ref, mods_ref, bias_ref, w_ref, aw_ref, fw_ref,
                   bh1_ref, gm_ref, mine_ref, other_ref, sums_ref,
                   act2_s, gelu_s, slope_s, bi_s, bb2_s, h1_s, ba_s, act3_s, bo_s, up_s):
     i = pl.program_id(0)
@@ -792,7 +813,7 @@
     dino = dino_ref[0].astype(F32)
     dot = jnp.sum(aligned * dino, axis=-1, keepdims=True)
     ra = lax.rsqrt(jnp.sum(aligned * aligned, axis=-1, keepdims=True) + NORM_EPS)
-    rd = lax.rsqrt(jnp.sum(dino * dino, axis=-1, keepdims=True) + NORM_EPS)
+    rd = rd_ref[0]
     x_two = expand(1)
     g_one = activate(0, x_one)
     scale = REPA_WEIGHT / (total_img * SEQ)
@@ -821,7 +842,9 @@
 
     b3 = mm_nt(bo, fw_ref[...])
     bh2 = norm_back(b3 * (1.0 + mod(7)), n3, inv3)
-    bb2 = (bh2 * mod(5)).astype(BF)
+    bb2 = bh2 * mod(5)
+    bb2_sum = column_sum(bb2)
+    bb2 = bb2.astype(BF)
     bb2_s[rows, :] = bb2
     b2 = jnp.zeros((SEQ, D), F32)
     for j in range(2):
@@ -833,7 +856,7 @@
         sums_ref[16 + 2 * j : 17 + 2 * j, :] += bi_sum[:, :D]
         sums_ref[17 + 2 * j : 18 + 2 * j, :] += bi_sum[:, D:]
         b2 = b2 + mm_nt(bi, up_s[:, lanes])
-    sums_ref[20:21, :] += column_sum(bb2.astype(F32))
+    sums_ref[20:21, :] += bb2_sum
     sums_ref[21:22, :] += ba_sum[:, :D]
     sums_ref[22:23, :] += ba_sum[:, D:]
     sums_ref[23:24, 0:128] += column_sum(bo.astype(F32))
@@ -883,6 +906,7 @@
     gm_ref[0, 2:3, :] = column_sum(bh1 * (mm(att, w_ref[3]) + bias_ref[3:4, :]))
     batt = mm_nt(bb1, w_ref[3]).astype(BF)
     q, k, v = qkv_ref[0, :, 0:D], qkv_ref[0, :, D : 2 * D], qkv_ref[0, :, 2 * D :]
+    k_t = k.T
     ready, halves, gq, gk, gv = [], [], [], [], []
     for h in range(HEADS + 2):
         if h < HEADS:
@@ -897,8 +921,8 @@
             p, ds = halves[h - 2]
             gv.append(mm(p, head(batt, h - 2)))
             gk.append(mm(ds, head(q, h - 2)))
-            gq.append(mm_tn(ds, head(k, h - 2)))
-    bq = (jnp.concatenate(gq, axis=1) * QK_SCALE).astype(BF)
+            gq.append(mm(k_t[HDIM * (h - 2) : HDIM * (h - 1), :], ds))
+    bq = (jnp.concatenate(gq, axis=0) * QK_SCALE).astype(BF).T
     bk = (jnp.concatenate(gk, axis=1) * QK_SCALE).astype(BF)
     bv = jnp.concatenate(gv, axis=1).astype(BF)
     bp_ref[0, :, 0:D] = bq
@@ -1030,7 +1054,7 @@
     )(noisy, mods, bias, patch_low, pos, blocks)
 
 
-def middle(total_img, at, time_weight, h1, velocity, dino, mods, bias, blocks, align_low, final_low):
+def middle(total_img, at, time_weight, h1, velocity, dino, dino_rd, mods, bias, blocks, align_low, final_low):
     images = h1.shape[0]
     each = functools.partial(rows_each, 0)
     full = lambda lanes, kind=BF: pltpu.VMEM((images * SEQ, lanes), kind)
@@ -1040,13 +1064,13 @@
         grid=(images,),
         out_shape=(shape((images, SEQ, D)), shape((images, 8, D)),
                    shape((16, EARLY, D), BF), shape((16, EARLY, D), BF), shape((SUMS_MLP, D))),
-        in_specs=[SM, SM, each(SEQ, D), each(PD, SEQ), each(SEQ, DINO), VM, VM, VM, VM, VM],
+        in_specs=[SM, SM, each(SEQ, D), each(PD, SEQ), each(SEQ, DINO), each(SEQ, 1), VM, VM, VM, VM, VM],
         out_specs=[each(SEQ, D), each(8, D), VM, VM, VM],
         scratch_shapes=[full(D), full(F), pltpu.VMEM((SEQ, F), F32), full(F), full(D), full(D),
                         full(DINO), full(D), full(128), pltpu.VMEM((D, F), BF)],
         compiler_params=room(40),
         cost_estimate=cost(9e9, 1.4e7),
-    )(at, time_weight, h1, velocity, dino, mods, bias, blocks, align_low, final_low)
+    )(at, time_weight, h1, velocity, dino, dino_rd, mods, bias, blocks, align_low, final_low)
 
 
 def attention_back(first, count, bh1, h0, qkv, att, noisy, mods, bias, blocks):
@@ -1139,6 +1163,7 @@
     mine = flat_w.astype(BF)
     features = jnp.pad(time_features(tstep_idx), ((0, 4), (0, 0)))
     pos = position_table()
+    dino_rd = encoder_norms(dino)
     noisy = jnp.transpose(noisy, (0, 2, 1))
     velocity = jnp.transpose(velocity, (0, 2, 1))
     rows = flat_w.shape[0]
@@ -1161,7 +1186,7 @@
         at, class_ids, features, pieces, places, rows)
     h0, qkv, att, h1 = front(noisy, mods, bias, patch_low, pos, blocks)
     bh1, gm2, mine, other, sums = middle(
-        total_img, at, time_weight, h1, velocity, dino, mods, bias, blocks, align_low, final_low)
+        total_img, at, time_weight, h1, velocity, dino, dino_rd, mods, bias, blocks, align_low, final_low)
     if near:
         early = reduce_units(at, mine, other)
     parts, gm3 = [], []

time: 192 us -> 190 us (0.990)
  transfers between devices with their start and end apart: 55 -> 55, of which waited for: 19 -> 21; matrix products, arithmetic and copies ran while one was open for 5% -> 5% of each run, Pallas kernels for 12% -> 13%
where the time goes in v4:
time: 190 us
  waiting for transfers between devices  64 us (34%)
  Pallas kernels  58.7 us (31%)
  starting transfers between devices  54.4 us (29%)
  local copies, waits for them, and re-layouts  7.35 us (4%)
  other arithmetic  4.13 us (2%)
    ppermute x55, waiting for transfers between devices, send(): return lax.ppermute(value, AXES, pairs)  64 us
    ppermute x55, starting transfers between devices, send(): return lax.ppermute(value, AXES, pairs)  54.4 us
    pallas_call x1, Pallas kernels, middle(): pl.pallas_call(functools.partial(middle_kernel, images, total_img), name=...  18.7 us
    pallas_call x2, Pallas kernels, attention_back(): pl.pallas_call(functools.partial(back_kernel, first), name='attention_bac...  10.4 us
    pallas_call x1, Pallas kernels, front(): pl.pallas_call(front_kernel, name='front', grid=(images,), out_shape=(sha...  8.31 us
    pallas_call x1, Pallas kernels, shampoo(): pl.pallas_call(functools.partial(shampoo_kernel, near), name='shampoo', g...  5.82 us
  transfers between devices with their start and end apart: 55, of which 21 were waited for; matrix products, arithmetic and copies ran while one was open for 5% of the time, Pallas kernels for 13%

profile of v4, /device:TPU:0, one launch (start us, length us, event | category | flops | bytes accessed | tf_op | source)
XLA Modules:
  0.0 189.8 jit_solution(3914360311711690156)
XLA Ops:
  0.6 1.9 convert_bitcast_fusion
  2.5 5.1 %collective-permute-start.2 = (bf16[520,128]{1,0:T(8,128)(2,1)}, bf16[520,128]{1,0:T(8,128)(2,1)S(1)}, u32[]{:S(2)}, u32[]{:S(2)}) collective-permute-start(bf16[520,128]{1,0:T(8,128)(2,1)} %get-tuple-element.180), channel_id=1, source_target_pairs={{0,24},{1,25},{2,26},{3,27},{4,28},{5,29},{6,30},{7,31},{8,16},{9,... | collective-permute-start | bytes 399368 | tf_op jit(solution)/shard_map/ppermute | solution.py:144
  8.1 1.7 collective-permute-start.5
  13.8 5.2 %collective-permute-done.1 = bf16[520,128]{1,0:T(8,128)(2,1)S(1)} collective-permute-done((bf16[520,128]{1,0:T(8,128)(2,1)}, bf16[520,128]{1,0:T(8,128)(2,1)S(1)}, u32[]{:S(2)}, u32[]{:S(2)}) %collective-permute-start.1) | collective-permute-done | bytes 133152 | tf_op jit(solution)/shard_map/ppermute | solution.py:144
  29.1 5.4 %collective-permute-done.3 = bf16[3,256,128]{2,1,0:T(8,128)(2,1)S(1)} collective-permute-done((bf16[3,256,128]{2,1,0:T(8,128)(2,1)S(1)}, bf16[3,256,128]{2,1,0:T(8,128)(2,1)S(1)}, u32[]{:S(2)}, u32[]{:S(2)}) %collective-permute-start.3) | collective-permute-done | bytes 196640 | tf_op jit(solution)/shard_map/ppermute | solution.py:144
  36.2 1.6 collective-permute-start.7
  40.6 4.8 %collective-permute-done.8.refs_6_ = bf16[7,256,128]{2,1,0:T(8,128)(2,1)S(1)} collective-permute-done((bf16[7,256,128]{2,1,0:T(8,128)(2,1)S(1)}, bf16[7,256,128]{2,1,0:T(8,128)(2,1)S(1)}, u32[]{:S(2)}, u32[]{:S(2)}) %collective-permute-start.8) | collective-permute-done | bytes 458784 | tf_op jit(solution)/shard_map/ppermute | solution.py:144
  45.7 3.8 %collective-permute-done.7.refs_5_ = bf16[7,264,128]{2,1,0:T(8,128)(2,1)S(1)} collective-permute-done((bf16[7,264,128]{2,1,0:T(8,128)(2,1)S(1)}, bf16[7,264,128]{2,1,0:T(8,128)(2,1)S(1)}, u32[]{:S(2)}, u32[]{:S(2)}) %collective-permute-start.7) | collective-permute-done | bytes 473120 | tf_op jit(solution)/shard_map/ppermute | solution.py:144
  50.1 4.7 %collective-permute-done.17.far_ref = bf16[3,192,384]{2,1,0:T(8,128)(2,1)S(1)} collective-permute-done((bf16[3,192,384]{2,1,0:T(8,128)(2,1)S(1)}, bf16[3,192,384]{2,1,0:T(8,128)(2,1)S(1)}, u32[]{:S(2)}, u32[]{:S(2)}) %collective-permute-start.17) | collective-permute-done | bytes 442400 | tf_op jit(solution)/shard_map/ppermute | solution.py:144
  55.6 2.6 %conditioning.1 = (f32[8,3072]{1,0:T(8,128)S(1)}, f32[8,384]{1,0:T(8,128)S(1)}, f32[8,384]{1,0:T(8,128)S(1)}, f32[8,384]{1,0:T(8,128)S(1)}, bf16[384,2304]{1,0:T...) custom-call(s32[4]{0:T(128)S(1)} %pad_add_fusion.at_ref, ...), custom_call_target="tpu_custom_call" | custom-call | flops 1000000000 | bytes 10000000 | tf_op jit(solution)/shard_map/conditioning/pallas_call | solution.py:276
  59.1 8.3 %front.1 = (f32[4,256,384]{2,1,0:T(8,128)S(1)}, bf16[4,256,1152]{2,1,0:T(8,128)(2,1)S(1)}, bf16[4,256,384]{2,1,0:T(8,128)(2,1)S(1)}, f32[4,256,384]{2,1,0:T(8,128)S(1)}) custom-call(f32[4,16,256]{2,1,0:T(8,128)S(1)} %bitcast.76, f32[8,3072]{1,0:T(8,128)S(1)} %get-tuple-element.96.mods_ref, f32[16,384]{1,0:T(8,128)S(1)} %get-tuple-element.97.bias_ref, ...), custom_call_target="tpu_custom_call" | custom-call | flops 2200000000 | bytes 12000000 | tf_op jit(solution)/shard_map/front/pallas_call | solution.py:1044
  67.4 18.7 %middle.1 = (f32[4,256,384]{2,1,0:T(8,128)S(1)}, f32[4,8,384]{2,1,0:T(8,128)S(1)}, bf16[16,120,384]{2,1,0:T(8,128)(2,1)S(1)}, bf16[16,120,384]{2,1,0:T(8,128)(2,1)S(1)}, f32[24,384]{1,0:T(8,128)S(1)}) custom-call(s32[4]{0:T(128)S(1)} %pad_add_fusion.at_ref, f32[4]{0:T(128)S(1)} %copy-done.13, f32[4,256,384]{2,1,0:T(8,128)S(1)} %get-tuple-element.101.h1_ref, ...), custom_call_target="tpu_custom_call" | custom-call | flops 8999999488 | bytes 14000000 | tf_op jit(solution)/shard_map/middle/pallas_call | solution.py:1061
  86.7 2.6 %attention_back.2 = (bf16[1,256,384]{2,1,0:T(8,128)(2,1)S(1)}, bf16[1,256,1152]{2,1,0:T(8,128)(2,1)S(1)}, bf16[1,256,384]{2,1,0:T(8,128)(2,1)S(1)}, f32[1,8,384]{2,1,0:T(8,128)S(1)}, f32[1,16,384]{2,1,0:T(8,128)S(1)}) custom-call(f32[4,256,384]{2,1,0:T(8,128)S(1)} %get-tuple-element.104.bh1_ref, f32[4,256,384]{2,1,0:T(8,128)S(1)} %get-tuple-element.105.h0_ref, ...), custom_call_target="tpu_custom_call" | custom-call | flops 1200000000 | bytes 3000000 | tf_op jit(solution)/shard_map/attention_back/pallas_call | solution.py:1079
  89.3 7.8 %attention_back.3 = (bf16[3,256,384]{2,1,0:T(8,128)(2,1)S(1)}, bf16[3,256,1152]{2,1,0:T(8,128)(2,1)S(1)}, bf16[3,256,384]{2,1,0:T(8,128)(2,1)S(1)}, f32[3,8,384]{2,1,0:T(8,128)S(1)}, f32[3,16,384]{2,1,0:T(8,128)S(1)}) custom-call(f32[4,256,384]{2,1,0:T(8,128)S(1)} %get-tuple-element.104.bh1_ref, f32[4,256,384]{2,1,0:T(8,128)S(1)} %get-tuple-element.105.h0_ref, ...), custom_call_target="tpu_custom_call" | custom-call | flops 3600000000 | bytes 9000000 | tf_op jit(solution)/shard_map/attention_back/pallas_call | solution.py:1079
  97.2 2.4 %last_gradients.1 = (bf16[16,48,384]{2,1,0:T(8,128)(2,1)S(1)}, bf16[16,48,384]{2,1,0:T(8,128)(2,1)S(1)}) custom-call(s32[4]{0:T(128)S(1)} %pad_add_fusion.at_ref, bf16[1024,384]{1,0:T(8,128)(2,1)S(1)} %bitcast.66, bf16[256,384]{1,0:T(8,128)(2,1)S(1)} %bitcast.73, bf16[256,1152]{1,0:T(8,128)(2,1)S(1)} %bitcast.68, bf16[256,384]{1,0:T(8,128)(2,1)S(1)} %bitcast.72, ...), custom_call_target="tpu_custom_call" | custom-call | flops 1200000000 | bytes 9000000 | tf_op jit(solution)/shard_map/last_gradients/pallas_call | solution.py:1096
  107.9 4.2 %collective-permute-done.29.refs_1_ = bf16[4,120,384]{2,1,0:T(8,128)(2,1)S(1)} collective-permute-done((bf16[4,120,384]{2,1,0:T(8,128)(2,1)S(1)}, bf16[4,120,384]{2,1,0:T(8,128)(2,1)S(1)}, u32[]{:S(2)}, u32[]{:S(2)}) %collective-permute-start.29) | collective-permute-done | bytes 368672 | tf_op jit(solution)/shard_map/ppermute | solution.py:144
  112.1 2.5 %collective-permute-start.24 = (bf16[4,48,384]{2,1,0:T(8,128)(2,1)S(1)}, bf16[4,48,384]{2,1,0:T(8,128)(2,1)S(1)}, u32[]{:S(2)}, u32[]{:S(2)}) collective-permute-start(bf16[4,48,384]{2,1,0:T(8,128)(2,1)S(1)} %get-tuple-element.118), channel_id=1, source_target_pairs={{0,6},{1,7},{2,4},{3,5},{4,2},{5,3},{6,0},{7,1},{8,14},{9,15},{10,... | collective-permute-start | bytes 442376 | tf_op jit(solution)/shard_map/ppermute | solution.py:144
  114.5 7.0 %collective-permute-done.30.refs_2_ = bf16[4,120,384]{2,1,0:T(8,128)(2,1)S(1)} collective-permute-done((bf16[4,120,384]{2,1,0:T(8,128)(2,1)S(1)}, bf16[4,120,384]{2,1,0:T(8,128)(2,1)S(1)}, u32[]{:S(2)}, u32[]{:S(2)}) %collective-permute-start.30) | collective-permute-done | bytes 368672 | tf_op jit(solution)/shard_map/ppermute | solution.py:144
  123.0 3.5 %collective-permute-start.33 = (bf16[120,384]{1,0:T(8,128)(2,1)S(1)}, bf16[120,384]{1,0:T(8,128)(2,1)S(1)}, u32[]{:S(2)}, u32[]{:S(2)}) collective-permute-start(bf16[120,384]{1,0:T(8,128)(2,1)S(1)} %get-tuple-element.143), channel_id=1, source_target_pairs={{0,16},{1,17},{2,18},{3,19},{4,20},{5,21},{6,22},{7,23},{8,24},{9,... | collective-permute-start | bytes 276488 | tf_op jit(solution)/shard_map/ppermute | solution.py:144
  129.0 3.0 %collective-permute-start.26 = (bf16[48,384]{1,0:T(8,128)(2,1)S(1)}, bf16[48,384]{1,0:T(8,128)(2,1)S(1)}, u32[]{:S(2)}, u32[]{:S(2)}) collective-permute-start(bf16[48,384]{1,0:T(8,128)(2,1)S(1)} %get-tuple-element.121), channel_id=1, source_target_pairs={{0,16},{1,17},{2,18},{3,19},{4,20},{5,21},{6,22},{7,23},{8,24},{9,... | collective-permute-start | bytes 110600 | tf_op jit(solution)/shard_map/ppermute | solution.py:144
  133.2 1.7 cond_back.1.pay_ref
  135.5 1.7 collective-permute-done.26.refs_2_
  139.4 2.0 %collective-permute-start.36 = (bf16[64,384]{1,0:T(8,128)(2,1)S(1)}, bf16[64,384]{1,0:T(8,128)(2,1)S(1)}, u32[]{:S(2)}, u32[]{:S(2)}) collective-permute-start(bf16[64,384]{1,0:T(8,128)(2,1)S(1)} %get-tuple-element.148), channel_id=1, source_target_pairs={{0,16},{1,17},{2,18},{3,19},{4,20},{5,21},{6,22},{7,23},{8,24},{9,... | collective-permute-start | bytes 147464 | tf_op jit(solution)/shard_map/ppermute | solution.py:144
  143.0 2.7 %collective-permute-done.36 = bf16[64,384]{1,0:T(8,128)(2,1)S(1)} collective-permute-done((bf16[64,384]{1,0:T(8,128)(2,1)S(1)}, bf16[64,384]{1,0:T(8,128)(2,1)S(1)}, u32[]{:S(2)}, u32[]{:S(2)}) %collective-permute-start.36) | collective-permute-done | bytes 49184 | tf_op jit(solution)/shard_map/ppermute | solution.py:144
  145.7 1.7 collective-permute-done.37
  149.5 3.7 %collective-permute-done.39.near_ref = bf16[3,24,384]{2,1,0:T(8,128)(2,1)S(1)} collective-permute-done((bf16[3,24,384]{2,1,0:T(8,128)(2,1)S(1)}, bf16[3,24,384]{2,1,0:T(8,128)(2,1)S(1)}, u32[]{:S(2)}, u32[]{:S(2)}) %collective-permute-start.39) | collective-permute-done | bytes 55328 | tf_op jit(solution)/shard_map/ppermute | solution.py:144
  155.6 3.4 %collective-permute-done.42.refs_1_ = bf16[2,3,24,384]{3,2,1,0:T(8,128)(2,1)S(1)} collective-permute-done((bf16[2,3,24,384]{3,2,1,0:T(8,128)(2,1)S(1)}, bf16[2,3,24,384]{3,2,1,0:T(8,128)(2,1)S(1)}, u32[]{:S(2)}, u32[]{:S(2)}) %collective-permute-start.42) | collective-permute-done | bytes 110624 | tf_op jit(solution)/shard_map/ppermute | solution.py:144
  161.6 3.7 %collective-permute-done.50.refs_3_ = bf16[4,64,384]{2,1,0:T(8,128)(2,1)S(1)} collective-permute-done((bf16[4,64,384]{2,1,0:T(8,128)(2,1)S(1)}, bf16[4,64,384]{2,1,0:T(8,128)(2,1)S(1)}, u32[]{:S(2)}, u32[]{:S(2)}) %collective-permute-start.50) | collective-permute-done | bytes 196640 | tf_op jit(solution)/shard_map/ppermute | solution.py:144
  165.3 1.8 collective-permute-done.43.refs_2_
  168.7 5.1 %collective-permute-done.44.refs_3_ = bf16[2,3,24,384]{3,2,1,0:T(8,128)(2,1)S(1)} collective-permute-done((bf16[2,3,24,384]{3,2,1,0:T(8,128)(2,1)S(1)}, bf16[2,3,24,384]{3,2,1,0:T(8,128)(2,1)S(1)}, u32[]{:S(2)}, u32[]{:S(2)}) %collective-permute-start.44) | collective-permute-done | bytes 110624 | tf_op jit(solution)/shard_map/ppermute | solution.py:144
  177.9 3.0 %adam.1 = (f32[1,1]{1,0:T(1,128)}, f32[520,128]{1,0:T(8,128)}, f32[520,128]{1,0:T(8,128)}, f32[520,128]{1,0:T(8,128)}) custom-call(s32[4]{0:T(128)S(1)} %pad_add_fusion.at_ref, bf16[4,64,384]{2,1,0:T(8,128)(2,1)S(1)} %pad_maximum_fusion.3.refs_0_, bf16[4,64,384]{2,1,0:T(8,128)(2,1)S(1)} %collective-permute-done.41.refs_1_, ...), custom_call_target="tpu_custom_call" | custom-call | flops 1000000000 | bytes 10000000 | tf_op jit(solution)/shard_map/adam/pallas_call | solution.py:595
  183.9 5.8 %shampoo.1 = (f32[3,384,384]{2,1,0:T(8,128)}, f32[3,384,384]{2,1,0:T(8,128)}, f32[3,384,384]{2,1,0:T(8,128)}) custom-call(s32[4]{0:T(128)S(1)} %pad_add_fusion.at_ref, bf16[2,3,24,384]{3,2,1,0:T(8,128)(2,1)S(1)} %join.1.refs_0_, bf16[2,3,24,384]{3,2,1,0:T(8,128)(2,1)S(1)} %collective-permute-done.42.refs_1_, ...), custom_call_target="tpu_custom_call" | custom-call | flops 3000000000 | bytes 15000000 | tf_op jit(solution)/shard_map/shampoo/pallas_call | solution.py:664
  (157 shorter events, 55.5 us)
Async XLA Ops:
  2.5 11.2 %collective-permute-start.2 = (bf16[520,128]{1,0:T(8,128)(2,1)}, bf16[520,128]{1,0:T(8,128)(2,1)S(1)}, u32[]{:S(2)}, u32[]{:S(2)}) collective-permute-start(bf16[520,128]{1,0:T(8,128)(2,1)} %get-tuple-element.180), channel_id=1, source_target_pairs={{0,24},{1,25},{2,26},{3,27},{4,28},{5,29},{6,30},{7,31},{8,16},{9,... | collective-permute-start | bytes 399368 | tf_op jit(solution)/shard_map/ppermute | solution.py:144
  7.6 11.5 %collective-permute-start.1 = (bf16[520,128]{1,0:T(8,128)(2,1)}, bf16[520,128]{1,0:T(8,128)(2,1)S(1)}, u32[]{:S(2)}, u32[]{:S(2)}) collective-permute-start(bf16[520,128]{1,0:T(8,128)(2,1)} %get-tuple-element.180), channel_id=1, source_target_pairs={{0,16},{1,17},{2,18},{3,19},{4,20},{5,21},{6,22},{7,23},{8,24},{9,... | collective-permute-start | bytes 399368 | tf_op jit(solution)/shard_map/ppermute | solution.py:144
  7.6 13.0 %collective-permute-start = (bf16[520,128]{1,0:T(8,128)(2,1)}, bf16[520,128]{1,0:T(8,128)(2,1)}, u32[]{:S(2)}, u32[]{:S(2)}) collective-permute-start(bf16[520,128]{1,0:T(8,128)(2,1)} %get-tuple-element.180), channel_id=1, source_target_pairs={{0,8},{1,9},{2,10},{3,11},{4,12},{5,13},{6,14},{7,15},{8,0},{9,1},... | collective-permute-start | bytes 399368 | tf_op jit(solution)/shard_map/ppermute | solution.py:144
  8.1 18.2 %collective-permute-start.5 = (bf16[520,128]{1,0:T(8,128)(2,1)}, bf16[520,128]{1,0:T(8,128)(2,1)}, u32[]{:S(2)}, u32[]{:S(2)}) collective-permute-start(bf16[520,128]{1,0:T(8,128)(2,1)} %get-tuple-element.180), channel_id=1, source_target_pairs={{0,2},{1,3},{2,0},{3,1},{4,6},{5,7},{6,4},{7,5},{8,10},{9,11},{10,... | collective-permute-start | bytes 399368 | tf_op jit(solution)/shard_map/ppermute | solution.py:144
  9.9 13.2 %collective-permute-start.4 = (bf16[520,128]{1,0:T(8,128)(2,1)}, bf16[520,128]{1,0:T(8,128)(2,1)}, u32[]{:S(2)}, u32[]{:S(2)}) collective-permute-start(bf16[520,128]{1,0:T(8,128)(2,1)} %get-tuple-element.180), channel_id=1, source_target_pairs={{0,4},{1,5},{2,6},{3,7},{4,0},{5,1},{6,2},{7,3},{8,12},{9,13},{10,... | collective-permute-start | bytes 399368 | tf_op jit(solution)/shard_map/ppermute | solution.py:144
  13.7 22.5 %collective-permute-start.9 = (bf16[520,128]{1,0:T(8,128)(2,1)}, bf16[520,128]{1,0:T(8,128)(2,1)S(1)}, u32[]{:S(2)}, u32[]{:S(2)}) collective-permute-start(bf16[520,128]{1,0:T(8,128)(2,1)} %get-tuple-element.180), channel_id=1, source_target_pairs={{0,1},{1,0},{2,3},{3,2},{4,5},{5,4},{6,7},{7,6},{8,9},{9,8},{10,11... | collective-permute-start | bytes 399368 | tf_op jit(solution)/shard_map/ppermute | solution.py:144
  19.0 21.2 %collective-permute-start.16 = (bf16[3,192,384]{2,1,0:T(8,128)(2,1)S(1)}, bf16[3,192,384]{2,1,0:T(8,128)(2,1)S(1)}, u32[]{:S(2)}, u32[]{:S(2)}) collective-permute-start(bf16[3,192,384]{2,1,0:T(8,128)(2,1)S(1)} %constant_dynamic-slice_fusion), channel_id=1, source_target_pairs={{0,2},{1,3},{2,0},{3,1},{4,6},{5,7},{6,4},{7,5},{8,10},{9,11},{10,... | collective-permute-start | bytes 1327112 | tf_op jit(solution)/shard_map/ppermute | solution.py:144
  21.6 12.9 %collective-permute-start.3 = (bf16[3,256,128]{2,1,0:T(8,128)(2,1)S(1)}, bf16[3,256,128]{2,1,0:T(8,128)(2,1)S(1)}, u32[]{:S(2)}, u32[]{:S(2)}) collective-permute-start(bf16[3,256,128]{2,1,0:T(8,128)(2,1)S(1)} %pad_maximum_fusion.2), channel_id=1, source_target_pairs={{0,2},{1,3},{2,0},{3,1},{4,6},{5,7},{6,4},{7,5},{8,10},{9,11},{10,... | collective-permute-start | bytes 589832 | tf_op jit(solution)/shard_map/ppermute | solution.py:144
  23.1 13.0 %collective-permute-start.6 = (bf16[3,264,128]{2,1,0:T(8,128)(2,1)S(1)}, bf16[3,264,128]{2,1,0:T(8,128)(2,1)S(1)}, u32[]{:S(2)}, u32[]{:S(2)}) collective-permute-start(bf16[3,264,128]{2,1,0:T(8,128)(2,1)S(1)} %pad_maximum_fusion.1), channel_id=1, source_target_pairs={{0,4},{1,5},{2,6},{3,7},{4,0},{5,1},{6,2},{7,3},{8,12},{9,13},{10,... | collective-permute-start | bytes 608264 | tf_op jit(solution)/shard_map/ppermute | solution.py:144
  26.4 12.3 %collective-permute-start.10 = (bf16[256,128]{1,0:T(8,128)(2,1)S(1)}, bf16[256,128]{1,0:T(8,128)(2,1)S(1)}, u32[]{:S(2)}, u32[]{:S(2)}) collective-permute-start(bf16[256,128]{1,0:T(8,128)(2,1)S(1)} %get-tuple-element.183), channel_id=1, source_target_pairs={{0,1},{1,0},{2,3},{3,2},{4,5},{5,4},{6,7},{7,6},{8,9},{9,8},{10,11... | collective-permute-start | bytes 196616 | tf_op jit(solution)/shard_map/ppermute | solution.py:144
  34.5 10.8 %collective-permute-start.8 = (bf16[7,256,128]{2,1,0:T(8,128)(2,1)S(1)}, bf16[7,256,128]{2,1,0:T(8,128)(2,1)S(1)}, u32[]{:S(2)}, u32[]{:S(2)}) collective-permute-start(bf16[7,256,128]{2,1,0:T(8,128)(2,1)S(1)} %constant_dynamic-update-slice_fusion.4.refs_4_), channel_id=1, source_target_pairs={{0,4},{1,5},{2,6},{3,7},{4,0},{5,1},{6,2},{7,3},{8,12},{9,13},{10,... | collective-permute-start | bytes 1376264 | tf_op jit(solution)/shard_map/ppermute | solution.py:144
  36.1 13.4 %collective-permute-start.13 = (bf16[7,256,128]{2,1,0:T(8,128)(2,1)S(1)}, bf16[7,256,128]{2,1,0:T(8,128)(2,1)S(1)}, u32[]{:S(2)}, u32[]{:S(2)}) collective-permute-start(bf16[7,256,128]{2,1,0:T(8,128)(2,1)S(1)} %constant_dynamic-update-slice_fusion.4.refs_4_), channel_id=1, source_target_pairs={{0,1},{1,0},{2,3},{3,2},{4,5},{5,4},{6,7},{7,6},{8,9},{9,8},{10,11... | collective-permute-start | bytes 1376264 | tf_op jit(solution)/shard_map/ppermute | solution.py:144
  36.2 13.3 %collective-permute-start.7 = (bf16[7,264,128]{2,1,0:T(8,128)(2,1)S(1)}, bf16[7,264,128]{2,1,0:T(8,128)(2,1)S(1)}, u32[]{:S(2)}, u32[]{:S(2)}) collective-permute-start(bf16[7,264,128]{2,1,0:T(8,128)(2,1)S(1)} %constant_dynamic-update-slice_fusion.refs_3_), channel_id=1, source_target_pairs={{0,2},{1,3},{2,0},{3,1},{4,6},{5,7},{6,4},{7,5},{8,10},{9,11},{10,... | collective-permute-start | bytes 1419272 | tf_op jit(solution)/shard_map/ppermute | solution.py:144
  40.0 10.0 %collective-permute-start.12 = (bf16[7,264,128]{2,1,0:T(8,128)(2,1)S(1)}, bf16[7,264,128]{2,1,0:T(8,128)(2,1)S(1)}, u32[]{:S(2)}, u32[]{:S(2)}) collective-permute-start(bf16[7,264,128]{2,1,0:T(8,128)(2,1)S(1)} %constant_dynamic-update-slice_fusion.refs_3_), channel_id=1, source_target_pairs={{0,1},{1,0},{2,3},{3,2},{4,5},{5,4},{6,7},{7,6},{8,9},{9,8},{10,11... | collective-permute-start | bytes 1419272 | tf_op jit(solution)/shard_map/ppermute | solution.py:144
  40.3 17.9 %collective-permute-start.18 = (bf16[3,384,384]{2,1,0:T(8,128)(2,1)S(1)}, bf16[3,384,384]{2,1,0:T(8,128)(2,1)S(1)}, u32[]{:S(2)}, u32[]{:S(2)}) collective-permute-start(bf16[3,384,384]{2,1,0:T(8,128)(2,1)S(1)} %convert_element_type.47.mine_ref), channel_id=1, source_target_pairs={{0,1},{1,0},{2,3},{3,2},{4,5},{5,4},{6,7},{7,6},{8,9},{9,8},{10,11... | collective-permute-start | bytes 2654216 | tf_op jit(solution)/shard_map/ppermute | solution.py:144
  45.3 9.5 %collective-permute-start.17 = (bf16[3,192,384]{2,1,0:T(8,128)(2,1)S(1)}, bf16[3,192,384]{2,1,0:T(8,128)(2,1)S(1)}, u32[]{:S(2)}, u32[]{:S(2)}) collective-permute-start(bf16[3,192,384]{2,1,0:T(8,128)(2,1)S(1)} %collective-permute-done.16.near_ref), channel_id=1, source_target_pairs={{0,8},{1,9},{2,10},{3,11},{4,12},{5,13},{6,14},{7,15},{8,0},{9,1},... | collective-permute-start | bytes 1327112 | tf_op jit(solution)/shard_map/ppermute | solution.py:144
  86.2 13.5 %collective-permute-start.28 = (bf16[16,120,384]{2,1,0:T(8,128)(2,1)S(1)}, bf16[16,120,384]{2,1,0:T(8,128)(2,1)S(1)}, u32[]{:S(2)}, u32[]{:S(2)}) collective-permute-start(bf16[16,120,384]{2,1,0:T(8,128)(2,1)S(1)} %get-tuple-element.136), channel_id=1, source_target_pairs={{0,1},{1,0},{2,3},{3,2},{4,5},{5,4},{6,7},{7,6},{8,9},{9,8},{10,11... | collective-permute-start | bytes 4423688 | tf_op jit(solution)/shard_map/ppermute | solution.py:144
  100.6 11.5 %collective-permute-start.29 = (bf16[4,120,384]{2,1,0:T(8,128)(2,1)S(1)}, bf16[4,120,384]{2,1,0:T(8,128)(2,1)S(1)}, u32[]{:S(2)}, u32[]{:S(2)}) collective-permute-start(bf16[4,120,384]{2,1,0:T(8,128)(2,1)S(1)} %get-tuple-element.138), channel_id=1, source_target_pairs={{0,4},{1,5},{2,6},{3,7},{4,0},{5,1},{6,2},{7,3},{8,12},{9,13},{10,... | collective-permute-start | bytes 1105928 | tf_op jit(solution)/shard_map/ppermute | solution.py:144
  102.1 19.4 %collective-permute-start.30 = (bf16[4,120,384]{2,1,0:T(8,128)(2,1)S(1)}, bf16[4,120,384]{2,1,0:T(8,128)(2,1)S(1)}, u32[]{:S(2)}, u32[]{:S(2)}) collective-permute-start(bf16[4,120,384]{2,1,0:T(8,128)(2,1)S(1)} %get-tuple-element.139), channel_id=1, source_target_pairs={{0,2},{1,3},{2,0},{3,1},{4,6},{5,7},{6,4},{7,5},{8,10},{9,11},{10,... | collective-permute-start | bytes 1105928 | tf_op jit(solution)/shard_map/ppermute | solution.py:144
  103.6 17.8 %collective-permute-start.31 = (bf16[4,120,384]{2,1,0:T(8,128)(2,1)S(1)}, bf16[4,120,384]{2,1,0:T(8,128)(2,1)S(1)}, u32[]{:S(2)}, u32[]{:S(2)}) collective-permute-start(bf16[4,120,384]{2,1,0:T(8,128)(2,1)S(1)} %get-tuple-element.140), channel_id=1, source_target_pairs={{0,6},{1,7},{2,4},{3,5},{4,2},{5,3},{6,0},{7,1},{8,14},{9,15},{10,... | collective-permute-start | bytes 1105928 | tf_op jit(solution)/shard_map/ppermute | solution.py:144
  104.8 21.7 %collective-permute-start.22 = (bf16[4,48,384]{2,1,0:T(8,128)(2,1)S(1)}, bf16[4,48,384]{2,1,0:T(8,128)(2,1)S(1)}, u32[]{:S(2)}, u32[]{:S(2)}) collective-permute-start(bf16[4,48,384]{2,1,0:T(8,128)(2,1)S(1)} %get-tuple-element.116), channel_id=1, source_target_pairs={{0,4},{1,5},{2,6},{3,7},{4,0},{5,1},{6,2},{7,3},{8,12},{9,13},{10,... | collective-permute-start | bytes 442376 | tf_op jit(solution)/shard_map/ppermute | solution.py:144
  106.4 21.3 %collective-permute-start.23 = (bf16[4,48,384]{2,1,0:T(8,128)(2,1)S(1)}, bf16[4,48,384]{2,1,0:T(8,128)(2,1)S(1)}, u32[]{:S(2)}, u32[]{:S(2)}) collective-permute-start(bf16[4,48,384]{2,1,0:T(8,128)(2,1)S(1)} %get-tuple-element.117), channel_id=1, source_target_pairs={{0,2},{1,3},{2,0},{3,1},{4,6},{5,7},{6,4},{7,5},{8,10},{9,11},{10,... | collective-permute-start | bytes 442376 | tf_op jit(solution)/shard_map/ppermute | solution.py:144
  112.1 15.6 %collective-permute-start.24 = (bf16[4,48,384]{2,1,0:T(8,128)(2,1)S(1)}, bf16[4,48,384]{2,1,0:T(8,128)(2,1)S(1)}, u32[]{:S(2)}, u32[]{:S(2)}) collective-permute-start(bf16[4,48,384]{2,1,0:T(8,128)(2,1)S(1)} %get-tuple-element.118), channel_id=1, source_target_pairs={{0,6},{1,7},{2,4},{3,5},{4,2},{5,3},{6,0},{7,1},{8,14},{9,15},{10,... | collective-permute-start | bytes 442376 | tf_op jit(solution)/shard_map/ppermute | solution.py:144
  122.2 9.7 %collective-permute-start.32 = (bf16[120,384]{1,0:T(8,128)(2,1)S(1)}, bf16[120,384]{1,0:T(8,128)(2,1)S(1)}, u32[]{:S(2)}, u32[]{:S(2)}) collective-permute-start(bf16[120,384]{1,0:T(8,128)(2,1)S(1)} %get-tuple-element.142), channel_id=1, source_target_pairs={{0,8},{1,9},{2,10},{3,11},{4,12},{5,13},{6,14},{7,15},{8,0},{9,1},... | collective-permute-start | bytes 276488 | tf_op jit(solution)/shard_map/ppermute | solution.py:144
  123.0 11.9 %collective-permute-start.33 = (bf16[120,384]{1,0:T(8,128)(2,1)S(1)}, bf16[120,384]{1,0:T(8,128)(2,1)S(1)}, u32[]{:S(2)}, u32[]{:S(2)}) collective-permute-start(bf16[120,384]{1,0:T(8,128)(2,1)S(1)} %get-tuple-element.143), channel_id=1, source_target_pairs={{0,16},{1,17},{2,18},{3,19},{4,20},{5,21},{6,22},{7,23},{8,24},{9,... | collective-permute-start | bytes 276488 | tf_op jit(solution)/shard_map/ppermute | solution.py:144
  126.5 8.4 %collective-permute-start.34 = (bf16[120,384]{1,0:T(8,128)(2,1)S(1)}, bf16[120,384]{1,0:T(8,128)(2,1)S(1)}, u32[]{:S(2)}, u32[]{:S(2)}) collective-permute-start(bf16[120,384]{1,0:T(8,128)(2,1)S(1)} %get-tuple-element.144), channel_id=1, source_target_pairs={{0,24},{1,25},{2,26},{3,27},{4,28},{5,29},{6,30},{7,31},{8,16},{9,... | collective-permute-start | bytes 276488 | tf_op jit(solution)/shard_map/ppermute | solution.py:144
  138.5 9.0 %collective-permute-start.38 = (bf16[3,24,384]{2,1,0:T(8,128)(2,1)S(1)}, bf16[3,24,384]{2,1,0:T(8,128)(2,1)S(1)}, u32[]{:S(2)}, u32[]{:S(2)}) collective-permute-start(bf16[3,24,384]{2,1,0:T(8,128)(2,1)S(1)} %get-tuple-element.150), channel_id=1, source_target_pairs={{0,1},{1,0},{2,3},{3,2},{4,5},{5,4},{6,7},{7,6},{8,9},{9,8},{10,11... | collective-permute-start | bytes 165896 | tf_op jit(solution)/shard_map/ppermute | solution.py:144
  147.5 11.5 %collective-permute-start.41 = (bf16[4,64,384]{2,1,0:T(8,128)(2,1)S(1)}, bf16[4,64,384]{2,1,0:T(8,128)(2,1)S(1)}, u32[]{:S(2)}, u32[]{:S(2)}) collective-permute-start(bf16[4,64,384]{2,1,0:T(8,128)(2,1)S(1)} %pad_maximum_fusion.3.refs_0_), channel_id=1, source_target_pairs={{0,4},{1,5},{2,6},{3,7},{4,0},{5,1},{6,2},{7,3},{8,12},{9,13},{10,... | collective-permute-start | bytes 589832 | tf_op jit(solution)/shard_map/ppermute | solution.py:144
  161.1 13.8 %collective-permute-start.51 = (bf16[4,64,384]{2,1,0:T(8,128)(2,1)S(1)}, bf16[4,64,384]{2,1,0:T(8,128)(2,1)S(1)}, u32[]{:S(2)}, u32[]{:S(2)}) collective-permute-start(bf16[4,64,384]{2,1,0:T(8,128)(2,1)S(1)} %pad_maximum_fusion.3.refs_0_), channel_id=1, source_target_pairs={{0,1},{1,0},{2,3},{3,2},{4,5},{5,4},{6,7},{7,6},{8,9},{9,8},{10,11... | collective-permute-start | bytes 589832 | tf_op jit(solution)/shard_map/ppermute | solution.py:144
  161.1 14.7 %collective-permute-start.52 = (bf16[4,64,384]{2,1,0:T(8,128)(2,1)S(1)}, bf16[4,64,384]{2,1,0:T(8,128)(2,1)S(1)}, u32[]{:S(2)}, u32[]{:S(2)}) collective-permute-start(bf16[4,64,384]{2,1,0:T(8,128)(2,1)S(1)} %collective-permute-done.41.refs_1_), channel_id=1, source_target_pairs={{0,1},{1,0},{2,3},{3,2},{4,5},{5,4},{6,7},{7,6},{8,9},{9,8},{10,11... | collective-permute-start | bytes 589832 | tf_op jit(solution)/shard_map/ppermute | solution.py:144
  161.6 15.3 %collective-permute-start.53 = (bf16[4,64,384]{2,1,0:T(8,128)(2,1)S(1)}, bf16[4,64,384]{2,1,0:T(8,128)(2,1)S(1)}, u32[]{:S(2)}, u32[]{:S(2)}) collective-permute-start(bf16[4,64,384]{2,1,0:T(8,128)(2,1)S(1)} %collective-permute-done.49.refs_2_), channel_id=1, source_target_pairs={{0,1},{1,0},{2,3},{3,2},{4,5},{5,4},{6,7},{7,6},{8,9},{9,8},{10,11... | collective-permute-start | bytes 589832 | tf_op jit(solution)/shard_map/ppermute | solution.py:144
  165.3 12.5 %collective-permute-start.54 = (bf16[4,64,384]{2,1,0:T(8,128)(2,1)S(1)}, bf16[4,64,384]{2,1,0:T(8,128)(2,1)S(1)}, u32[]{:S(2)}, u32[]{:S(2)}) collective-permute-start(bf16[4,64,384]{2,1,0:T(8,128)(2,1)S(1)} %collective-permute-done.50.refs_3_), channel_id=1, source_target_pairs={{0,1},{1,0},{2,3},{3,2},{4,5},{5,4},{6,7},{7,6},{8,9},{9,8},{10,11... | collective-permute-start | bytes 589832 | tf_op jit(solution)/shard_map/ppermute | solution.py:144
  (37 other events, 478.1 us)
